TPU v7x, 128 devices: a whole 4x4x4 slice. The times are simulated.
128 devices in a mesh: slide: 16 (over z, y_hi, core), tile: 8 (over y_lo, x).
Axes of the slice: x: 4, y: 4 (y_hi: 2, y_lo: 2; y = y_hi * 2 + y_lo), z: 4, core: 2. Of those that a mesh axis runs over, the one named last changes fastest.
Arguments:
- features: bfloat16 [16, 8, 32, 32, 768], P('slide', 'tile'), may hold values from -6 to 6
- cotangent: bfloat16 [16, 8, 32, 32, 768], P('slide', 'tile'), may hold values from -0.59765625 to 0.59765625
- neighbours: int32 [16, 8, 8], P('slide'), may hold values from 0 to 8, as said below
- skip_flags: int32 [1, 16], P(None, 'slide'), may hold values 0 or 1
- dw_weight: float32 [1, 7, 7, 768], replicated, may hold values from -0.875 to 0.875
- ln_gain: float32 [1, 768], replicated, may hold values from 0.5 to 1.5
- ln_bias: float32 [1, 768], replicated, may hold values from -3 to 3
- up_weight: bfloat16 [1, 3072, 768], replicated, may hold values from -0.21875 to 0.21875
- up_bias: float32 [1, 3072], replicated, may hold values from -3 to 3
- down_weight: bfloat16 [1, 768, 3072], replicated, may hold values from -0.109375 to 0.109375
- down_bias: float32 [1, 768], replicated, may hold values from -3 to 3
- layer_scale: float32 [1, 768], replicated, may hold values from 0.5 to 1.5
Outputs:
- block_out: bfloat16 [16, 8, 32, 32, 768], P('slide', 'tile')
- input_grad: bfloat16 [16, 8, 32, 32, 768], P('slide', 'tile')
- weight_grads: float32 [1, 3072, 1536], P(None, ('slide', 'tile'))
- kernel_grads: float32 [1, 7, 7, 768], replicated
- channel_grads: float32 [1, 4, 768], replicated
- bias_grads: float32 [1, 3072], replicated
Inputs may be any that keep to these rules, and one draw needn't show every extreme that they name: neighbours[s, a, d] is the tile of slide s next to tile a in direction d, or 8 where no tissue tile lies there; tiles of a slide sit on a grid four tiles wide, and b is a's neighbour in one direction exactly when a is b's in the opposite direction.
All inputs are finite; a program needn't handle non-finite values. No bound on the sum of `skip_flags` on one device may be relied on, other than what follows from the above.
Results may differ from a plain program's by a relative error of at most 0.015.
Values may be sent and summed in bfloat16 or wider, within the bound.
No kernel may reach another device: no remote copies, remote signals or barrier semaphores. Data moves between devices by JAX's collectives and lax.ppermute only.
A program may use at most 192 MiB of HBM per device.

v0:
```python
import jax
import jax.numpy as jnp
from jax import lax
from jax.sharding import PartitionSpec as P

ln_eps = 1e-06
root_half = 0.7071067811865476
inv_root_two_pi = 0.3989422804014327
conv_dims = ("NHWC", "HWIO", "NHWC")


def border_rows(tiles):
    return jnp.stack([tiles[:, :3], tiles[:, -3:]], 1)


def border_columns(tiles):
    return jnp.stack([tiles[:, :, :3], tiles[:, :, -3:]], 1)


def extend(tiles, row_strips, column_strips, table_rows):
    row_strips = jnp.concatenate([row_strips, jnp.zeros_like(row_strips[:1])], 0)
    column_strips = jnp.concatenate([column_strips, jnp.zeros_like(column_strips[:1])], 0)
    north = row_strips[table_rows[:, 0], 1]
    south = row_strips[table_rows[:, 1], 0]
    west = column_strips[table_rows[:, 2], 1]
    east = column_strips[table_rows[:, 3], 0]
    north_west = row_strips[table_rows[:, 4], 1][:, :, -3:]
    north_east = row_strips[table_rows[:, 5], 1][:, :, :3]
    south_west = row_strips[table_rows[:, 6], 0][:, :, -3:]
    south_east = row_strips[table_rows[:, 7], 0][:, :, :3]
    upper = jnp.concatenate([north_west, north, north_east], 2)
    middle = jnp.concatenate([west, tiles, east], 2)
    lower = jnp.concatenate([south_west, south, south_east], 2)
    return jnp.concatenate([upper, middle, lower], 1)


def depthwise(extended, kernel):
    channels = kernel.shape[-1]
    return lax.conv_general_dilated(
        extended,
        kernel[:, :, None, :],
        (1, 1),
        "VALID",
        dimension_numbers=conv_dims,
        feature_group_count=channels,
        precision=lax.Precision.HIGHEST,
    )


def kernel_grad(extended, conv_grad):
    channels = conv_grad.shape[-1]
    total = jnp.zeros((7, 7, channels), jnp.float32)
    kernel = jnp.transpose(conv_grad, (1, 2, 0, 3))
    single = lax.conv_general_dilated(
        extended,
        kernel,
        (1, 1),
        "VALID",
        dimension_numbers=conv_dims,
        feature_group_count=channels,
        precision=lax.Precision.HIGHEST,
    )
    total = total + single[0]
    return total


def normalize(values):
    average = jnp.mean(values, axis=-1, keepdims=True)
    centred = values - average
    inv_std = lax.rsqrt(jnp.mean(centred * centred, axis=-1, keepdims=True) + ln_eps)
    return (centred * inv_std, inv_std)


def gelu_parts(pre):
    cdf = 0.5 * (1.0 + lax.erf(pre * root_half))
    return (cdf, cdf + pre * inv_root_two_pi * jnp.exp(-0.5 * pre * pre))


def contract(left, right):
    return lax.dot_general(
        left, right, (((1,), (1,)), ((), ())), preferred_element_type=jnp.float32
    )


def over_pixels(left, right):
    return lax.dot_general(
        left, right, (((0,), (0,)), ((), ())), preferred_element_type=jnp.float32
    )


def mlp_forward(flat, up_matrix, up_shift, down_matrix, down_shift):
    pre = contract(flat, up_matrix) + up_shift
    cdf, slope = gelu_parts(pre)
    act = (pre * cdf).astype(jnp.bfloat16)
    branch = contract(act, down_matrix) + down_shift
    return (pre, act, branch)


def mlp_backward(grad_flat, branch_factor, whitened, inv_std, pre, up_matrix, down_matrix, gain):
    branch_grad = (branch_factor * grad_flat).astype(jnp.bfloat16)
    act_grad = jnp.dot(branch_grad, down_matrix, preferred_element_type=jnp.float32)
    cdf, slope = gelu_parts(pre)
    pre_grad = (act_grad * slope).astype(jnp.bfloat16)
    normed_grad = jnp.dot(pre_grad, up_matrix, preferred_element_type=jnp.float32)
    scaled = normed_grad * gain
    conv_grad = inv_std * (
        scaled
        - jnp.mean(scaled, axis=-1, keepdims=True)
        - whitened * jnp.mean(scaled * whitened, axis=-1, keepdims=True)
    )
    sums = jnp.stack(
        [
            jnp.sum(normed_grad * whitened, axis=0),
            jnp.sum(normed_grad, axis=0),
            jnp.sum(branch_grad.astype(jnp.float32), axis=0),
        ]
    )
    return (
        branch_grad,
        pre_grad,
        conv_grad.astype(jnp.bfloat16),
        sums,
        jnp.sum(pre_grad.astype(jnp.float32), axis=0),
    )


def on_device(
    features,
    cotangent,
    neighbours,
    skip_flags,
    dw_weight,
    ln_gain,
    ln_bias,
    up_weight,
    up_bias,
    down_weight,
    down_bias,
    layer_scale,
):
    tile_count = features.shape[1]
    channels = features.shape[4]
    blocks = dw_weight.shape[0]
    hidden_units = up_weight.shape[1]
    tile_shape = features.shape[1:]
    first_tile = lax.axis_index("tile") * tile_count
    table_rows = lax.dynamic_slice_in_dim(neighbours[0], first_tile, tile_count, 0)
    current = features[0]
    layer = 0
    keep = (1 - skip_flags[layer, 0]).astype(jnp.float32)
    row_strips = lax.all_gather(border_rows(current), "tile", axis=0, tiled=True)
    column_strips = lax.all_gather(border_columns(current), "tile", axis=0, tiled=True)
    extended = extend(current, row_strips, column_strips, table_rows).astype(jnp.float32)
    conv = depthwise(extended, dw_weight[layer])
    whitened, inv_std = normalize(conv.reshape(-1, channels))
    flat = (whitened * ln_gain[layer] + ln_bias[layer]).astype(jnp.bfloat16)
    pre, act, branch = mlp_forward(
        flat, up_weight[layer], up_bias[layer], down_weight[layer], down_bias[layer]
    )
    output = (
        current.astype(jnp.float32).reshape(-1, channels) + keep * layer_scale[layer] * branch
    ).astype(jnp.bfloat16)
    saved = [(extended, whitened, inv_std, flat, pre, act, branch, keep)]
    current = output.reshape(tile_shape)
    step_grad = cotangent[0]
    weight_list = []
    kernel_list = []
    channel_list = []
    bias_list = []
    for layer in reversed(range(blocks)):
        extended, whitened, inv_std, flat, pre, act, branch, keep = saved[layer]
        grad_flat = step_grad.astype(jnp.float32).reshape(-1, channels)
        scale_grad = jnp.sum(grad_flat * keep * branch, axis=0)
        branch_factor = keep * layer_scale[layer]
        branch_grad, pre_grad, conv_grad, sums, up_bias_sum = mlp_backward(
            grad_flat,
            branch_factor,
            whitened,
            inv_std,
            pre,
            up_weight[layer],
            down_weight[layer],
            ln_gain[layer],
        )
        first_row = jnp.int32(0)
        pre_rows = lax.dynamic_slice_in_dim(
            pre_grad,
            first_row,
            hidden_units // lax.axis_size(("slide", "tile")) * lax.axis_size(("slide", "tile")),
            1,
        )
        act_rows = lax.dynamic_slice_in_dim(
            act,
            first_row,
            hidden_units // lax.axis_size(("slide", "tile")) * lax.axis_size(("slide", "tile")),
            1,
        )
        weight_rows = lax.psum_scatter(
            jnp.concatenate([over_pixels(pre_rows, flat), over_pixels(act_rows, branch_grad)], 1),
            ("slide", "tile"),
            scatter_dimension=0,
            tiled=True,
        )
        conv_tiles = conv_grad.reshape(tile_shape)
        grad_rows, grad_columns = (
            lax.all_gather(border_rows(conv_tiles), "tile", axis=0, tiled=True),
            lax.all_gather(border_columns(conv_tiles), "tile", axis=0, tiled=True),
        )
        kernel_sum = kernel_grad(extended, conv_tiles.astype(jnp.float32))
        channel_sum = jnp.concatenate([sums, scale_grad[None]], 0)
        kernel_total, channel_total, bias_total = lax.psum(
            (kernel_sum, channel_sum, up_bias_sum), ("slide", "tile")
        )
        grad_extended = extend(conv_tiles, grad_rows, grad_columns, table_rows).astype(jnp.float32)
        back = depthwise(grad_extended, dw_weight[layer][::-1, ::-1])
        step_grad = (step_grad.astype(jnp.float32) + back).astype(jnp.bfloat16)
        weight_list.append(weight_rows)
        kernel_list.append(kernel_total)
        channel_list.append(channel_total)
        bias_list.append(bias_total)
    weight_grads = jnp.stack(weight_list[::-1])
    kernel_grads = jnp.stack(kernel_list[::-1])
    channel_grads = jnp.stack(channel_list[::-1])
    bias_grads = jnp.stack(bias_list[::-1])
    return (current[None], step_grad[None], weight_grads, kernel_grads, channel_grads, bias_grads)


def solution(mesh):
    return jax.shard_map(
        on_device,
        mesh=mesh,
        in_specs=(
            P("slide", "tile", None, None, None),
            P("slide", "tile", None, None, None),
            P("slide", None, None),
            P(None, "slide"),
            P(),
            P(),
            P(),
            P(),
            P(),
            P(),
            P(),
            P(),
        ),
        out_specs=(
            P("slide", "tile", None, None, None),
            P("slide", "tile", None, None, None),
            P(None, ("slide", "tile"), None),
            P(),
            P(),
            P(),
        ),
        check_vma=False,
    )
```

profile of v0, /device:TPU:0, one launch (start us, length us, event | category | flops | bytes accessed | tf_op | source)
XLA Modules:
  0.0 1166.0 jit_solution(9460932228575306207)
XLA Ops:
  7.2 1.0 slice_bitcast_fusion.7
  8.2 0.7 pad_maximum_fusion.3
  9.1 1.3 slice_bitcast_fusion.3
  10.4 0.3 pad_maximum_fusion.1
  10.6 0.8 copy.58
  11.5 0.7 fusion.61
  22.4 4.5 copy.60
  27.7 7.3 convert_reduce_fusion.1
  34.9 1.5 copy.83
  41.5 13.3 %all-gather.5.cloned.1.call-done = bf16[8,2,3,32,768]{4,3,2,1,0:T(8,128)(2,1)} async-done(((bf16[1,2,3,32,768]{4,3,2,1,0:T(8,128)(2,1)}), bf16[8,2,3,32,768]{4,3,2,1,0:T(8,128)(2,1)}) %all-gather.5.cloned.1.call-update) | async-done | bytes 2359312 | tf_op jit(solution)/shard_map/all_gather | solution.py:151
  54.8 1.1 fusion.43
  56.1 0.6 copy.91
  56.7 0.2 copy.55
  57.0 0.9 copy.64
  57.9 39.7 %all-gather.7.cloned.1.call-done = bf16[8,2,32,3,768]{4,2,3,1,0:T(8,128)(2,1)} async-done(((bf16[1,2,32,3,768]{4,2,3,1,0:T(8,128)(2,1)}), bf16[8,2,32,3,768]{4,2,3,1,0:T(8,128)(2,1)}) %all-gather.7.cloned.1.call-update) | async-done | bytes 2359312 | tf_op jit(solution)/shard_map/all_gather | solution.py:152
  97.7 0.2 copy.59
  98.0 0.2 copy.61
  98.2 0.4 copy-done.10
  98.6 24.6 %maximum_maximum_fusion = bf16[1,38,38,768]{3,0,2,1:T(2,128)(2,1)S(1)} fusion(bf16[1,3,3,768]{3,0,2,1:T(2,128)(2,1)S(1)} %copy-done.15, bf16[1,3,32,768]{3,0,2,1:T(2,128)(2,1)S(1)} %copy-done.10, bf16[1,3,3,768]{3,0,2,1:T(2,128)(2,1)S(1)} %copy.90, bf16[1,32,3,768]{3,0,2,1:T(2,128)(2,1)S(1)} %copy.61, bf16[1,32,32,768]{3,0,2,1:T(2,128)(2,1)S(1)} %copy.60, ...), kind=kLoop, calls=%fused_computation.17 | loop fusion | flops 8871936 | bytes 4435968 | tf_op jit(solution)/shard_map/concatenate | solution.py:34
  123.3 71.6 %fusion.62 = (f32[32,32]{1,0:T(8,128)S(1)}, f32[1,32,32,768]{3,0,2,1:T(1,128)S(1)}) fusion(bf16[1,38,38,768]{3,0,2,1:T(2,128)(2,1)S(1)} %maximum_maximum_fusion, f32[1,7,7,768]{3,0,2,1:T(1,128)S(1)} %copy-done.12), kind=kOutput, calls=%fused_computation.118 | convolution fusion | flops 463207424 | bytes 5518336 | tf_op jit(solution)/shard_map/conv_general_dilated | solution.py:39
  195.0 0.1 div.17
  195.0 16.0 %multiply_reduce_fusion.2 = f32[32,32]{1,0:T(8,128)S(1)} fusion(f32[1,32,32,768]{3,0,2,1:T(1,128)S(1)} %get-tuple-element.245, f32[32,32]{1,0:T(8,128)S(1)} %broadcast_multiply_fusion), kind=kLoop, calls=%fused_computation.57 | loop fusion | flops 2358272 | bytes 3153920 | tf_op jit(solution)/shard_map/reduce_sum | solution.py:70
  211.0 2.0 copy.84
  213.0 0.1 rsqrt.13
  213.1 5.2 add_convert_fusion.1
  218.4 0.4 copy.82
  218.8 0.3 copy-done.21
  219.1 9.6 multiply_convert_fusion
  228.7 12.3 %convert_reduce_fusion = (f32[3072]{0:T(1024)S(1)}, bf16[1024,3072]{1,0:T(8,128)(2,1)}) fusion(f32[1024,3072]{1,0:T(8,128)S(1)} %get-tuple-element.247, f32[3072]{0:T(1024)S(1)} %bitcast.168, bf16[1024,768]{1,0:T(8,128)(2,1)S(1)} %bitcast.157, bf16[1,768,3072]{2,1,0:T(8,128)(2,1)S(1)} %bitcast.166), kind=kOutput, calls=%fused_computation.7 | convolution fusion | flops 4872729600 | bytes 25190400 | tf_op jit(solution)/shard_map/dot_general | solution.py:101
  241.0 8.8 multiply_reduce_fusion
  249.9 1.4 multiply_convert_fusion.1
  251.3 0.9 pad_maximum_fusion.4
  252.2 0.4 all-gather.11.cloned.1.call-start
  252.7 2.4 copy_convert_fusion
  255.1 2.0 copy.87
  257.1 0.2 slice_bitcast_fusion.1
  257.3 0.3 pad_maximum_fusion.2
  257.5 0.8 copy.69
  258.4 10.4 fusion.32
  268.8 7.4 fusion.64
  276.3 7.3 fusion.63
  283.5 7.0 pad_maximum_fusion
  290.5 18.7 %copy.80 = f32[3072,1536]{1,0:T(8,128)} copy(f32[3072,1536]{0,1:T(8,128)} %pad_maximum_fusion) | data formatting | bytes 37748736
  309.2 0.2 all-reduce.7.cloned.1.call-start
  309.4 0.7 copy-done.13
  310.1 1.9 rev.3
  312.1 4.5 copy.71
  316.7 66.2 %all-reduce.4 = (f32[1,4,768]{2,1,0:T(4,128)}, f32[1,3072]{1,0:T(1,128)}) all-reduce(f32[1,4,768]{2,1,0:T(4,128)S(1)} %maximum_bitcast_fusion, f32[1,3072]{1,0:T(1,128)S(1)} %bitcast.162), channel_id=1, replica_groups=mesh['slide'=16,'tile'=8] {'slide','tile'}, use_global_device_ids=true, to_apply=%region_10.0 | all-reduce | flops 6144 | bytes 49152 | tf_op jit(solution)/shard_map/psum | solution.py:211
  382.9 32.7 %fusion.36 = f32[1,7,7,768]{3,0,2,1:T(1,128)} fusion(bf16[1,38,38,768]{3,0,2,1:T(2,128)(2,1)} %copy-done.6, bf16[32,32,1,768]{3,1,0,2:T(8,128)(2,1)} %bitcast.152), kind=kOutput, calls=%fused_computation.47 | convolution fusion | flops 77070336 | bytes 3941376 | tf_op jit(solution)/shard_map/conv_general_dilated | solution.py:54
  415.7 1.2 fusion.49
  417.0 0.6 copy.95
  417.7 0.2 copy.68
  417.9 0.9 copy.75
  418.9 0.2 copy.70
  419.1 0.2 copy.72
  419.4 0.4 copy-done.9
  419.8 24.4 %fusion.78 = bf16[1,38,38,768]{3,0,2,1:T(2,128)(2,1)S(1)} fusion(bf16[1,3,3,768]{3,0,2,1:T(2,128)(2,1)S(1)} %copy-done.14, bf16[1,3,32,768]{3,0,2,1:T(2,128)(2,1)S(1)} %copy-done.9, bf16[1,3,3,768]{3,0,2,1:T(2,128)(2,1)S(1)} %copy.94, bf16[1,32,3,768]{3,0,2,1:T(2,128)(2,1)S(1)} %copy.72, bf16[1,32,32,768]{3,0,2,1:T(2,128)(2,1)S(1)} %copy.71, ...), kind=kLoop, calls=%fused_computation.19.clone.clone.clone.1 | loop fusion | flops 8871936 | bytes 4435968 | tf_op jit(solution)/shard_map/conv_general_dilated | solution.py:39
  444.3 30.4 %fusion.35 = bf16[1,32,32,768]{3,0,2,1:T(2,128)(2,1)S(1)} fusion(f32[7,7,1,768]{3,1,0,2:T(8,128)S(1)} %bitcast.161, bf16[1,1,32,32,768]{4,3,2,1,0:T(8,128)(2,1)S(1)} %copy-done.5, bf16[1,38,38,768]{3,0,2,1:T(2,128)(2,1)S(1)} %fusion.78), kind=kOutput, calls=%fused_computation.46 | convolution fusion | flops 464781312 | bytes 5514240 | tf_op jit(solution)/shard_map/conv_general_dilated | solution.py:39
  474.7 1.5 copy.110
  476.2 538.4 %reduce-scatter.4.cloned.1.call-done = f32[24,1536]{1,0:T(8,128)} async-done(((f32[3072,1536]{1,0:T(8,128)}), f32[24,1536]{1,0:T(8,128)}) %reduce-scatter.4.cloned.1.call-update) | async-done | bytes 147472
  1014.5 1.2 copy.81
  1015.7 0.9 copy.78
  1016.6 140.7 %all-reduce.7.cloned.1.call-done = f32[1,7,7,768]{3,0,2,1:T(1,128)} async-done(((f32[1,7,7,768]{3,0,2,1:T(1,128)}), f32[1,7,7,768]{3,0,2,1:T(1,128)}) %all-reduce.7.cloned.1.call-update) | async-done | bytes 150544 | tf_op jit(solution)/shard_map/psum | solution.py:211
  1157.3 1.6 copy.114
  (95 shorter events, 0.9 us)
Async XLA Ops:
  7.2 4.3 copy-start
  7.2 47.6 %all-gather.5.cloned.1.call-start = ((), (), s32[]{:S(2)}) async-start(), calls=%async_computation.1 | async-start | bytes 2654208 | tf_op jit(solution)/shard_map/all_gather | solution.py:151
  9.0 88.7 %all-gather.7.cloned.1.call-start = ((), (), s32[]{:S(2)}) async-start(), calls=%async_computation.2 | async-start | bytes 2654208 | tf_op jit(solution)/shard_map/all_gather | solution.py:152
  10.3 17.2 %copy-start.17 = (f32[1,768]{1,0:T(1,128)S(1)}, f32[1,768]{1,0:T(1,128)}, u32[]{:S(2)}) copy-start(f32[1,768]{1,0:T(1,128)} %param.17) | copy-start | bytes 9220
  10.3 17.3 %copy-start.18 = (f32[1,768]{1,0:T(1,128)S(1)}, f32[1,768]{1,0:T(1,128)}, u32[]{:S(2)}) copy-start(f32[1,768]{1,0:T(1,128)} %param.18) | copy-start | bytes 9220
  10.4 17.3 %copy-start.19 = (f32[1,768]{1,0:T(1,128)S(1)}, f32[1,768]{1,0:T(1,128)}, u32[]{:S(2)}) copy-start(f32[1,768]{1,0:T(1,128)} %param.23) | copy-start | bytes 9220
  11.4 404.2 %all-gather.9.cloned.1.call-start = ((), (), s32[]{:S(2)}) async-start(), calls=%async_computation.3 | async-start | bytes 2654208 | tf_op jit(solution)/shard_map/all_gather | solution.py:206
  97.7 1.0 copy-start.10
  97.7 1.0 copy-start.15
  98.6 24.7 %copy-start.12 = (f32[1,7,7,768]{3,0,2,1:T(1,128)S(1)}, f32[1,7,7,768]{3,0,2,1:T(1,128)}, u32[]{:S(2)}) copy-start(f32[1,7,7,768]{3,0,2,1:T(1,128)} %param.16) | copy-start | bytes 451588
  123.3 71.7 %copy-start.6 = (bf16[1,38,38,768]{3,0,2,1:T(2,128)(2,1)}, bf16[1,38,38,768]{3,0,2,1:T(2,128)(2,1)S(1)}, u32[]{:S(2)}) copy-start(bf16[1,38,38,768]{3,0,2,1:T(2,128)(2,1)S(1)} %maximum_maximum_fusion) | copy-start | bytes 6653956
  218.4 0.7 copy-start.21
  218.4 10.3 slice-start.2
  219.1 9.6 copy-start.8
  219.1 9.6 slice-start.3
  219.1 21.9 %slice-start = ((s8[4718592]{0:T(1024)(128)(4,1)}), s8[4194304]{0:T(1024)(128)(4,1)S(1)}, s32[]{:S(2)}) async-start(s8[4718592]{0:T(1024)(128)(4,1)} %bitcast.163), calls=%async_computation.7 | async-start | bytes 8388608
  228.7 12.3 %copy-start.2 = (f32[1,32,32,768]{3,2,0,1:T(8,128)S(1)}, f32[1,32,32,768]{3,2,0,1:T(8,128)}, u32[]{:S(2)}) copy-start(f32[1,32,32,768]{3,2,0,1:T(8,128)} %copy.84) | copy-start | bytes 9437188
  228.7 12.3 %slice-start.1 = ((s8[4718592]{0:T(1024)(128)(4,1)}), s8[524288]{0:T(1024)(128)(4,1)S(1)}, s32[]{:S(2)}) async-start(s8[4718592]{0:T(1024)(128)(4,1)} %bitcast.163), calls=%async_computation.8 | async-start | bytes 1048576
  249.9 2.7 copy-start.20
  249.9 2.8 copy-start.4
  251.2 5.9 copy-start.3
  252.2 166.7 %all-gather.11.cloned.1.call-start = ((), (), s32[]{:S(2)}) async-start(), calls=%async_computation.4 | async-start | bytes 2654208 | tf_op jit(solution)/shard_map/all_gather | solution.py:207
  255.1 3.3 copy-start.7
  258.3 756.2 %reduce-scatter.4.cloned.1.call-start = ((), (), s32[]{:S(2)}) async-start(), calls=%async_computation.6 | async-start | bytes 19021824
  268.8 7.4 copy-start.22
  309.2 0.9 copy-start.13
  309.2 2.9 copy-start.16
  309.2 848.1 %all-reduce.7.cloned.1.call-start = ((), (), s32[]{:S(2)}) async-start(), calls=%async_computation.5 | async-start | bytes 301056 | tf_op jit(solution)/shard_map/psum | solution.py:211
  418.8 1.0 copy-start.9
  418.8 1.0 copy-start.14
  419.8 24.4 %copy-start.5 = (bf16[1,1,32,32,768]{4,3,2,1,0:T(8,128)(2,1)S(1)}, bf16[1,1,32,32,768]{4,3,2,1,0:T(8,128)(2,1)}, u32[]{:S(2)}) copy-start(bf16[1,1,32,32,768]{4,3,2,1,0:T(8,128)(2,1)} %param.13) | copy-start | bytes 4718596
  419.8 24.4 %copy-start.11 = (f32[7,7,768]{2,1,0:T(8,128)S(1)}, f32[7,7,768]{2,1,0:T(8,128)}, u32[]{:S(2)}) copy-start(f32[7,7,768]{2,1,0:T(8,128)} %rev.3) | copy-start | bytes 451588
  444.3 714.7 %copy-start.1 = (s32[1,8,8]{2,1,0:T(8,128)S(1)}, s32[1,8,8]{2,1,0:T(8,128)}, u32[]{:S(2)}) copy-start(s32[1,8,8]{2,1,0:T(8,128)} %param.14) | copy-start | bytes 772
Sparse Core Ops, SparseCore 0:
  10.2 44.5 all-gather.4
  56.4 41.1 all-gather.6
  252.3 41.5 all-gather.8
  295.3 40.9 all-gather.10
  338.6 675.9 reduce-scatter.3
  1019.7 137.5 all-reduce.6
where the time goes:
time: 1180 us; the launch traced here: 1170 us
  waiting for transfers between devices  732 us (62%)
  matrix products  191 us (16%)
  other arithmetic  90.5 us (8%)
  blocking collectives  66.2 us (6%)
  local copies, waits for them, and re-layouts  54.8 us (5%)
  between operations  30.8 us (3%)
    unnamed x7, waiting for transfers between devices  538 us
    psum x1, waiting for transfers between devices, on_device(): lax.psum((kernel_sum, channel_sum, up_bias_sum), ('slide', 'tile'))  141 us
    conv_general_dilated x2, matrix products, depthwise(): lax.conv_general_dilated(extended, kernel[:, :, None, :], (1, 1), 'VALID'...  102 us
    psum x1, blocking collectives, on_device(): lax.psum((kernel_sum, channel_sum, up_bias_sum), ('slide', 'tile'))  66.2 us
    all_gather x1, waiting for transfers between devices, on_device(): lax.all_gather(border_columns(current), 'tile', axis=0, tiled=True)  39.7 us
    unnamed x72, local copies, waits for them, and re-layouts  33.1 us
    conv_general_dilated x1, matrix products, kernel_grad(): lax.conv_general_dilated(extended, kernel, (1, 1), 'VALID', dimension_num...  32.7 us
    concatenate x1, other arithmetic, extend(): return jnp.concatenate([upper, middle, lower], 1)  24.6 us
  transfers between devices with their start and end apart: 6, of which 4 were waited for; matrix products, arithmetic and copies ran while one was open for 15% of the time, Pallas kernels for 0%

commit v1 on v0

v1 whole, which is shorter than its diff:
```python
import functools

import jax
import jax.numpy as jnp
from jax import lax
from jax.experimental import pallas as pl
from jax.experimental.pallas import tpu as pltpu
from jax.sharding import PartitionSpec as P

ln_eps = 1e-06
root_half = 0.7071067811865476
inv_root_two_pi = 0.3989422804014327
f32 = jnp.float32
bf16 = jnp.bfloat16
both_axes = ("slide", "tile")
lanes = 128
side = 32
rim = 3
taps = 7
row_block = 16
own_column = 8
wide = 48
vmem_limit = 58 * 1024 * 1024


def swap(value, distance):
    pairs = [(d, d ^ distance) for d in range(lax.axis_size(both_axes))]
    return lax.ppermute(value, both_axes, pairs)


def pack_kernel(table_ref, tile_ref, *refs):
    outs, column_ref, edge_ref = refs[:7], refs[7], refs[8]
    me = lax.axis_index("tile")
    channels = tile_ref.shape[-1]
    for block in range(channels // lanes):
        here = pl.ds(block * lanes, lanes)
        for which, start, first in ((0, 0, 0), (1, 16, 13)):
            column_ref[...] = tile_ref[:, start : start + 16, here].astype(f32).reshape(16 * side, lanes)
            for c in range(rim):
                edge_ref[which, c, :, here] = column_ref[pl.ds(first + c, side, stride=16), :].astype(bf16)
    for k in range(1, 8):
        peer = jnp.bitwise_xor(me, k)

        def faces(*directions):
            hits = [table_ref[0, me, d] == peer for d in directions]
            return functools.reduce(jnp.logical_or, hits)

        out = outs[k - 1]

        @pl.when(faces(0, 4, 5))
        def _():
            out[...] = tile_ref[0:rim]

        @pl.when(faces(1, 6, 7))
        def _():
            out[...] = tile_ref[side - rim : side]

        @pl.when(faces(2))
        def _():
            out[...] = edge_ref[0]

        @pl.when(faces(3))
        def _():
            out[...] = edge_ref[1]


def pack(table, tile):
    channels = tile.shape[-1]
    strip = jax.ShapeDtypeStruct((rim, side, channels), bf16)
    return pl.pallas_call(
        pack_kernel,
        out_shape=[strip] * 7,
        in_specs=[pl.BlockSpec(memory_space=pltpu.SMEM), pl.BlockSpec(memory_space=pltpu.VMEM)],
        out_specs=[pl.BlockSpec(memory_space=pltpu.VMEM)] * 7,
        scratch_shapes=[
            pltpu.VMEM((16 * side, lanes), f32),
            pltpu.VMEM((2, rim, side, channels), bf16),
        ],
        name="pack_strips",
    )(table, tile)


def exchange_strips(table, tile):
    strips = pack(table, tile)
    return [swap(strips[k - 1], k) for k in range(1, 8)]


def assemble(table_ref, tile_ref, strip_refs, stack_ref, extended_ref):
    me = lax.axis_index("tile")
    stack_ref[0] = jnp.zeros((rim, side, lanes), f32)
    for k in range(1, 8):
        stack_ref[k] = strip_refs[k - 1][...].astype(f32)
    extended_ref[rim : rim + side, own_column : own_column + side, :] = tile_ref[...].astype(f32)

    def strip(direction):
        other = table_ref[0, me, direction]
        index = jnp.where(other < 8, jnp.bitwise_xor(other, me), 0)
        return stack_ref[index]

    last = rim + side
    right = own_column + side
    extended_ref[0:rim, own_column:right, :] = strip(0)
    extended_ref[last : last + rim, own_column:right, :] = strip(1)
    west = strip(2)
    east = strip(3)
    for c in range(rim):
        extended_ref[rim:last, own_column - rim + c, :] = west[c]
        extended_ref[rim:last, right + c, :] = east[c]
    extended_ref[0:rim, 0:8, :] = strip(4)[:, side - 8 :]
    extended_ref[0:rim, right : right + 8, :] = strip(5)[:, :8]
    extended_ref[last : last + rim, 0:8, :] = strip(6)[:, side - 8 :]
    extended_ref[last : last + rim, right : right + 8, :] = strip(7)[:, :8]


def spread_weights(weight_ref, spread_ref, flipped):
    for a in range(taps):
        rows = weight_ref[0, taps - 1 - a if flipped else a]
        for b in range(taps):
            at = taps - 1 - b if flipped else b
            spread_ref[b, a] = jnp.broadcast_to(rows[at : at + 1], (8, lanes))


def depthwise(extended_ref, spread_ref, store):
    def rows(block, carry):
        base = block * row_block
        for w in range(side // 8):
            totals = [None] * row_block
            for b in range(taps):
                start = own_column - rim + b + w * 8
                values = [extended_ref[base + r, start : start + 8, :] for r in range(row_block + taps - 1)]
                for a in range(taps):
                    factor = spread_ref[b, a]
                    for r in range(row_block):
                        term = values[r + a] * factor
                        totals[r] = term if totals[r] is None else totals[r] + term
            for r in range(row_block):
                store(base + r, w * 8, totals[r])
        return carry

    lax.fori_loop(0, side // row_block, rows, 0)


def conv_kernel(table_ref, tile_ref, *refs):
    strip_refs, (weight_ref, gain_ref, shift_ref) = refs[:7], refs[7:10]
    whitened_ref, inv_ref, normed_ref, stack_ref, extended_ref, spread_ref, conv_ref = refs[10:]
    block = pl.program_id(0)
    blocks = whitened_ref.shape[1] // lanes
    assemble(table_ref, tile_ref, strip_refs, stack_ref, extended_ref)
    spread_weights(weight_ref, spread_ref, False)

    def store(row, column, value):
        conv_ref[block, row, column : column + 8, :] = value

    depthwise(extended_ref, spread_ref, store)

    @pl.when(block == blocks - 1)
    def _():
        def norm(row, carry):
            parts = [conv_ref[j, row] for j in range(blocks)]
            count = blocks * lanes
            average = jnp.sum(sum(parts), axis=-1, keepdims=True) / count
            centred = [part - average for part in parts]
            spread = jnp.sum(sum(part * part for part in centred), axis=-1, keepdims=True) / count
            inv_std = lax.rsqrt(spread + ln_eps)
            here = pl.ds(pl.multiple_of(row * side, side), side)
            inv_ref[here, :] = inv_std
            for j in range(blocks):
                at = pl.ds(j * lanes, lanes)
                whitened = centred[j] * inv_std
                whitened_ref[here, at] = whitened
                normed_ref[here, at] = (whitened * gain_ref[:, at] + shift_ref[:, at]).astype(bf16)
            return carry

        lax.fori_loop(0, side, norm, 0)


def strip_specs():
    return [pl.BlockSpec((rim, side, lanes), lambda i: (0, 0, i))] * 7


def conv_norm(table, tile, strips, weight, gain, shift):
    channels = tile.shape[-1]
    pixels = side * side
    blocks = channels // lanes
    whole = lambda i: (0, 0)
    return pl.pallas_call(
        conv_kernel,
        grid=(blocks,),
        out_shape=[
            jax.ShapeDtypeStruct((pixels, channels), f32),
            jax.ShapeDtypeStruct((pixels, 1), f32),
            jax.ShapeDtypeStruct((pixels, channels), bf16),
        ],
        in_specs=[
            pl.BlockSpec(memory_space=pltpu.SMEM),
            pl.BlockSpec((side, side, lanes), lambda i: (0, 0, i)),
            *strip_specs(),
            pl.BlockSpec((1, taps, taps, lanes), lambda i: (0, 0, 0, i)),
            pl.BlockSpec((1, channels), whole),
            pl.BlockSpec((1, channels), whole),
        ],
        out_specs=[
            pl.BlockSpec((pixels, channels), whole),
            pl.BlockSpec((pixels, 1), whole),
            pl.BlockSpec((pixels, channels), whole),
        ],
        scratch_shapes=[
            pltpu.VMEM((8, rim, side, lanes), f32),
            pltpu.VMEM((side + 2 * rim, wide, lanes), f32),
            pltpu.VMEM((taps, taps, 8, lanes), f32),
            pltpu.VMEM((blocks, side, side, lanes), f32),
        ],
        compiler_params=pltpu.CompilerParams(vmem_limit_bytes=vmem_limit),
        cost_estimate=pl.CostEstimate(flops=14_000_000_000, bytes_accessed=10_000_000, transcendentals=0),
        name="conv_norm",
    )(table, tile, *strips, weight, gain, shift)


def mlp_kernel(
    skip_ref, normed_ref, grad_ref, tile_ref, whitened_ref, inv_ref, up_ref, up_bias_ref, down_ref,
    down_bias_ref, scale_ref, gain_ref,
    out_ref, conv_grad_ref, mine_ref, theirs_ref, channel_ref, bias_ref,
    branch_grad_ref, branch_ref, normed_grad_ref, act_ref, pre_grad_ref, pair_ref,
):
    step = pl.program_id(0)
    steps = pl.num_programs(0)
    pixels, channels = normed_ref.shape
    keep = (1 - skip_ref[0, 0]).astype(f32)
    factor = keep * scale_ref[...]
    tile_rows = 256

    @pl.when(step == 0)
    def _():
        branch_grad_ref[...] = (factor * grad_ref[...].astype(f32)).astype(bf16)
        branch_ref[...] = jnp.zeros_like(branch_ref)
        normed_grad_ref[...] = jnp.zeros_like(normed_grad_ref)

    dot = functools.partial(lax.dot_general, preferred_element_type=f32)
    by_rows = (((1,), (1,)), ((), ()))
    plain = (((1,), (0,)), ((), ()))
    by_pixels = (((0,), (0,)), ((), ()))
    bias_sum = jnp.zeros((1, up_ref.shape[0]), f32)
    for m in range(pixels // tile_rows):
        rows = pl.ds(m * tile_rows, tile_rows)
        pre = dot(normed_ref[rows, :], up_ref[...], by_rows) + up_bias_ref[...]
        cdf = 0.5 * (1.0 + lax.erf(pre * root_half))
        slope = cdf + pre * inv_root_two_pi * jnp.exp(-0.5 * pre * pre)
        act = (pre * cdf).astype(bf16)
        act_ref[rows, :] = act
        act_grad = dot(branch_grad_ref[rows, :], down_ref[...], plain)
        pre_grad = (act_grad * slope).astype(bf16)
        pre_grad_ref[rows, :] = pre_grad
        bias_sum = bias_sum + jnp.sum(pre_grad.astype(f32), axis=0, keepdims=True)
        branch_ref[rows, :] += dot(act, down_ref[...], by_rows)
        normed_grad_ref[rows, :] += dot(pre_grad, up_ref[...], plain)
    bias_ref[...] = bias_sum
    quarter = pair_ref.shape[1]
    left = dot(pre_grad_ref[...], normed_ref[...], by_pixels).astype(bf16)
    for q in range(4):
        pair_ref[q, :, :channels] = left[q * quarter : (q + 1) * quarter]
    right = dot(act_ref[...], branch_grad_ref[...], by_pixels).astype(bf16)
    for q in range(4):
        pair_ref[q, :, channels:] = right[q * quarter : (q + 1) * quarter]
    core = lax.axis_index("slide") % 2
    for high in range(2):
        mine_ref[0, high] = pair_ref[2 * high + core]
        theirs_ref[0, high] = pair_ref[2 * high + 1 - core]

    @pl.when(step == steps - 1)
    def _():
        rows_each = 64

        def finish(m, sums):
            rows = pl.ds(pl.multiple_of(m * rows_each, rows_each), rows_each)
            grad = grad_ref[rows, :].astype(f32)
            branch = branch_ref[rows, :] + down_bias_ref[...]
            out_ref[rows, :] = (tile_ref[rows, :].astype(f32) + factor * branch).astype(bf16)
            whitened = whitened_ref[rows, :]
            normed_grad = normed_grad_ref[rows, :]
            scaled = normed_grad * gain_ref[...]
            product = normed_grad * whitened
            mean_one = jnp.sum(scaled, axis=-1, keepdims=True) / channels
            mean_two = jnp.sum(scaled * whitened, axis=-1, keepdims=True) / channels
            conv_grad = inv_ref[rows, :] * (scaled - mean_one - whitened * mean_two)
            conv_grad_ref[rows, :] = conv_grad.astype(bf16)
            terms = (product, normed_grad, branch_grad_ref[rows, :].astype(f32), grad * keep * branch)
            return tuple(
                total + jnp.sum(term.reshape(rows_each // 8, 8, channels), axis=0)
                for total, term in zip(sums, terms)
            )

        zero = jnp.zeros((8, channels), f32)
        sums = lax.fori_loop(0, pixels // rows_each, finish, (zero,) * 4)
        for at in range(4):
            channel_ref[at : at + 1, :] = jnp.sum(sums[at], axis=0, keepdims=True)


def mlp(skip, normed, grad, tile, whitened, inv_std, up, up_bias, down, down_bias, scale, gain):
    pixels, channels = normed.shape
    hidden = up.shape[0]
    steps = 4
    chunk = hidden // steps
    quarter = chunk // 4
    once = pl.Buffered(1)
    whole = lambda i: (0, 0)
    full = lambda *shape: pl.BlockSpec(shape, whole, pipeline_mode=once)
    part = jax.ShapeDtypeStruct((steps, 2, quarter, 2 * channels), bf16)
    part_spec = pl.BlockSpec((1, 2, quarter, 2 * channels), lambda i: (i, 0, 0, 0))
    return pl.pallas_call(
        mlp_kernel,
        grid=(steps,),
        out_shape=[
            jax.ShapeDtypeStruct((pixels, channels), bf16),
            jax.ShapeDtypeStruct((pixels, channels), bf16),
            part,
            part,
            jax.ShapeDtypeStruct((4, channels), f32),
            jax.ShapeDtypeStruct((1, hidden), f32),
        ],
        in_specs=[
            pl.BlockSpec(memory_space=pltpu.SMEM),
            full(pixels, channels),
            full(pixels, channels),
            full(pixels, channels),
            full(pixels, channels),
            full(pixels, 1),
            pl.BlockSpec((chunk, channels), lambda i: (i, 0)),
            pl.BlockSpec((1, chunk), lambda i: (0, i)),
            pl.BlockSpec((channels, chunk), lambda i: (0, i)),
            full(1, channels),
            full(1, channels),
            full(1, channels),
        ],
        out_specs=[
            full(pixels, channels),
            full(pixels, channels),
            part_spec,
            part_spec,
            full(4, channels),
            pl.BlockSpec((1, chunk), lambda i: (0, i)),
        ],
        scratch_shapes=[
            pltpu.VMEM((pixels, channels), bf16),
            pltpu.VMEM((pixels, channels), f32),
            pltpu.VMEM((pixels, channels), f32),
            pltpu.VMEM((pixels, chunk), bf16),
            pltpu.VMEM((pixels, chunk), bf16),
            pltpu.VMEM((4, quarter, 2 * channels), bf16),
        ],
        compiler_params=pltpu.CompilerParams(vmem_limit_bytes=vmem_limit),
        cost_estimate=pl.CostEstimate(flops=40_000_000_000, bytes_accessed=40_000_000, transcendentals=0),
        name="mlp_both",
    )(skip, normed, grad, tile, whitened, inv_std, up, up_bias, down, down_bias, scale, gain)


def kernel_grad_kernel(table_ref, tile_ref, *refs):
    strip_refs, grad_ref, out_ref = refs[:7], refs[7], refs[8]
    stack_ref, extended_ref, wide_ref, total_ref = refs[9:]
    assemble(table_ref, tile_ref, strip_refs, stack_ref, extended_ref)
    wide_ref[...] = grad_ref[...].astype(f32)
    total_ref[...] = jnp.zeros_like(total_ref)

    def rows(block, carry):
        base = block * row_block
        for w in range(side // 8):
            grads = [wide_ref[base + r, w * 8 : w * 8 + 8, :] for r in range(row_block)]
            for b in range(taps):
                start = own_column - rim + b + w * 8
                values = [extended_ref[base + r, start : start + 8, :] for r in range(row_block + taps - 1)]
                for a in range(taps):
                    terms = [values[r + a] * grads[r] for r in range(row_block)]
                    while len(terms) > 1:
                        terms = [terms[i] + terms[i + 1] for i in range(0, len(terms), 2)]
                    total_ref[a, b] += terms[0]
        return carry

    lax.fori_loop(0, side // row_block, rows, 0)
    for a in range(taps):
        out_ref[a] = jnp.sum(total_ref[a], axis=1)


def kernel_grad(table, tile, strips, conv_grad):
    channels = tile.shape[-1]
    block_spec = pl.BlockSpec((side, side, lanes), lambda i: (0, 0, i))
    return pl.pallas_call(
        kernel_grad_kernel,
        grid=(channels // lanes,),
        out_shape=jax.ShapeDtypeStruct((taps, taps, channels), f32),
        in_specs=[pl.BlockSpec(memory_space=pltpu.SMEM), block_spec, *strip_specs(), block_spec],
        out_specs=pl.BlockSpec((taps, taps, lanes), lambda i: (0, 0, i)),
        scratch_shapes=[
            pltpu.VMEM((8, rim, side, lanes), f32),
            pltpu.VMEM((side + 2 * rim, wide, lanes), f32),
            pltpu.VMEM((side, side, lanes), f32),
            pltpu.VMEM((taps, taps, 8, lanes), f32),
        ],
        cost_estimate=pl.CostEstimate(flops=14_000_000_000, bytes_accessed=5_000_000, transcendentals=0),
        name="kernel_grad",
    )(table, tile, *strips, conv_grad)


def back_kernel(table_ref, tile_ref, *refs):
    strip_refs, weight_ref, grad_ref, out_ref = refs[:7], refs[7], refs[8], refs[9]
    stack_ref, extended_ref, spread_ref, total_ref = refs[10:]
    assemble(table_ref, tile_ref, strip_refs, stack_ref, extended_ref)
    spread_weights(weight_ref, spread_ref, True)

    def store(row, column, value):
        total_ref[row, column : column + 8, :] = value

    depthwise(extended_ref, spread_ref, store)
    out_ref[...] = (grad_ref[...].astype(f32) + total_ref[...]).astype(bf16)


def back_conv(table, tile, strips, weight, grad):
    channels = tile.shape[-1]
    block_spec = pl.BlockSpec((side, side, lanes), lambda i: (0, 0, i))
    return pl.pallas_call(
        back_kernel,
        grid=(channels // lanes,),
        out_shape=jax.ShapeDtypeStruct(tile.shape, bf16),
        in_specs=[
            pl.BlockSpec(memory_space=pltpu.SMEM),
            block_spec,
            *strip_specs(),
            pl.BlockSpec((1, taps, taps, lanes), lambda i: (0, 0, 0, i)),
            block_spec,
        ],
        out_specs=block_spec,
        scratch_shapes=[
            pltpu.VMEM((8, rim, side, lanes), f32),
            pltpu.VMEM((side + 2 * rim, wide, lanes), f32),
            pltpu.VMEM((taps, taps, 8, lanes), f32),
            pltpu.VMEM((side, side, lanes), f32),
        ],
        cost_estimate=pl.CostEstimate(flops=14_000_000_000, bytes_accessed=5_000_000, transcendentals=0),
        name="back_conv",
    )(table, tile, *strips, weight, grad)


def pick(value, positions):
    for axis, index in positions:
        value = lax.dynamic_index_in_dim(value, index, axis, keepdims=False)
    return value


def fold(parts, dtype):
    wide_parts = [part.astype(f32) for part in parts]
    while len(wide_parts) > 1:
        wide_parts = [wide_parts[i] + wide_parts[i + 1] for i in range(0, len(wide_parts), 2)]
    return wide_parts[0].astype(dtype)


def reduce_axis(take, distance, dtype):
    kept = take(0)
    arrived = [swap(take(k), k * distance) for k in (1, 2, 3)]
    return fold([kept, *arrived], dtype)


def scatter_sum(mine, theirs):
    slide, tile = lax.axis_index("slide"), lax.axis_index("tile")
    z, y_hi = slide // 4, (slide // 2) % 2
    y_lo, x = tile // 4, tile % 4
    steps, _, quarter, width = mine.shape
    rows = quarter // 8

    def take_x(value):
        return lambda k: pick(value, [(value.ndim - 3, x ^ k)])

    def take_y(value):
        return lambda k: pick(value, [(2, y_lo ^ (k % 2)), (1, y_hi ^ (k // 2))])

    def y_stage(value):
        take = take_y(value)
        arrived = [swap(take(k), d) for k, d in ((1, 4), (2, 16), (3, 20))]
        return fold([take(0), *arrived], bf16)

    received = swap(theirs, 8)
    pieces = []
    for piece in range(2):
        here = slice(2 * piece, 2 * piece + 2)
        both = fold([mine[here], received[here]], bf16).reshape(2, 2, 2, 4, rows, width)
        if piece == 0:
            once = reduce_axis(take_x(both), 1, bf16)
            pieces.append(y_stage(once))
        else:
            once = y_stage(both)
            pieces.append(reduce_axis(take_x(once), 1, bf16))
    last = jnp.concatenate(pieces, 0)
    return reduce_axis(lambda k: pick(last, [(0, z ^ k)]), 32, f32)


def sum_everywhere(value):
    value = value + swap(value, 8)
    for distances in ((1, 2, 3), (4, 16, 20), (32, 64, 96)):
        value = fold([value, *[swap(value, d) for d in distances]], f32)
    return value


def on_device(
    features,
    cotangent,
    neighbours,
    skip_flags,
    dw_weight,
    ln_gain,
    ln_bias,
    up_weight,
    up_bias,
    down_weight,
    down_bias,
    layer_scale,
):
    channels = features.shape[-1]
    hidden = up_weight.shape[1]
    tile = features[0, 0]
    grad = cotangent[0, 0]
    flat = (side * side, channels)
    strips = exchange_strips(neighbours, tile)
    whitened, inv_std, normed = conv_norm(neighbours, tile, strips, dw_weight, ln_gain, ln_bias)
    out, conv_grad, mine, theirs, channel_sums, bias_sums = mlp(
        skip_flags, normed, grad.reshape(flat), tile.reshape(flat), whitened, inv_std,
        up_weight[0], up_bias, down_weight[0], down_bias, layer_scale, ln_gain,
    )
    conv_grad = conv_grad.reshape(tile.shape)
    grad_strips = exchange_strips(neighbours, conv_grad)
    weight_rows = scatter_sum(mine, theirs)
    kernel_sums = kernel_grad(neighbours, tile, strips, conv_grad)
    small = jnp.concatenate(
        [kernel_sums.reshape(taps * taps, channels), channel_sums, bias_sums.reshape(-1, channels)], 0
    )
    small = sum_everywhere(small)
    input_grad = back_conv(neighbours, conv_grad, grad_strips, dw_weight, grad)
    split = taps * taps
    return (
        out.reshape(features.shape),
        input_grad[None, None],
        weight_rows[None],
        small[:split].reshape(1, taps, taps, channels),
        small[split : split + 4][None],
        small[split + 4 :].reshape(1, hidden),
    )


def solution(mesh):
    return jax.shard_map(
        on_device,
        mesh=mesh,
        in_specs=(
            P("slide", "tile", None, None, None),
            P("slide", "tile", None, None, None),
            P("slide", None, None),
            P(None, "slide"),
            P(),
            P(),
            P(),
            P(),
            P(),
            P(),
            P(),
            P(),
        ),
        out_specs=(
            P("slide", "tile", None, None, None),
            P("slide", "tile", None, None, None),
            P(None, ("slide", "tile"), None),
            P(),
            P(),
            P(),
        ),
        check_vma=False,
    )
```

time: 1180 us -> 230 us (0.19); the launches traced: 1170 us -> 229 us
  waiting for transfers between devices: 732 us -> 50.7 us
  matrix products: 191 us -> 0 us
  Pallas kernels: 0 us -> 97.9 us
  other arithmetic: 90.5 us -> 9.18 us
  blocking collectives: 66.2 us -> 0 us
  starting transfers between devices: 0.82 us -> 60.6 us
  local copies, waits for them, and re-layouts: 54.8 us -> 9.42 us
  between operations: 30.8 us -> 1.7 us
    unnamed x7 -> x0, waiting for transfers between devices: 538 us -> none
    psum x1 -> x0, waiting for transfers between devices: 141 us -> none  [on_device(): lax.psum((kernel_sum, channel_sum, up_bias_sum), ('slide', 'tile'))]
    conv_general_dilated x3 -> x0, matrix products: 135 us -> none  [the longest x2 102 us: depthwise(): lax.conv_general_dilated(extended, kernel[:, :, None, :], (1, 1), 'VALID'...]
    pallas_call x0 -> x6, Pallas kernels: none -> 97.9 us  [the longest x1 43.4 us: mlp(): pl.pallas_call(mlp_kernel, grid=(steps,), out_shape=[jax.ShapeDtypeStruct...]
    psum x1 -> x0, blocking collectives: 66.2 us -> none  [on_device(): lax.psum((kernel_sum, channel_sum, up_bias_sum), ('slide', 'tile'))]
    ppermute x0 -> x40, starting transfers between devices: none -> 60.6 us  [swap(): return lax.ppermute(value, both_axes, pairs)]
    dot_general x6 -> x0, matrix products: 55.8 us -> none  [the longest x2 20 us: contract(): lax.dot_general(left, right, (((1,), (1,)), ((), ())), preferred_element_...]
    all_gather x4 -> x0, waiting for transfers between devices: 53 us -> none  [the longest x1 39.7 us: on_device(): lax.all_gather(border_columns(current), 'tile', axis=0, tiled=True)]
  transfers between devices with their start and end apart: 6 -> 40, of which waited for: 4 -> 16; matrix products, arithmetic and copies ran while one was open for 15% -> 7% of each run, Pallas kernels for 0% -> 13%
where the time goes in v1:
time: 230 us; the launch traced here: 229 us
  Pallas kernels  97.9 us (43%)
  starting transfers between devices  60.6 us (26%)
  waiting for transfers between devices  50.7 us (22%)
  local copies, waits for them, and re-layouts  9.42 us (4%)
  other arithmetic  9.18 us (4%)
    ppermute x40, starting transfers between devices, swap(): return lax.ppermute(value, both_axes, pairs)  60.6 us
    ppermute x40, waiting for transfers between devices, swap(): return lax.ppermute(value, both_axes, pairs)  50.7 us
    pallas_call x1, Pallas kernels, mlp(): pl.pallas_call(mlp_kernel, grid=(steps,), out_shape=[jax.ShapeDtypeStruct...  43.4 us
    pallas_call x1, Pallas kernels, conv_norm(): pl.pallas_call(conv_kernel, grid=(blocks,), out_shape=[jax.ShapeDtypeStru...  21.1 us
    pallas_call x1, Pallas kernels, kernel_grad(): pl.pallas_call(kernel_grad_kernel, grid=(channels // lanes,), out_shape=j...  13.8 us
    pallas_call x1, Pallas kernels, back_conv(): pl.pallas_call(back_kernel, grid=(channels // lanes,), out_shape=jax.Shap...  13.7 us
    convert_element_type x5, other arithmetic, fold(): return wide_parts[0].astype(dtype)  6.57 us
    pallas_call x2, Pallas kernels, pack(): pl.pallas_call(pack_kernel, out_shape=[strip] * 7, in_specs=[pl.BlockSpec...  5.87 us
  transfers between devices with their start and end apart: 40, of which 16 were waited for; matrix products, arithmetic and copies ran while one was open for 7% of the time, Pallas kernels for 13%

profile of v1, /device:TPU:0, one launch (start us, length us, event | category | flops | bytes accessed | tf_op | source)
XLA Modules:
  0.0 229.5 jit_solution(4777241573237783117)
XLA Ops:
  0.6 2.9 %pack_strips.2 = (bf16[3,32,768]{2,1,0:T(8,128)(2,1)}, bf16[3,32,768]{2,1,0:T(8,128)(2,1)}, bf16[3,32,768]{2,1,0:T(8,128)(2,1)}, bf16[3,32,768]{2,1,0:T(8,128)(2...) custom-call(s32[1,8,8]{2,1,0:T(8,128)} %table_ref.9, ...), custom_call_target="tpu_custom_call" | custom-call | tf_op jit(solution)/shard_map/pack_strips/pallas_call | solution.py:70
  3.6 1.6 collective-permute-start
  5.1 2.7 %collective-permute-start.1 = (bf16[3,32,768]{2,1,0:T(8,128)(2,1)}, bf16[3,32,768]{2,1,0:T(8,128)(2,1)S(1)}, u32[]{:S(2)}, u32[]{:S(2)}) collective-permute-start(bf16[3,32,768]{2,1,0:T(8,128)(2,1)} %get-tuple-element.30), channel_id=1, source_target_pairs={{0,2},{1,3},{2,0},{3,1},{4,6},{5,7},{6,4},{7,5},{8,10},{9,11},{10,... | collective-permute-start | bytes 442376 | tf_op jit(solution)/shard_map/ppermute | solution.py:28
  7.9 0.4 collective-permute-start.2
  8.3 1.7 collective-permute-start.3
  10.1 5.0 %collective-permute-start.5 = (bf16[3,32,768]{2,1,0:T(8,128)(2,1)}, bf16[3,32,768]{2,1,0:T(8,128)(2,1)S(1)}, u32[]{:S(2)}, u32[]{:S(2)}) collective-permute-start(bf16[3,32,768]{2,1,0:T(8,128)(2,1)} %get-tuple-element.34), channel_id=1, source_target_pairs={{0,6},{1,7},{2,4},{3,5},{4,2},{5,3},{6,0},{7,1},{8,14},{9,15},{10,... | collective-permute-start | bytes 442376 | tf_op jit(solution)/shard_map/ppermute | solution.py:28
  15.1 0.9 collective-permute-done.1.refs_1_
  16.0 1.4 collective-permute-start.6
  17.3 1.6 copy.18.refs_7_
  19.7 2.5 %collective-permute-done.5.refs_5_ = bf16[3,32,768]{2,1,0:T(8,128)(2,1)S(1)} collective-permute-done((bf16[3,32,768]{2,1,0:T(8,128)(2,1)}, bf16[3,32,768]{2,1,0:T(8,128)(2,1)S(1)}, u32[]{:S(2)}, u32[]{:S(2)}) %collective-permute-start.5) | collective-permute-done | bytes 147488 | tf_op jit(solution)/shard_map/ppermute | solution.py:28
  22.1 2.4 %collective-permute-done.6.refs_6_ = bf16[3,32,768]{2,1,0:T(8,128)(2,1)S(1)} collective-permute-done((bf16[3,32,768]{2,1,0:T(8,128)(2,1)}, bf16[3,32,768]{2,1,0:T(8,128)(2,1)S(1)}, u32[]{:S(2)}, u32[]{:S(2)}) %collective-permute-start.6) | collective-permute-done | bytes 147488 | tf_op jit(solution)/shard_map/ppermute | solution.py:28
  24.6 0.6 copy-done.17
  25.3 21.1 %conv_norm.1 = (f32[1024,768]{1,0:T(8,128)}, f32[1024,1]{1,0:T(8,128)}, bf16[1024,768]{1,0:T(8,128)(2,1)}) custom-call(s32[1,8,8]{2,1,0:T(8,128)} %table_ref.9, bf16[32,32,768]{2,1,0:T(8,128)(2,1)} %bitcast.79, bf16[3,32,768]{2,1,0:T(8,128)(2,1)} %copy-done.9, bf16[3,32,768]{2,1,0:T(8,128)(2,1)} %copy-done.11, bf16[3,32,768]{2,1,0:T(8,128)(2,1)} %copy-done.12, ...), custom_call_target="tpu_custom_call" | custom-call | flops 14000000000 | bytes 10000000 | tf_op jit(solution)/shard_map/conv_norm/pallas_call | solution.py:186
  46.4 43.4 %mlp_both.1 = (bf16[1024,768]{1,0:T(8,128)(2,1)}, bf16[1024,768]{1,0:T(8,128)(2,1)}, bf16[4,2,192,1536]{3,2,1,0:T(8,128)(2,1)}, bf16[4,2,192,1536]{3,2,1,0:T(8,1...) custom-call(s32[1,1]{1,0:T(1,128)S(6)} %copy.49.skip_ref, bf16[1024,768]{1,0:T(8,128)(2,1)} %get-tuple-element.36.normed_ref, ...), custom_call_target="tpu_custom_call" | custom-call | flops 40000000000 | bytes 40000000 | tf_op jit(solution)/shard_map/mlp_both/pallas_call | solution.py:309
  90.1 13.8 %kernel_grad.1 = f32[7,7,768]{2,1,0:T(8,128)} custom-call(s32[1,8,8]{2,1,0:T(8,128)} %table_ref.9, bf16[32,32,768]{2,1,0:T(8,128)(2,1)} %bitcast.81, bf16[3,32,768]{2,1,0:T(8,128)(2,1)} %copy-done.9, bf16[3,32,768]{2,1,0:T(8,128)(2,1)} %copy-done.11, bf16[3,32,768]{2,1,0:T(8,128)(2,1)} %copy-done.12, bf16[3,32,768]{2,1,0:T(8,128)(2,1)} %copy-done.14, ...), custom_call_target="tpu_custom_call" | custom-call | flops 14000000000 | bytes 5000000 | tf_op jit(solution)/shard_map/kernel_grad/pallas_call | solution.py:385
  103.9 0.9 reshape.66
  104.9 0.5 broadcast.8
  105.4 0.7 reduce.3
  106.1 0.6 collective-permute-start.30
  106.7 1.1 collective-permute-done.30
  108.0 2.7 %collective-permute-start.32 = (f32[57,768]{1,0:T(8,128)S(1)}, f32[57,768]{1,0:T(8,128)S(1)}, u32[]{:S(2)}, u32[]{:S(2)}) collective-permute-start(f32[57,768]{1,0:T(8,128)S(1)} %fusion.18), channel_id=1, source_target_pairs={{0,2},{1,3},{2,0},{3,1},{4,6},{5,7},{6,4},{7,5},{8,10},{9,11},{10,... | collective-permute-start | bytes 525320 | tf_op jit(solution)/shard_map/ppermute | solution.py:28
  110.7 1.9 collective-permute-start.33
  112.6 3.0 %collective-permute-done.31 = f32[57,768]{1,0:T(8,128)S(1)} collective-permute-done((f32[57,768]{1,0:T(8,128)S(1)}, f32[57,768]{1,0:T(8,128)S(1)}, u32[]{:S(2)}, u32[]{:S(2)}) %collective-permute-start.31) | collective-permute-done | bytes 175136 | tf_op jit(solution)/shard_map/ppermute | solution.py:28
  115.6 4.6 %collective-permute-done.32 = f32[57,768]{1,0:T(8,128)S(1)} collective-permute-done((f32[57,768]{1,0:T(8,128)S(1)}, f32[57,768]{1,0:T(8,128)S(1)}, u32[]{:S(2)}, u32[]{:S(2)}) %collective-permute-start.32) | collective-permute-done | bytes 175136 | tf_op jit(solution)/shard_map/ppermute | solution.py:28
  120.1 2.6 %collective-permute-done.33 = f32[57,768]{1,0:T(8,128)S(1)} collective-permute-done((f32[57,768]{1,0:T(8,128)S(1)}, f32[57,768]{1,0:T(8,128)S(1)}, u32[]{:S(2)}, u32[]{:S(2)}) %collective-permute-start.33) | collective-permute-done | bytes 175136 | tf_op jit(solution)/shard_map/ppermute | solution.py:28
  122.8 2.0 collective-permute-start.34
  124.8 3.0 %collective-permute-start.35 = (f32[57,768]{1,0:T(8,128)S(1)}, f32[57,768]{1,0:T(8,128)S(1)}, u32[]{:S(2)}, u32[]{:S(2)}) collective-permute-start(f32[57,768]{1,0:T(8,128)S(1)} %add_add_fusion.2), channel_id=1, source_target_pairs={{0,16},{1,17},{2,18},{3,19},{4,20},{5,21},{6,22},{7,23},{8,24},{9,... | collective-permute-start | bytes 525320 | tf_op jit(solution)/shard_map/ppermute | solution.py:28
  127.8 2.9 %pack_strips.3 = (bf16[3,32,768]{2,1,0:T(8,128)(2,1)}, bf16[3,32,768]{2,1,0:T(8,128)(2,1)}, bf16[3,32,768]{2,1,0:T(8,128)(2,1)}, bf16[3,32,768]{2,1,0:T(8,128)(2...) custom-call(s32[1,8,8]{2,1,0:T(8,128)} %table_ref.9, ...), custom_call_target="tpu_custom_call" | custom-call | tf_op jit(solution)/shard_map/pack_strips/pallas_call | solution.py:70
  130.7 0.4 collective-permute-start.10
  131.2 12.2 %collective-permute-done.35 = f32[57,768]{1,0:T(8,128)S(1)} collective-permute-done((f32[57,768]{1,0:T(8,128)S(1)}, f32[57,768]{1,0:T(8,128)S(1)}, u32[]{:S(2)}, u32[]{:S(2)}) %collective-permute-start.35) | collective-permute-done | bytes 175136 | tf_op jit(solution)/shard_map/ppermute | solution.py:28
  143.5 4.4 %collective-permute-start.7 = (bf16[3,32,768]{2,1,0:T(8,128)(2,1)}, bf16[3,32,768]{2,1,0:T(8,128)(2,1)S(1)}, u32[]{:S(2)}, u32[]{:S(2)}) collective-permute-start(bf16[3,32,768]{2,1,0:T(8,128)(2,1)} %get-tuple-element.41), channel_id=1, source_target_pairs={{0,1},{1,0},{2,3},{3,2},{4,5},{5,4},{6,7},{7,6},{8,9},{9,8},{10,11... | collective-permute-start | bytes 442376 | tf_op jit(solution)/shard_map/ppermute | solution.py:28
  148.0 4.4 %add_convert_fusion = (bf16[2,2,192,1536]{3,2,1,0:T(8,128)(2,1)S(1)}, bf16[2,2,192,1536]{3,2,1,0:T(8,128)(2,1)S(1)}) fusion(bf16[4,2,192,1536]{3,2,1,0:T(8,128)(2,1)} %collective-permute-done.14, bf16[4,2,192,1536]{3,2,1,0:T(8,128)(2,1)} %get-tuple-element.48), kind=kLoop, calls=%fused_computation | loop fusion | flops 9437184 | bytes 14155776 | tf_op jit(solution)/shard_map/convert_element_type | solution.py:451
  152.5 0.5 collective-permute-start.8
  153.0 2.3 %collective-permute-start.9 = (bf16[3,32,768]{2,1,0:T(8,128)(2,1)S(1)}, bf16[3,32,768]{2,1,0:T(8,128)(2,1)S(1)}, u32[]{:S(2)}, u32[]{:S(2)}) collective-permute-start(bf16[3,32,768]{2,1,0:T(8,128)(2,1)S(1)} %copy-done.5), channel_id=1, source_target_pairs={{0,3},{1,2},{2,1},{3,0},{4,7},{5,6},{6,5},{7,4},{8,11},{9,10},{10,... | collective-permute-start | bytes 442376 | tf_op jit(solution)/shard_map/ppermute | solution.py:28
  155.3 1.9 collective-permute-start.37
  157.5 0.9 copy.45
  158.4 0.9 copy.44
  159.2 0.9 copy.43
  160.1 3.6 %collective-permute-start.38 = (f32[57,768]{1,0:T(8,128)S(1)}, f32[57,768]{1,0:T(8,128)S(1)}, u32[]{:S(2)}, u32[]{:S(2)}) collective-permute-start(f32[57,768]{1,0:T(8,128)S(1)} %add_add_fusion.1), channel_id=1, source_target_pairs={{0,64},{1,65},{2,66},{3,67},{4,68},{5,69},{6,70},{7,71},{8,72},{9,... | collective-permute-start | bytes 525320 | tf_op jit(solution)/shard_map/ppermute | solution.py:28
  164.0 0.4 copy-done.8
  164.4 4.2 %collective-permute-start.23 = (bf16[2,4,24,1536]{3,2,0,1:T(8,128)(2,1)}, bf16[2,4,24,1536]{3,2,0,1:T(8,128)(2,1)}, u32[]{:S(2)}, u32[]{:S(2)}) collective-permute-start(bf16[2,4,24,1536]{3,2,0,1:T(8,128)(2,1)} %bitcast.70), channel_id=1, source_target_pairs={{0,20},{1,21},{2,22},{3,23},{4,16},{5,17},{6,18},{7,19},{8,28},{9,... | collective-permute-start | bytes 1769480 | tf_op jit(solution)/shard_map/ppermute | solution.py:28
  168.6 13.7 %back_conv.1 = bf16[32,32,768]{2,1,0:T(8,128)(2,1)} custom-call(s32[1,8,8]{2,1,0:T(8,128)} %table_ref.9, bf16[32,32,768]{2,1,0:T(8,128)(2,1)} %bitcast.84, bf16[3,32,768]{2,1,0:T(8,128)(2,1)} %copy-done.8, bf16[3,32,768]{2,1,0:T(8,128)(2,1)} %copy-done.10, bf16[3,32,768]{2,1,0:T(8,128)(2,1)} %copy-done.13, bf16[3,32,768]{2,1,0:T(8,128)(2,1)} %copy-done.2, ...), custom_call_target="tpu_custom_call" | custom-call | flops 14000000000 | bytes 5000000 | tf_op jit(solution)/shard_map/back_conv/pallas_call | solution.py:418
  182.3 1.0 add_add_fusion
  183.5 0.9 collective-permute-start.15
  184.4 1.7 collective-permute-start.16
  186.2 2.4 %collective-permute-start.17 = (bf16[2,2,2,24,1536]{4,3,0,2,1:T(8,128)(2,1)S(1)}, bf16[2,2,2,24,1536]{4,3,0,2,1:T(8,128)(2,1)S(1)}, u32[]{:S(2)}, u32[]{:S(2)}) collective-permute-start(bf16[2,2,2,24,1536]{4,3,0,2,1:T(8,128)(2,1)S(1)} %bitcast.86), channel_id=1, source_target_pairs={{0,3},{1,2},{2,1},{3,0},{4,7},{5,6},{6,5},{7,4},{8,11},{9,10},{10,... | collective-permute-start | bytes 1769480 | tf_op jit(solution)/shard_map/ppermute | solution.py:28
  188.6 1.7 fusion.1
  190.4 2.4 %collective-permute-start.25 = (bf16[2,24,1536]{2,1,0:T(8,128)(2,1)S(1)}, bf16[2,24,1536]{2,1,0:T(8,128)(2,1)S(1)}, u32[]{:S(2)}, u32[]{:S(2)}) collective-permute-start(bf16[2,24,1536]{2,1,0:T(8,128)(2,1)S(1)} %get-tuple-element.64), channel_id=1, source_target_pairs={{0,2},{1,3},{2,0},{3,1},{4,6},{5,7},{6,4},{7,5},{8,10},{9,11},{10,... | collective-permute-start | bytes 442376 | tf_op jit(solution)/shard_map/ppermute | solution.py:28
  192.8 4.1 %collective-permute-done.15 = bf16[2,2,2,24,1536]{4,3,0,2,1:T(8,128)(2,1)S(1)} collective-permute-done((bf16[2,2,2,24,1536]{4,3,0,2,1:T(8,128)(2,1)S(1)}, bf16[2,2,2,24,1536]{4,3,0,2,1:T(8,128)(2,1)S(1)}, u32[]{:S(2)}, u32[]{:S(2)}) %collective-permute-start.15) | collective-permute-done | bytes 589856 | tf_op jit(solution)/shard_map/ppermute | solution.py:28
  197.0 2.3 collective-permute-start.26
  199.2 5.9 %collective-permute-done.16 = bf16[2,2,2,24,1536]{4,3,0,2,1:T(8,128)(2,1)S(1)} collective-permute-done((bf16[2,2,2,24,1536]{4,3,0,2,1:T(8,128)(2,1)S(1)}, bf16[2,2,2,24,1536]{4,3,0,2,1:T(8,128)(2,1)S(1)}, u32[]{:S(2)}, u32[]{:S(2)}) %collective-permute-start.16) | collective-permute-done | bytes 589856 | tf_op jit(solution)/shard_map/ppermute | solution.py:28
  205.1 4.4 %collective-permute-done.17 = bf16[2,2,2,24,1536]{4,3,0,2,1:T(8,128)(2,1)S(1)} collective-permute-done((bf16[2,2,2,24,1536]{4,3,0,2,1:T(8,128)(2,1)S(1)}, bf16[2,2,2,24,1536]{4,3,0,2,1:T(8,128)(2,1)S(1)}, u32[]{:S(2)}, u32[]{:S(2)}) %collective-permute-start.17) | collective-permute-done | bytes 589856 | tf_op jit(solution)/shard_map/ppermute | solution.py:28
  209.8 0.5 collective-permute-start.18
  210.3 2.0 collective-permute-start.19
  212.3 2.3 %collective-permute-start.20 = (bf16[2,24,1536]{2,1,0:T(8,128)(2,1)S(1)}, bf16[2,24,1536]{2,1,0:T(8,128)(2,1)S(1)}, u32[]{:S(2)}, u32[]{:S(2)}) collective-permute-start(bf16[2,24,1536]{2,1,0:T(8,128)(2,1)S(1)} %get-tuple-element.66), channel_id=1, source_target_pairs={{0,20},{1,21},{2,22},{3,23},{4,16},{5,17},{6,18},{7,19},{8,28},{9,... | collective-permute-start | bytes 442376 | tf_op jit(solution)/shard_map/ppermute | solution.py:28
  215.0 1.9 collective-permute-done.19
  217.0 1.7 collective-permute-done.20
  219.0 4.2 %collective-permute-start.28 = (bf16[24,1536]{1,0:T(8,128)(2,1)S(1)}, bf16[24,1536]{1,0:T(8,128)(2,1)S(1)}, u32[]{:S(2)}, u32[]{:S(2)}) collective-permute-start(bf16[24,1536]{1,0:T(8,128)(2,1)S(1)} %get-tuple-element.69), channel_id=1, source_target_pairs={{0,64},{1,65},{2,66},{3,67},{4,68},{5,69},{6,70},{7,71},{8,72},{9,... | collective-permute-start | bytes 221192 | tf_op jit(solution)/shard_map/ppermute | solution.py:28
  223.6 0.6 slice_bitcast_fusion
  224.2 0.8 reshape.68
  225.0 0.6 copy.30
  225.7 0.7 collective-permute-done.28
  226.3 2.4 %collective-permute-done.29 = bf16[24,1536]{1,0:T(8,128)(2,1)S(1)} collective-permute-done((bf16[24,1536]{1,0:T(8,128)(2,1)S(1)}, bf16[24,1536]{1,0:T(8,128)(2,1)S(1)}, u32[]{:S(2)}, u32[]{:S(2)}) %collective-permute-start.29) | collective-permute-done | bytes 73760 | tf_op jit(solution)/shard_map/ppermute | solution.py:28
  228.8 0.7 fusion.9
  (89 shorter events, 3.4 us)
Async XLA Ops:
  3.6 6.5 %collective-permute-start = (bf16[3,32,768]{2,1,0:T(8,128)(2,1)}, bf16[3,32,768]{2,1,0:T(8,128)(2,1)S(1)}, u32[]{:S(2)}, u32[]{:S(2)}) collective-permute-start(bf16[3,32,768]{2,1,0:T(8,128)(2,1)} %get-tuple-element.29), channel_id=1, source_target_pairs={{0,1},{1,0},{2,3},{3,2},{4,5},{5,4},{6,7},{7,6},{8,9},{9,8},{10,11... | collective-permute-start | bytes 442376 | tf_op jit(solution)/shard_map/ppermute | solution.py:28
  5.1 10.8 %collective-permute-start.1 = (bf16[3,32,768]{2,1,0:T(8,128)(2,1)}, bf16[3,32,768]{2,1,0:T(8,128)(2,1)S(1)}, u32[]{:S(2)}, u32[]{:S(2)}) collective-permute-start(bf16[3,32,768]{2,1,0:T(8,128)(2,1)} %get-tuple-element.30), channel_id=1, source_target_pairs={{0,2},{1,3},{2,0},{3,1},{4,6},{5,7},{6,4},{7,5},{8,10},{9,11},{10,... | collective-permute-start | bytes 442376 | tf_op jit(solution)/shard_map/ppermute | solution.py:28
  7.9 11.7 %collective-permute-start.2 = (bf16[3,32,768]{2,1,0:T(8,128)(2,1)}, bf16[3,32,768]{2,1,0:T(8,128)(2,1)S(1)}, u32[]{:S(2)}, u32[]{:S(2)}) collective-permute-start(bf16[3,32,768]{2,1,0:T(8,128)(2,1)} %get-tuple-element.31), channel_id=1, source_target_pairs={{0,3},{1,2},{2,1},{3,0},{4,7},{5,6},{6,5},{7,4},{8,11},{9,10},{10,... | collective-permute-start | bytes 442376 | tf_op jit(solution)/shard_map/ppermute | solution.py:28
  8.3 11.4 %collective-permute-start.3 = (bf16[3,32,768]{2,1,0:T(8,128)(2,1)}, bf16[3,32,768]{2,1,0:T(8,128)(2,1)S(1)}, u32[]{:S(2)}, u32[]{:S(2)}) collective-permute-start(bf16[3,32,768]{2,1,0:T(8,128)(2,1)} %get-tuple-element.32), channel_id=1, source_target_pairs={{0,4},{1,5},{2,6},{3,7},{4,0},{5,1},{6,2},{7,3},{8,12},{9,13},{10,... | collective-permute-start | bytes 442376 | tf_op jit(solution)/shard_map/ppermute | solution.py:28
  9.9 9.7 %collective-permute-start.4 = (bf16[3,32,768]{2,1,0:T(8,128)(2,1)}, bf16[3,32,768]{2,1,0:T(8,128)(2,1)S(1)}, u32[]{:S(2)}, u32[]{:S(2)}) collective-permute-start(bf16[3,32,768]{2,1,0:T(8,128)(2,1)} %get-tuple-element.33), channel_id=1, source_target_pairs={{0,5},{1,4},{2,7},{3,6},{4,1},{5,0},{6,3},{7,2},{8,13},{9,12},{10,... | collective-permute-start | bytes 442376 | tf_op jit(solution)/shard_map/ppermute | solution.py:28
  10.1 14.5 %copy-start.9 = (bf16[3,32,768]{2,1,0:T(8,128)(2,1)}, bf16[3,32,768]{2,1,0:T(8,128)(2,1)S(1)}, u32[]{:S(2)}) copy-start(bf16[3,32,768]{2,1,0:T(8,128)(2,1)S(1)} %collective-permute-done.refs_0_) | copy-start | bytes 442372
  10.1 12.0 %collective-permute-start.5 = (bf16[3,32,768]{2,1,0:T(8,128)(2,1)}, bf16[3,32,768]{2,1,0:T(8,128)(2,1)S(1)}, u32[]{:S(2)}, u32[]{:S(2)}) collective-permute-start(bf16[3,32,768]{2,1,0:T(8,128)(2,1)} %get-tuple-element.34), channel_id=1, source_target_pairs={{0,6},{1,7},{2,4},{3,5},{4,2},{5,3},{6,0},{7,1},{8,14},{9,15},{10,... | collective-permute-start | bytes 442376 | tf_op jit(solution)/shard_map/ppermute | solution.py:28
  15.9 8.6 %copy-start.11 = (bf16[3,32,768]{2,1,0:T(8,128)(2,1)}, bf16[3,32,768]{2,1,0:T(8,128)(2,1)S(1)}, u32[]{:S(2)}) copy-start(bf16[3,32,768]{2,1,0:T(8,128)(2,1)S(1)} %collective-permute-done.1.refs_1_) | copy-start | bytes 442372
  16.0 8.6 %collective-permute-start.6 = (bf16[3,32,768]{2,1,0:T(8,128)(2,1)}, bf16[3,32,768]{2,1,0:T(8,128)(2,1)S(1)}, u32[]{:S(2)}, u32[]{:S(2)}) collective-permute-start(bf16[3,32,768]{2,1,0:T(8,128)(2,1)} %get-tuple-element.35), channel_id=1, source_target_pairs={{0,7},{1,6},{2,5},{3,4},{4,3},{5,2},{6,1},{7,0},{8,15},{9,14},{10,... | collective-permute-start | bytes 442376 | tf_op jit(solution)/shard_map/ppermute | solution.py:28
  19.6 5.0 %copy-start.12 = (bf16[3,32,768]{2,1,0:T(8,128)(2,1)}, bf16[3,32,768]{2,1,0:T(8,128)(2,1)S(1)}, u32[]{:S(2)}) copy-start(bf16[3,32,768]{2,1,0:T(8,128)(2,1)S(1)} %collective-permute-done.2.refs_2_) | copy-start | bytes 442372
  19.6 5.0 %copy-start.14 = (bf16[3,32,768]{2,1,0:T(8,128)(2,1)}, bf16[3,32,768]{2,1,0:T(8,128)(2,1)S(1)}, u32[]{:S(2)}) copy-start(bf16[3,32,768]{2,1,0:T(8,128)(2,1)S(1)} %collective-permute-done.3.refs_3_) | copy-start | bytes 442372
  19.6 5.0 %copy-start.15 = (bf16[3,32,768]{2,1,0:T(8,128)(2,1)}, bf16[3,32,768]{2,1,0:T(8,128)(2,1)S(1)}, u32[]{:S(2)}) copy-start(bf16[3,32,768]{2,1,0:T(8,128)(2,1)S(1)} %collective-permute-done.4.refs_4_) | copy-start | bytes 442372
  22.1 2.5 %copy-start.16 = (bf16[3,32,768]{2,1,0:T(8,128)(2,1)}, bf16[3,32,768]{2,1,0:T(8,128)(2,1)S(1)}, u32[]{:S(2)}) copy-start(bf16[3,32,768]{2,1,0:T(8,128)(2,1)S(1)} %collective-permute-done.5.refs_5_) | copy-start | bytes 442372
  24.6 0.6 copy-start.17
  89.8 53.8 %collective-permute-start.14 = (bf16[4,2,192,1536]{3,2,1,0:T(8,128)(2,1)}, bf16[4,2,192,1536]{3,2,1,0:T(8,128)(2,1)}, u32[]{:S(2)}, u32[]{:S(2)}) collective-permute-start(bf16[4,2,192,1536]{3,2,1,0:T(8,128)(2,1)} %get-tuple-element.49), channel_id=1, source_target_pairs={{0,8},{1,9},{2,10},{3,11},{4,12},{5,13},{6,14},{7,15},{8,0},{9,1},... | collective-permute-start | bytes 14155784 | tf_op jit(solution)/shard_map/ppermute | solution.py:28
  90.1 15.3 %copy-start.1 = (f32[1,3072]{1,0:T(1,128)S(1)}, f32[1,3072]{1,0:T(1,128)}, u32[]{:S(2)}) copy-start(f32[1,3072]{1,0:T(1,128)} %get-tuple-element.51) | copy-start | bytes 36868
  90.1 16.0 %copy-start = (f32[4,768]{1,0:T(4,128)S(1)}, f32[4,768]{1,0:T(4,128)}, u32[]{:S(2)}) copy-start(f32[4,768]{1,0:T(4,128)} %get-tuple-element.50) | copy-start | bytes 36868
  106.1 1.6 collective-permute-start.30
  107.8 7.8 %collective-permute-start.31 = (f32[57,768]{1,0:T(8,128)S(1)}, f32[57,768]{1,0:T(8,128)S(1)}, u32[]{:S(2)}, u32[]{:S(2)}) collective-permute-start(f32[57,768]{1,0:T(8,128)S(1)} %fusion.18), channel_id=1, source_target_pairs={{0,1},{1,0},{2,3},{3,2},{4,5},{5,4},{6,7},{7,6},{8,9},{9,8},{10,11... | collective-permute-start | bytes 525320 | tf_op jit(solution)/shard_map/ppermute | solution.py:28
  108.0 12.1 %collective-permute-start.32 = (f32[57,768]{1,0:T(8,128)S(1)}, f32[57,768]{1,0:T(8,128)S(1)}, u32[]{:S(2)}, u32[]{:S(2)}) collective-permute-start(f32[57,768]{1,0:T(8,128)S(1)} %fusion.18), channel_id=1, source_target_pairs={{0,2},{1,3},{2,0},{3,1},{4,6},{5,7},{6,4},{7,5},{8,10},{9,11},{10,... | collective-permute-start | bytes 525320 | tf_op jit(solution)/shard_map/ppermute | solution.py:28
  110.7 12.0 %collective-permute-start.33 = (f32[57,768]{1,0:T(8,128)S(1)}, f32[57,768]{1,0:T(8,128)S(1)}, u32[]{:S(2)}, u32[]{:S(2)}) collective-permute-start(f32[57,768]{1,0:T(8,128)S(1)} %fusion.18), channel_id=1, source_target_pairs={{0,3},{1,2},{2,1},{3,0},{4,7},{5,6},{6,5},{7,4},{8,11},{9,10},{10,... | collective-permute-start | bytes 525320 | tf_op jit(solution)/shard_map/ppermute | solution.py:28
  122.8 8.4 %collective-permute-start.34 = (f32[57,768]{1,0:T(8,128)S(1)}, f32[57,768]{1,0:T(8,128)S(1)}, u32[]{:S(2)}, u32[]{:S(2)}) collective-permute-start(f32[57,768]{1,0:T(8,128)S(1)} %add_add_fusion.2), channel_id=1, source_target_pairs={{0,4},{1,5},{2,6},{3,7},{4,0},{5,1},{6,2},{7,3},{8,12},{9,13},{10,... | collective-permute-start | bytes 525320 | tf_op jit(solution)/shard_map/ppermute | solution.py:28
  124.8 18.7 %collective-permute-start.35 = (f32[57,768]{1,0:T(8,128)S(1)}, f32[57,768]{1,0:T(8,128)S(1)}, u32[]{:S(2)}, u32[]{:S(2)}) collective-permute-start(f32[57,768]{1,0:T(8,128)S(1)} %add_add_fusion.2), channel_id=1, source_target_pairs={{0,16},{1,17},{2,18},{3,19},{4,20},{5,21},{6,22},{7,23},{8,24},{9,... | collective-permute-start | bytes 525320 | tf_op jit(solution)/shard_map/ppermute | solution.py:28
  127.8 15.7 %collective-permute-start.36 = (f32[57,768]{1,0:T(8,128)S(1)}, f32[57,768]{1,0:T(8,128)S(1)}, u32[]{:S(2)}, u32[]{:S(2)}) collective-permute-start(f32[57,768]{1,0:T(8,128)S(1)} %add_add_fusion.2), channel_id=1, source_target_pairs={{0,20},{1,21},{2,22},{3,23},{4,16},{5,17},{6,18},{7,19},{8,28},{9,... | collective-permute-start | bytes 525320 | tf_op jit(solution)/shard_map/ppermute | solution.py:28
  130.7 21.7 %collective-permute-start.10 = (bf16[3,32,768]{2,1,0:T(8,128)(2,1)}, bf16[3,32,768]{2,1,0:T(8,128)(2,1)S(1)}, u32[]{:S(2)}, u32[]{:S(2)}) collective-permute-start(bf16[3,32,768]{2,1,0:T(8,128)(2,1)} %get-tuple-element.44), channel_id=1, source_target_pairs={{0,4},{1,5},{2,6},{3,7},{4,0},{5,1},{6,2},{7,3},{8,12},{9,13},{10,... | collective-permute-start | bytes 442376 | tf_op jit(solution)/shard_map/ppermute | solution.py:28
  131.2 21.8 %collective-permute-start.11 = (bf16[3,32,768]{2,1,0:T(8,128)(2,1)}, bf16[3,32,768]{2,1,0:T(8,128)(2,1)S(1)}, u32[]{:S(2)}, u32[]{:S(2)}) collective-permute-start(bf16[3,32,768]{2,1,0:T(8,128)(2,1)} %get-tuple-element.45), channel_id=1, source_target_pairs={{0,5},{1,4},{2,7},{3,6},{4,1},{5,0},{6,3},{7,2},{8,13},{9,12},{10,... | collective-permute-start | bytes 442376 | tf_op jit(solution)/shard_map/ppermute | solution.py:28
  143.5 11.9 %collective-permute-start.12 = (bf16[3,32,768]{2,1,0:T(8,128)(2,1)}, bf16[3,32,768]{2,1,0:T(8,128)(2,1)S(1)}, u32[]{:S(2)}, u32[]{:S(2)}) collective-permute-start(bf16[3,32,768]{2,1,0:T(8,128)(2,1)} %get-tuple-element.46), channel_id=1, source_target_pairs={{0,6},{1,7},{2,4},{3,5},{4,2},{5,3},{6,0},{7,1},{8,14},{9,15},{10,... | collective-permute-start | bytes 442376 | tf_op jit(solution)/shard_map/ppermute | solution.py:28
  143.5 16.6 %collective-permute-start.13 = (bf16[3,32,768]{2,1,0:T(8,128)(2,1)}, bf16[3,32,768]{2,1,0:T(8,128)(2,1)S(1)}, u32[]{:S(2)}, u32[]{:S(2)}) collective-permute-start(bf16[3,32,768]{2,1,0:T(8,128)(2,1)} %get-tuple-element.47), channel_id=1, source_target_pairs={{0,7},{1,6},{2,5},{3,4},{4,3},{5,2},{6,1},{7,0},{8,15},{9,14},{10,... | collective-permute-start | bytes 442376 | tf_op jit(solution)/shard_map/ppermute | solution.py:28
  143.5 20.2 %collective-permute-start.7 = (bf16[3,32,768]{2,1,0:T(8,128)(2,1)}, bf16[3,32,768]{2,1,0:T(8,128)(2,1)S(1)}, u32[]{:S(2)}, u32[]{:S(2)}) collective-permute-start(bf16[3,32,768]{2,1,0:T(8,128)(2,1)} %get-tuple-element.41), channel_id=1, source_target_pairs={{0,1},{1,0},{2,3},{3,2},{4,5},{5,4},{6,7},{7,6},{8,9},{9,8},{10,11... | collective-permute-start | bytes 442376 | tf_op jit(solution)/shard_map/ppermute | solution.py:28
  148.0 4.5 %copy-start.7 = (bf16[3,32,768]{2,1,0:T(8,128)(2,1)S(1)}, bf16[3,32,768]{2,1,0:T(8,128)(2,1)}, u32[]{:S(2)}) copy-start(bf16[3,32,768]{2,1,0:T(8,128)(2,1)} %get-tuple-element.42) | copy-start | bytes 442372
  148.0 5.0 %copy-start.5 = (bf16[3,32,768]{2,1,0:T(8,128)(2,1)S(1)}, bf16[3,32,768]{2,1,0:T(8,128)(2,1)}, u32[]{:S(2)}) copy-start(bf16[3,32,768]{2,1,0:T(8,128)(2,1)} %get-tuple-element.43) | copy-start | bytes 442372
  152.4 5.0 %copy-start.2 = (bf16[3,32,768]{2,1,0:T(8,128)(2,1)}, bf16[3,32,768]{2,1,0:T(8,128)(2,1)S(1)}, u32[]{:S(2)}) copy-start(bf16[3,32,768]{2,1,0:T(8,128)(2,1)S(1)} %collective-permute-done.10.refs_3_) | copy-start | bytes 442372
  152.5 11.3 %collective-permute-start.8 = (bf16[3,32,768]{2,1,0:T(8,128)(2,1)S(1)}, bf16[3,32,768]{2,1,0:T(8,128)(2,1)S(1)}, u32[]{:S(2)}, u32[]{:S(2)}) collective-permute-start(bf16[3,32,768]{2,1,0:T(8,128)(2,1)S(1)} %copy-done.7), channel_id=1, source_target_pairs={{0,2},{1,3},{2,0},{3,1},{4,6},{5,7},{6,4},{7,5},{8,10},{9,11},{10,... | collective-permute-start | bytes 442376 | tf_op jit(solution)/shard_map/ppermute | solution.py:28
  153.0 4.5 %copy-start.3 = (bf16[3,32,768]{2,1,0:T(8,128)(2,1)}, bf16[3,32,768]{2,1,0:T(8,128)(2,1)S(1)}, u32[]{:S(2)}) copy-start(bf16[3,32,768]{2,1,0:T(8,128)(2,1)S(1)} %collective-permute-done.11.refs_4_) | copy-start | bytes 442372
  153.0 10.9 %collective-permute-start.9 = (bf16[3,32,768]{2,1,0:T(8,128)(2,1)S(1)}, bf16[3,32,768]{2,1,0:T(8,128)(2,1)S(1)}, u32[]{:S(2)}, u32[]{:S(2)}) collective-permute-start(bf16[3,32,768]{2,1,0:T(8,128)(2,1)S(1)} %copy-done.5), channel_id=1, source_target_pairs={{0,3},{1,2},{2,1},{3,0},{4,7},{5,6},{6,5},{7,4},{8,11},{9,10},{10,... | collective-permute-start | bytes 442376 | tf_op jit(solution)/shard_map/ppermute | solution.py:28
  155.3 2.2 copy-start.4
  155.3 8.6 %collective-permute-start.37 = (f32[57,768]{1,0:T(8,128)S(1)}, f32[57,768]{1,0:T(8,128)S(1)}, u32[]{:S(2)}, u32[]{:S(2)}) collective-permute-start(f32[57,768]{1,0:T(8,128)S(1)} %add_add_fusion.1), channel_id=1, source_target_pairs={{0,32},{1,33},{2,34},{3,35},{4,36},{5,37},{6,38},{7,39},{8,40},{9,... | collective-permute-start | bytes 525320 | tf_op jit(solution)/shard_map/ppermute | solution.py:28
  160.1 3.8 %copy-start.6 = (bf16[3,32,768]{2,1,0:T(8,128)(2,1)}, bf16[3,32,768]{2,1,0:T(8,128)(2,1)S(1)}, u32[]{:S(2)}) copy-start(bf16[3,32,768]{2,1,0:T(8,128)(2,1)S(1)} %collective-permute-done.13.refs_6_) | copy-start | bytes 442372
  160.1 22.2 %collective-permute-start.38 = (f32[57,768]{1,0:T(8,128)S(1)}, f32[57,768]{1,0:T(8,128)S(1)}, u32[]{:S(2)}, u32[]{:S(2)}) collective-permute-start(f32[57,768]{1,0:T(8,128)S(1)} %add_add_fusion.1), channel_id=1, source_target_pairs={{0,64},{1,65},{2,66},{3,67},{4,68},{5,69},{6,70},{7,71},{8,72},{9,... | collective-permute-start | bytes 525320 | tf_op jit(solution)/shard_map/ppermute | solution.py:28
  163.7 0.7 copy-start.8
  163.7 18.6 %collective-permute-start.39 = (f32[57,768]{1,0:T(8,128)S(1)}, f32[57,768]{1,0:T(8,128)}, u32[]{:S(2)}, u32[]{:S(2)}) collective-permute-start(f32[57,768]{1,0:T(8,128)S(1)} %add_add_fusion.1), channel_id=1, source_target_pairs={{0,96},{1,97},{2,98},{3,99},{4,100},{5,101},{6,102},{7,103},{8,104... | collective-permute-start | bytes 525320 | tf_op jit(solution)/shard_map/ppermute | solution.py:28
  163.7 4.9 %copy-start.10 = (bf16[3,32,768]{2,1,0:T(8,128)(2,1)}, bf16[3,32,768]{2,1,0:T(8,128)(2,1)S(1)}, u32[]{:S(2)}) copy-start(bf16[3,32,768]{2,1,0:T(8,128)(2,1)S(1)} %collective-permute-done.8.refs_1_) | copy-start | bytes 442372
  163.7 22.5 %collective-permute-start.21 = (bf16[2,4,24,1536]{3,2,0,1:T(8,128)(2,1)}, bf16[2,4,24,1536]{3,2,0,1:T(8,128)(2,1)}, u32[]{:S(2)}, u32[]{:S(2)}) collective-permute-start(bf16[2,4,24,1536]{3,2,0,1:T(8,128)(2,1)} %bitcast.72), channel_id=1, source_target_pairs={{0,4},{1,5},{2,6},{3,7},{4,0},{5,1},{6,2},{7,3},{8,12},{9,13},{10,... | collective-permute-start | bytes 1769480 | tf_op jit(solution)/shard_map/ppermute | solution.py:28
  163.8 4.8 %copy-start.13 = (bf16[3,32,768]{2,1,0:T(8,128)(2,1)}, bf16[3,32,768]{2,1,0:T(8,128)(2,1)S(1)}, u32[]{:S(2)}) copy-start(bf16[3,32,768]{2,1,0:T(8,128)(2,1)S(1)} %collective-permute-done.9.refs_2_) | copy-start | bytes 442372
  163.8 24.7 %collective-permute-start.22 = (bf16[2,4,24,1536]{3,2,0,1:T(8,128)(2,1)}, bf16[2,4,24,1536]{3,2,0,1:T(8,128)(2,1)}, u32[]{:S(2)}, u32[]{:S(2)}) collective-permute-start(bf16[2,4,24,1536]{3,2,0,1:T(8,128)(2,1)} %bitcast.71), channel_id=1, source_target_pairs={{0,16},{1,17},{2,18},{3,19},{4,20},{5,21},{6,22},{7,23},{8,24},{9,... | collective-permute-start | bytes 1769480 | tf_op jit(solution)/shard_map/ppermute | solution.py:28
  164.4 24.2 %collective-permute-start.23 = (bf16[2,4,24,1536]{3,2,0,1:T(8,128)(2,1)}, bf16[2,4,24,1536]{3,2,0,1:T(8,128)(2,1)}, u32[]{:S(2)}, u32[]{:S(2)}) collective-permute-start(bf16[2,4,24,1536]{3,2,0,1:T(8,128)(2,1)} %bitcast.70), channel_id=1, source_target_pairs={{0,20},{1,21},{2,22},{3,23},{4,16},{5,17},{6,18},{7,19},{8,28},{9,... | collective-permute-start | bytes 1769480 | tf_op jit(solution)/shard_map/ppermute | solution.py:28
  183.5 13.4 %collective-permute-start.15 = (bf16[2,2,2,24,1536]{4,3,0,2,1:T(8,128)(2,1)S(1)}, bf16[2,2,2,24,1536]{4,3,0,2,1:T(8,128)(2,1)S(1)}, u32[]{:S(2)}, u32[]{:S(2)}) collective-permute-start(bf16[2,2,2,24,1536]{4,3,0,2,1:T(8,128)(2,1)S(1)} %bitcast.87), channel_id=1, source_target_pairs={{0,1},{1,0},{2,3},{3,2},{4,5},{5,4},{6,7},{7,6},{8,9},{9,8},{10,11... | collective-permute-start | bytes 1769480 | tf_op jit(solution)/shard_map/ppermute | solution.py:28
  184.4 20.7 %collective-permute-start.16 = (bf16[2,2,2,24,1536]{4,3,0,2,1:T(8,128)(2,1)S(1)}, bf16[2,2,2,24,1536]{4,3,0,2,1:T(8,128)(2,1)S(1)}, u32[]{:S(2)}, u32[]{:S(2)}) collective-permute-start(bf16[2,2,2,24,1536]{4,3,0,2,1:T(8,128)(2,1)S(1)} %bitcast.85), channel_id=1, source_target_pairs={{0,2},{1,3},{2,0},{3,1},{4,6},{5,7},{6,4},{7,5},{8,10},{9,11},{10,... | collective-permute-start | bytes 1769480 | tf_op jit(solution)/shard_map/ppermute | solution.py:28
  186.2 23.2 %collective-permute-start.17 = (bf16[2,2,2,24,1536]{4,3,0,2,1:T(8,128)(2,1)S(1)}, bf16[2,2,2,24,1536]{4,3,0,2,1:T(8,128)(2,1)S(1)}, u32[]{:S(2)}, u32[]{:S(2)}) collective-permute-start(bf16[2,2,2,24,1536]{4,3,0,2,1:T(8,128)(2,1)S(1)} %bitcast.86), channel_id=1, source_target_pairs={{0,3},{1,2},{2,1},{3,0},{4,7},{5,6},{6,5},{7,4},{8,11},{9,10},{10,... | collective-permute-start | bytes 1769480 | tf_op jit(solution)/shard_map/ppermute | solution.py:28
  190.3 21.9 %collective-permute-start.24 = (bf16[2,24,1536]{2,1,0:T(8,128)(2,1)S(1)}, bf16[2,24,1536]{2,1,0:T(8,128)(2,1)S(1)}, u32[]{:S(2)}, u32[]{:S(2)}) collective-permute-start(bf16[2,24,1536]{2,1,0:T(8,128)(2,1)S(1)} %get-tuple-element.62), channel_id=1, source_target_pairs={{0,1},{1,0},{2,3},{3,2},{4,5},{5,4},{6,7},{7,6},{8,9},{9,8},{10,11... | collective-permute-start | bytes 442376 | tf_op jit(solution)/shard_map/ppermute | solution.py:28
  190.4 24.2 %collective-permute-start.25 = (bf16[2,24,1536]{2,1,0:T(8,128)(2,1)S(1)}, bf16[2,24,1536]{2,1,0:T(8,128)(2,1)S(1)}, u32[]{:S(2)}, u32[]{:S(2)}) collective-permute-start(bf16[2,24,1536]{2,1,0:T(8,128)(2,1)S(1)} %get-tuple-element.64), channel_id=1, source_target_pairs={{0,2},{1,3},{2,0},{3,1},{4,6},{5,7},{6,4},{7,5},{8,10},{9,11},{10,... | collective-permute-start | bytes 442376 | tf_op jit(solution)/shard_map/ppermute | solution.py:28
  197.0 17.6 %collective-permute-start.26 = (bf16[2,24,1536]{2,1,0:T(8,128)(2,1)S(1)}, bf16[2,24,1536]{2,1,0:T(8,128)(2,1)S(1)}, u32[]{:S(2)}, u32[]{:S(2)}) collective-permute-start(bf16[2,24,1536]{2,1,0:T(8,128)(2,1)S(1)} %get-tuple-element.63), channel_id=1, source_target_pairs={{0,3},{1,2},{2,1},{3,0},{4,7},{5,6},{6,5},{7,4},{8,11},{9,10},{10,... | collective-permute-start | bytes 442376 | tf_op jit(solution)/shard_map/ppermute | solution.py:28
  209.8 5.2 %collective-permute-start.18 = (bf16[2,24,1536]{2,1,0:T(8,128)(2,1)S(1)}, bf16[2,24,1536]{2,1,0:T(8,128)(2,1)S(1)}, u32[]{:S(2)}, u32[]{:S(2)}) collective-permute-start(bf16[2,24,1536]{2,1,0:T(8,128)(2,1)S(1)} %get-tuple-element.65), channel_id=1, source_target_pairs={{0,4},{1,5},{2,6},{3,7},{4,0},{5,1},{6,2},{7,3},{8,12},{9,13},{10,... | collective-permute-start | bytes 442376 | tf_op jit(solution)/shard_map/ppermute | solution.py:28
  210.3 6.7 %collective-permute-start.19 = (bf16[2,24,1536]{2,1,0:T(8,128)(2,1)S(1)}, bf16[2,24,1536]{2,1,0:T(8,128)(2,1)S(1)}, u32[]{:S(2)}, u32[]{:S(2)}) collective-permute-start(bf16[2,24,1536]{2,1,0:T(8,128)(2,1)S(1)} %get-tuple-element.67), channel_id=1, source_target_pairs={{0,16},{1,17},{2,18},{3,19},{4,20},{5,21},{6,22},{7,23},{8,24},{9,... | collective-permute-start | bytes 442376 | tf_op jit(solution)/shard_map/ppermute | solution.py:28
  212.3 6.4 %collective-permute-start.20 = (bf16[2,24,1536]{2,1,0:T(8,128)(2,1)S(1)}, bf16[2,24,1536]{2,1,0:T(8,128)(2,1)S(1)}, u32[]{:S(2)}, u32[]{:S(2)}) collective-permute-start(bf16[2,24,1536]{2,1,0:T(8,128)(2,1)S(1)} %get-tuple-element.66), channel_id=1, source_target_pairs={{0,20},{1,21},{2,22},{3,23},{4,16},{5,17},{6,18},{7,19},{8,28},{9,... | collective-permute-start | bytes 442376 | tf_op jit(solution)/shard_map/ppermute | solution.py:28
  218.8 6.8 %collective-permute-start.27 = (bf16[24,1536]{1,0:T(8,128)(2,1)S(1)}, bf16[24,1536]{1,0:T(8,128)(2,1)S(1)}, u32[]{:S(2)}, u32[]{:S(2)}) collective-permute-start(bf16[24,1536]{1,0:T(8,128)(2,1)S(1)} %get-tuple-element.68), channel_id=1, source_target_pairs={{0,32},{1,33},{2,34},{3,35},{4,36},{5,37},{6,38},{7,39},{8,40},{9,... | collective-permute-start | bytes 221192 | tf_op jit(solution)/shard_map/ppermute | solution.py:28
  219.0 7.3 %collective-permute-start.28 = (bf16[24,1536]{1,0:T(8,128)(2,1)S(1)}, bf16[24,1536]{1,0:T(8,128)(2,1)S(1)}, u32[]{:S(2)}, u32[]{:S(2)}) collective-permute-start(bf16[24,1536]{1,0:T(8,128)(2,1)S(1)} %get-tuple-element.69), channel_id=1, source_target_pairs={{0,64},{1,65},{2,66},{3,67},{4,68},{5,69},{6,70},{7,71},{8,72},{9,... | collective-permute-start | bytes 221192 | tf_op jit(solution)/shard_map/ppermute | solution.py:28
  223.2 5.6 %collective-permute-start.29 = (bf16[24,1536]{1,0:T(8,128)(2,1)S(1)}, bf16[24,1536]{1,0:T(8,128)(2,1)S(1)}, u32[]{:S(2)}, u32[]{:S(2)}) collective-permute-start(bf16[24,1536]{1,0:T(8,128)(2,1)S(1)} %get-tuple-element.70), channel_id=1, source_target_pairs={{0,96},{1,97},{2,98},{3,99},{4,100},{5,101},{6,102},{7,103},{8,104... | collective-permute-start | bytes 221192 | tf_op jit(solution)/shard_map/ppermute | solution.py:28

commit v2 on v1

v2 whole, which is shorter than its diff:
```python
import functools

import jax
import jax.numpy as jnp
from jax import lax
from jax.experimental import pallas as pl
from jax.experimental.pallas import tpu as pltpu
from jax.sharding import PartitionSpec as P

ln_eps = 1e-06
root_half = 0.7071067811865476
inv_root_two_pi = 0.3989422804014327
f32 = jnp.float32
bf16 = jnp.bfloat16
both_axes = ("slide", "tile")
lanes = 128
side = 32
rim = 3
taps = 7
row_block = 16
own_column = 8
wide = 48
vmem_limit = 58 * 1024 * 1024


def swap(value, distance):
    pairs = [(d, d ^ distance) for d in range(lax.axis_size(both_axes))]
    return lax.ppermute(value, both_axes, pairs)


def pack_kernel(table_ref, tile_ref, out_ref, column_ref, edge_ref):
    me = lax.axis_index("tile")
    tiles = out_ref.shape[0]
    channels = tile_ref.shape[-1]
    for block in range(channels // lanes):
        here = pl.ds(block * lanes, lanes)
        for which, start, first in ((0, 0, 0), (1, 16, 13)):
            column_ref[...] = tile_ref[:, start : start + 16, here].astype(f32).reshape(16 * side, lanes)
            for c in range(rim):
                edge_ref[which, c, :, here] = column_ref[pl.ds(first + c, side, stride=16), :].astype(bf16)
    sources = (
        lambda: tile_ref[0:rim],
        lambda: tile_ref[side - rim : side],
        lambda: edge_ref[0],
        lambda: edge_ref[1],
    )
    for direction, source in enumerate((0, 1, 2, 3, 0, 0, 1, 1)):
        other = table_ref[0, me, direction]

        @pl.when(other < tiles)
        def _():
            out_ref[other] = sources[source]()


def pack_strips(table, tile):
    tiles = table.shape[1]
    channels = tile.shape[-1]
    return pl.pallas_call(
        pack_kernel,
        out_shape=jax.ShapeDtypeStruct((tiles, rim, side, channels), bf16),
        in_specs=[pl.BlockSpec(memory_space=pltpu.SMEM), pl.BlockSpec(memory_space=pltpu.VMEM)],
        out_specs=pl.BlockSpec(memory_space=pltpu.VMEM),
        scratch_shapes=[
            pltpu.VMEM((16 * side, lanes), f32),
            pltpu.VMEM((2, rim, side, channels), bf16),
        ],
        name="pack_strips",
    )(table, tile)


def assemble(table_ref, tile_ref, strip_ref, extended_ref):
    me = lax.axis_index("tile")
    tiles = strip_ref.shape[0]
    extended_ref[rim : rim + side, own_column : own_column + side, :] = tile_ref[...].astype(f32)

    def strip(direction):
        other = table_ref[0, me, direction]
        values = strip_ref[jnp.minimum(other, tiles - 1)].astype(f32)
        return jnp.where(other < tiles, values, jnp.zeros_like(values))

    last = rim + side
    right = own_column + side
    extended_ref[0:rim, own_column:right, :] = strip(0)
    extended_ref[last : last + rim, own_column:right, :] = strip(1)
    west = strip(2)
    east = strip(3)
    for c in range(rim):
        extended_ref[rim:last, own_column - rim + c, :] = west[c]
        extended_ref[rim:last, right + c, :] = east[c]
    extended_ref[0:rim, 0:8, :] = strip(4)[:, side - 8 :]
    extended_ref[0:rim, right : right + 8, :] = strip(5)[:, :8]
    extended_ref[last : last + rim, 0:8, :] = strip(6)[:, side - 8 :]
    extended_ref[last : last + rim, right : right + 8, :] = strip(7)[:, :8]


def spread_weights(weight_ref, spread_ref, flipped):
    for a in range(taps):
        rows = weight_ref[0, taps - 1 - a if flipped else a]
        for b in range(taps):
            at = taps - 1 - b if flipped else b
            spread_ref[b, a] = jnp.broadcast_to(rows[at : at + 1], (8, lanes))


def depthwise(extended_ref, spread_ref, store):
    def rows(block, carry):
        base = block * row_block
        for w in range(side // 8):
            totals = [None] * row_block
            for b in range(taps):
                start = own_column - rim + b + w * 8
                values = [extended_ref[base + r, start : start + 8, :] for r in range(row_block + taps - 1)]
                for a in range(taps):
                    factor = spread_ref[b, a]
                    for r in range(row_block):
                        term = values[r + a] * factor
                        totals[r] = term if totals[r] is None else totals[r] + term
            for r in range(row_block):
                store(base + r, w * 8, totals[r])
        return carry

    lax.fori_loop(0, side // row_block, rows, 0)


def conv_kernel(table_ref, tile_ref, *refs):
    strip_ref, weight_ref, gain_ref, shift_ref = refs[:4]
    whitened_ref, inv_ref, normed_ref, extended_ref, spread_ref, conv_ref = refs[4:]
    block = pl.program_id(0)
    blocks = whitened_ref.shape[1] // lanes
    assemble(table_ref, tile_ref, strip_ref, extended_ref)
    spread_weights(weight_ref, spread_ref, False)

    def store(row, column, value):
        conv_ref[block, row, column : column + 8, :] = value

    depthwise(extended_ref, spread_ref, store)

    @pl.when(block == blocks - 1)
    def _():
        def norm(row, carry):
            parts = [conv_ref[j, row] for j in range(blocks)]
            count = blocks * lanes
            average = jnp.sum(sum(parts), axis=-1, keepdims=True) / count
            centred = [part - average for part in parts]
            spread = jnp.sum(sum(part * part for part in centred), axis=-1, keepdims=True) / count
            inv_std = lax.rsqrt(spread + ln_eps)
            here = pl.ds(pl.multiple_of(row * side, side), side)
            inv_ref[here, :] = inv_std
            for j in range(blocks):
                at = pl.ds(j * lanes, lanes)
                whitened = centred[j] * inv_std
                whitened_ref[here, at] = whitened
                normed_ref[here, at] = (whitened * gain_ref[:, at] + shift_ref[:, at]).astype(bf16)
            return carry

        lax.fori_loop(0, side, norm, 0)


def strip_spec(strips, first=0):
    return pl.BlockSpec((*strips.shape[:3], lanes), lambda i: (0, 0, 0, first + i))


def conv_norm(table, tile, strips, weight, gain, shift):
    channels = tile.shape[-1]
    pixels = side * side
    blocks = channels // lanes
    whole = lambda i: (0, 0)
    return pl.pallas_call(
        conv_kernel,
        grid=(blocks,),
        out_shape=[
            jax.ShapeDtypeStruct((pixels, channels), f32),
            jax.ShapeDtypeStruct((pixels, 1), f32),
            jax.ShapeDtypeStruct((pixels, channels), bf16),
        ],
        in_specs=[
            pl.BlockSpec(memory_space=pltpu.SMEM),
            pl.BlockSpec((side, side, lanes), lambda i: (0, 0, i)),
            strip_spec(strips),
            pl.BlockSpec((1, taps, taps, lanes), lambda i: (0, 0, 0, i)),
            pl.BlockSpec((1, channels), whole),
            pl.BlockSpec((1, channels), whole),
        ],
        out_specs=[
            pl.BlockSpec((pixels, channels), whole),
            pl.BlockSpec((pixels, 1), whole),
            pl.BlockSpec((pixels, channels), whole),
        ],
        scratch_shapes=[
            pltpu.VMEM((side + 2 * rim, wide, lanes), f32),
            pltpu.VMEM((taps, taps, 8, lanes), f32),
            pltpu.VMEM((blocks, side, side, lanes), f32),
        ],
        compiler_params=pltpu.CompilerParams(vmem_limit_bytes=vmem_limit),
        cost_estimate=pl.CostEstimate(flops=14_000_000_000, bytes_accessed=10_000_000, transcendentals=0),
        name="conv_norm",
    )(table, tile, strips, weight, gain, shift)


dot = functools.partial(lax.dot_general, preferred_element_type=f32)
by_rows = (((1,), (1,)), ((), ()))
plain = (((1,), (0,)), ((), ()))
by_pixels = (((0,), (0,)), ((), ()))


def join_blocks(up_first_ref, up_second_ref, down_first_ref, down_second_ref, up_ref, down_ref):
    block = up_first_ref.shape[0]
    up_ref[:block] = up_first_ref[...]
    up_ref[block:] = up_second_ref[...]
    down_ref[:, :block] = down_first_ref[...]
    down_ref[:, block:] = down_second_ref[...]


def hidden_kernel(
    skip_ref, normed_ref, grad_ref, up_first_ref, up_second_ref, up_bias_ref, down_first_ref, down_second_ref,
    scale_ref,
    act_ref, pre_grad_ref, mine_ref, theirs_ref, bias_ref,
    branch_grad_ref, pair_ref, up_ref, down_ref,
):
    step = pl.program_id(0)
    pixels, channels = normed_ref.shape
    keep = (1 - skip_ref[0, 0]).astype(f32)
    tile_rows = 256
    join_blocks(up_first_ref, up_second_ref, down_first_ref, down_second_ref, up_ref, down_ref)

    @pl.when(step == 0)
    def _():
        branch_grad_ref[...] = (keep * scale_ref[...] * grad_ref[...].astype(f32)).astype(bf16)

    def rows_of(m):
        return pl.ds(m * tile_rows, tile_rows)

    def lift(m):
        return dot(normed_ref[rows_of(m), :], up_ref[...], by_rows) + up_bias_ref[0]

    bias_sum = jnp.zeros((1, up_ref.shape[0]), f32)
    count = pixels // tile_rows
    following = lift(0)
    for m in range(count):
        rows = rows_of(m)
        pre = following
        act_grad = dot(branch_grad_ref[rows, :], down_ref[...], plain)
        if m + 1 < count:
            following = lift(m + 1)
        cdf = 0.5 * (1.0 + lax.erf(pre * root_half))
        slope = cdf + pre * inv_root_two_pi * jnp.exp(-0.5 * pre * pre)
        act_ref[rows, :] = (pre * cdf).astype(bf16)
        pre_grad = (act_grad * slope).astype(bf16)
        pre_grad_ref[rows, :] = pre_grad
        bias_sum = bias_sum + jnp.sum(pre_grad.astype(f32), axis=0, keepdims=True)
    bias_ref[0] = bias_sum
    quarter = pair_ref.shape[1]
    left = dot(pre_grad_ref[...], normed_ref[...], by_pixels).astype(bf16)
    for q in range(4):
        pair_ref[q, :, :channels] = left[q * quarter : (q + 1) * quarter]
    right = dot(act_ref[...], branch_grad_ref[...], by_pixels).astype(bf16)
    for q in range(4):
        pair_ref[q, :, channels:] = right[q * quarter : (q + 1) * quarter]
    core = lax.axis_index("slide") % 2
    for high in range(2):
        mine_ref[0, high] = pair_ref[2 * high + core]
        theirs_ref[0, high] = pair_ref[2 * high + 1 - core]


once = pl.Buffered(1)
anywhere = pl.BlockSpec(memory_space=pl.ANY)
in_scalars = pl.BlockSpec(memory_space=pltpu.SMEM)


def full(*shape):
    return pl.BlockSpec(shape, lambda i: (0, 0), pipeline_mode=once)


def hidden_half(half, skip, normed, grad, up, up_bias, down, scale):
    pixels, channels = normed.shape
    hidden = up.shape[0]
    steps = 2
    chunk = hidden // 4
    quarter = chunk // 4
    block = chunk // 2
    part = jax.ShapeDtypeStruct((steps, 2, quarter, 2 * channels), bf16)
    part_spec = pl.BlockSpec((1, 2, quarter, 2 * channels), lambda i: (i, 0, 0, 0))
    wide_shape = jax.ShapeDtypeStruct((pixels, steps * chunk), bf16)
    wide_spec = pl.BlockSpec((pixels, chunk), lambda i: (0, i))
    return pl.pallas_call(
        hidden_kernel,
        grid=(steps,),
        out_shape=[wide_shape, wide_shape, part, part, jax.ShapeDtypeStruct((steps, 1, chunk), f32)],
        in_specs=[
            in_scalars,
            full(pixels, channels),
            full(pixels, channels),
            pl.BlockSpec((block, channels), lambda i: (4 * i + half, 0)),
            pl.BlockSpec((block, channels), lambda i: (4 * i + 2 + half, 0)),
            pl.BlockSpec((1, 1, chunk), lambda i: (2 * half + i, 0, 0)),
            pl.BlockSpec((channels, block), lambda i: (0, 4 * i + half)),
            pl.BlockSpec((channels, block), lambda i: (0, 4 * i + 2 + half)),
            full(1, channels),
        ],
        out_specs=[wide_spec, wide_spec, part_spec, part_spec, pl.BlockSpec((1, 1, chunk), lambda i: (i, 0, 0))],
        scratch_shapes=[
            pltpu.VMEM((pixels, channels), bf16),
            pltpu.VMEM((4, quarter, 2 * channels), bf16),
            pltpu.VMEM((chunk, channels), bf16),
            pltpu.VMEM((channels, chunk), bf16),
        ],
        compiler_params=pltpu.CompilerParams(vmem_limit_bytes=vmem_limit),
        cost_estimate=pl.CostEstimate(flops=14_000_000_000, bytes_accessed=20_000_000, transcendentals=0),
        name="hidden_half",
    )(skip, normed, grad, up, up, up_bias, down, down, scale)


def join_kernel(
    skip_ref, act_low_ref, act_high_ref, pre_low_ref, pre_high_ref,
    up_first_ref, up_second_ref, down_first_ref, down_second_ref, inv_ref, down_bias_ref, scale_ref, gain_ref, whitened_hbm_ref, tile_hbm_ref, grad_hbm_ref,
    out_ref, conv_grad_ref, channel_ref,
    branch_ref, normed_grad_ref, whitened_ref, tile_ref, grad_ref, arrived, up_ref, down_ref,
):
    step = pl.program_id(0)
    steps = pl.num_programs(0)
    pixels, channels = out_ref.shape
    pairs = ((whitened_hbm_ref, whitened_ref), (tile_hbm_ref, tile_ref), (grad_hbm_ref, grad_ref))
    copies = [pltpu.make_async_copy(*pair, arrived.at[at]) for at, pair in enumerate(pairs)]
    join_blocks(up_first_ref, up_second_ref, down_first_ref, down_second_ref, up_ref, down_ref)

    @pl.when(step == 0)
    def _():
        for copy in copies:
            copy.start()
        branch_ref[...] = dot(act_low_ref[...], down_ref[...], by_rows)
        normed_grad_ref[...] = dot(pre_low_ref[...], up_ref[...], plain)

    @pl.when(step == 1)
    def _():
        branch_ref[...] += dot(act_low_ref[...], down_ref[...], by_rows)
        normed_grad_ref[...] += dot(pre_low_ref[...], up_ref[...], plain)

    @pl.when(step >= 2)
    def _():
        branch_ref[...] += dot(act_high_ref[...], down_ref[...], by_rows)
        normed_grad_ref[...] += dot(pre_high_ref[...], up_ref[...], plain)

    @pl.when(step == steps - 1)
    def _():
        rows_each = 64
        keep = (1 - skip_ref[0, 0]).astype(f32)
        factor = keep * scale_ref[...]
        for copy in copies:
            copy.wait()

        def finish(m, sums):
            rows = pl.ds(pl.multiple_of(m * rows_each, rows_each), rows_each)
            grad = grad_ref[rows, :].astype(f32)
            branch = branch_ref[rows, :] + down_bias_ref[...]
            out_ref[rows, :] = (tile_ref[rows, :].astype(f32) + factor * branch).astype(bf16)
            whitened = whitened_ref[rows, :]
            normed_grad = normed_grad_ref[rows, :]
            scaled = normed_grad * gain_ref[...]
            product = normed_grad * whitened
            mean_one = jnp.sum(scaled, axis=-1, keepdims=True) / channels
            mean_two = jnp.sum(scaled * whitened, axis=-1, keepdims=True) / channels
            conv_grad = inv_ref[rows, :] * (scaled - mean_one - whitened * mean_two)
            conv_grad_ref[rows, :] = conv_grad.astype(bf16)
            branch_grad = (factor * grad).astype(bf16).astype(f32)
            terms = (product, normed_grad, branch_grad, grad * keep * branch)
            return tuple(
                total + jnp.sum(term.reshape(rows_each // 8, 8, channels), axis=0)
                for total, term in zip(sums, terms)
            )

        zero = jnp.zeros((8, channels), f32)
        sums = lax.fori_loop(0, pixels // rows_each, finish, (zero,) * 4)
        for at in range(4):
            channel_ref[at : at + 1, :] = jnp.sum(sums[at], axis=0, keepdims=True)


def join(skip, acts, pre_grads, up, down, inv_std, down_bias, scale, gain, whitened, tile, grad):
    pixels, channels = grad.shape
    chunk = acts[0].shape[1] // 2
    block = chunk // 2
    at_first = lambda i: 4 * (i % 2) + i // 2
    low_spec = pl.BlockSpec((pixels, chunk), lambda i: (0, jnp.minimum(i, 1)))
    high_spec = pl.BlockSpec((pixels, chunk), lambda i: (0, jnp.maximum(i - 2, 0)))
    pixel = jax.ShapeDtypeStruct((pixels, channels), bf16)
    return pl.pallas_call(
        join_kernel,
        grid=(4,),
        out_shape=[pixel, pixel, jax.ShapeDtypeStruct((4, channels), f32)],
        in_specs=[
            in_scalars,
            low_spec,
            high_spec,
            low_spec,
            high_spec,
            pl.BlockSpec((block, channels), lambda i: (at_first(i), 0)),
            pl.BlockSpec((block, channels), lambda i: (at_first(i) + 2, 0)),
            pl.BlockSpec((channels, block), lambda i: (0, at_first(i))),
            pl.BlockSpec((channels, block), lambda i: (0, at_first(i) + 2)),
            full(pixels, 1),
            full(1, channels),
            full(1, channels),
            full(1, channels),
            anywhere,
            anywhere,
            anywhere,
        ],
        out_specs=[full(pixels, channels), full(pixels, channels), full(4, channels)],
        scratch_shapes=[
            pltpu.VMEM((pixels, channels), f32),
            pltpu.VMEM((pixels, channels), f32),
            pltpu.VMEM((pixels, channels), f32),
            pltpu.VMEM((pixels, channels), bf16),
            pltpu.VMEM((pixels, channels), bf16),
            pltpu.SemaphoreType.DMA((3,)),
            pltpu.VMEM((chunk, channels), bf16),
            pltpu.VMEM((channels, chunk), bf16),
        ],
        compiler_params=pltpu.CompilerParams(vmem_limit_bytes=vmem_limit),
        cost_estimate=pl.CostEstimate(flops=14_000_000_000, bytes_accessed=30_000_000, transcendentals=0),
        name="join_halves",
    )(skip, *acts, *pre_grads, up, up, down, down, inv_std, down_bias, scale, gain, whitened, tile, grad)


def kernel_grad_kernel(table_ref, tile_ref, *refs):
    strip_ref, grad_ref, out_ref, extended_ref, wide_ref, total_ref = refs
    assemble(table_ref, tile_ref, strip_ref, extended_ref)
    wide_ref[...] = grad_ref[...].astype(f32)
    total_ref[...] = jnp.zeros_like(total_ref)

    def rows(block, carry):
        base = block * row_block
        for w in range(side // 8):
            grads = [wide_ref[base + r, w * 8 : w * 8 + 8, :] for r in range(row_block)]
            for b in range(taps):
                start = own_column - rim + b + w * 8
                values = [extended_ref[base + r, start : start + 8, :] for r in range(row_block + taps - 1)]
                for a in range(taps):
                    terms = [values[r + a] * grads[r] for r in range(row_block)]
                    while len(terms) > 1:
                        terms = [terms[i] + terms[i + 1] for i in range(0, len(terms), 2)]
                    total_ref[a, b] += terms[0]
        return carry

    lax.fori_loop(0, side // row_block, rows, 0)
    for a in range(taps):
        out_ref[a] = jnp.sum(total_ref[a], axis=1)


def kernel_grad(table, tile, strips, conv_grad):
    channels = tile.shape[-1]
    block_spec = pl.BlockSpec((side, side, lanes), lambda i: (0, 0, i))
    return pl.pallas_call(
        kernel_grad_kernel,
        grid=(channels // lanes,),
        out_shape=jax.ShapeDtypeStruct((taps, taps, channels), f32),
        in_specs=[pl.BlockSpec(memory_space=pltpu.SMEM), block_spec, strip_spec(strips), block_spec],
        out_specs=pl.BlockSpec((taps, taps, lanes), lambda i: (0, 0, i)),
        scratch_shapes=[
            pltpu.VMEM((side + 2 * rim, wide, lanes), f32),
            pltpu.VMEM((side, side, lanes), f32),
            pltpu.VMEM((taps, taps, 8, lanes), f32),
        ],
        cost_estimate=pl.CostEstimate(flops=14_000_000_000, bytes_accessed=5_000_000, transcendentals=0),
        name="kernel_grad",
    )(table, tile, strips, conv_grad)


def back_kernel(table_ref, tile_ref, *refs):
    strip_ref, weight_ref, grad_ref = refs[:3]
    out_ref, extended_ref, spread_ref, total_ref = refs[-4:]
    assemble(table_ref, tile_ref, strip_ref, extended_ref)
    spread_weights(weight_ref, spread_ref, True)

    def store(row, column, value):
        total_ref[row, column : column + 8, :] = value

    depthwise(extended_ref, spread_ref, store)
    out_ref[...] = (grad_ref[...].astype(f32) + total_ref[...]).astype(bf16)


def back_conv(table, tile, strips, weight, grad, part, parts, done=None):
    channels = tile.shape[-1]
    steps = channels // lanes // parts
    first = part * steps
    block_spec = pl.BlockSpec((side, side, lanes), lambda i: (0, 0, first + i))
    earlier = [] if done is None else [done]
    return pl.pallas_call(
        back_kernel,
        grid=(steps,),
        out_shape=jax.ShapeDtypeStruct(tile.shape, bf16),
        in_specs=[
            pl.BlockSpec(memory_space=pltpu.SMEM),
            block_spec,
            strip_spec(strips, first),
            pl.BlockSpec((1, taps, taps, lanes), lambda i: (0, 0, 0, first + i)),
            block_spec,
            *[pl.BlockSpec(memory_space=pl.ANY) for _ in earlier],
        ],
        out_specs=block_spec,
        scratch_shapes=[
            pltpu.VMEM((side + 2 * rim, wide, lanes), f32),
            pltpu.VMEM((taps, taps, 8, lanes), f32),
            pltpu.VMEM((side, side, lanes), f32),
        ],
        input_output_aliases={5: 0} if earlier else {},
        cost_estimate=pl.CostEstimate(
            flops=14_000_000_000 // parts, bytes_accessed=5_000_000 // parts, transcendentals=0
        ),
        name="back_conv",
    )(table, tile, strips, weight, grad, *earlier)


def pick(value, positions):
    for axis, index in positions:
        value = lax.dynamic_index_in_dim(value, index, axis, keepdims=False)
    return value


def fold(parts, dtype):
    wide_parts = [part.astype(f32) for part in parts]
    while len(wide_parts) > 1:
        wide_parts = [wide_parts[i] + wide_parts[i + 1] for i in range(0, len(wide_parts), 2)]
    return wide_parts[0].astype(dtype)


def reduce_axis(take, distance, dtype):
    kept = take(0)
    arrived = [swap(take(k), k * distance) for k in (1, 2, 3)]
    return fold([kept, *arrived], dtype)


def place():
    slide, tile = lax.axis_index("slide"), lax.axis_index("tile")
    return slide // 4, (slide // 2) % 2, tile // 4, tile % 4


def x_parts(value):
    x = place()[3]
    return [pick(value, [(value.ndim - 3, x ^ k)]) for k in range(4)]


def y_parts(value):
    _, y_hi, y_lo, _ = place()
    return [pick(value, [(1, y_lo ^ (k % 2)), (0, y_hi ^ (k // 2))]) for k in range(4)]


def z_parts(value):
    z = place()[0]
    return [pick(value, [(0, z ^ k)]) for k in range(4)]


x_distances = (1, 2, 3)
y_distances = (4, 16, 20)
z_distances = (32, 64, 96)


def gather_sum(parts, distances, dtype):
    arrived = [swap(part, d) for part, d in zip(parts[1:], distances)]
    return fold([parts[0], *arrived], dtype)


def after(value, *others):
    return lax.optimization_barrier((value, *others))[0]


def trade(value, distance, ready):
    arrived = swap(value, distance)
    return after(value, ready) + arrived


def ride(parts, small):
    width = parts[0].shape[-1]
    extra = small.astype(bf16).reshape(-1, width)
    sent = [jnp.concatenate([part.reshape(-1, width), extra], 0) for part in parts[1:]]
    return sent, lax.reduce_precision(small, 8, 7)


def land(sent, small, parts, distances, dtype, ready):
    arrived = [swap(value, d) for value, d in zip(sent, distances)]
    size = parts[0].size // parts[0].shape[-1]
    mine, small = lax.optimization_barrier((parts[0], small, ready))[:2]
    total = fold([mine, *[value[:size].reshape(mine.shape) for value in arrived]], dtype)
    return total, fold([small, *[value[size:].reshape(small.shape) for value in arrived]], f32)


def on_device(
    features,
    cotangent,
    neighbours,
    skip_flags,
    dw_weight,
    ln_gain,
    ln_bias,
    up_weight,
    up_bias,
    down_weight,
    down_bias,
    layer_scale,
):
    channels = features.shape[-1]
    hidden = up_weight.shape[1]
    tile = features[0, 0]
    grad = cotangent[0, 0]
    flat = (side * side, channels)
    strips = lax.all_to_all(pack_strips(neighbours, tile), "tile", 0, 0)
    whitened, inv_std, normed = conv_norm(neighbours, tile, strips, dw_weight, ln_gain, ln_bias)
    flat_grad = grad.reshape(flat)
    bias_order = jnp.swapaxes(up_bias.reshape(4, 2, -1), 0, 1).reshape(4, 1, -1)
    mlp_in = (flat_grad, up_weight[0], bias_order, down_weight[0], layer_scale)
    act_low, pre_low, mine_low, theirs_low, bias_low = hidden_half(0, skip_flags, normed, *mlp_in)
    received_low = swap(theirs_low, 8)
    act_high, pre_high, mine_high, theirs_high, bias_high = hidden_half(1, skip_flags, after(normed, theirs_low), *mlp_in)
    rows = mine_low.shape[2] // 8
    width = mine_low.shape[3]
    grid = (4, 2, 4, rows, width)
    received_high = swap(theirs_high, 8)
    low_x = x_parts(fold([after(mine_low, act_high), received_low], bf16).reshape(grid))
    out, conv_grad, channel_sums = join(
        skip_flags, (after(act_low, *low_x), act_high), (pre_low, pre_high), up_weight[0], down_weight[0],
        inv_std, down_bias, layer_scale, ln_gain, whitened, tile.reshape(flat), flat_grad,
    )
    conv_grad = conv_grad.reshape(tile.shape)
    packed = pack_strips(neighbours, conv_grad)
    low_x[0] = after(low_x[0], packed)
    mine_high = after(mine_high, packed)
    grad_strips = lax.all_to_all(packed, "tile", 0, 0)
    low_z = z_parts(gather_sum(low_x, x_distances, bf16))
    high_z = z_parts(fold([mine_high, received_high], bf16).reshape(grid))
    sent_z = [
        jnp.concatenate([low.reshape(-1, width), high.reshape(-1, width)], 0) for low, high in zip(low_z, high_z)
    ]
    kernel_sums = kernel_grad(neighbours, tile, strips, after(conv_grad, *sent_z))
    small = jnp.concatenate(
        [
            kernel_sums.reshape(taps * taps, channels),
            channel_sums,
            jnp.stack([bias_low.reshape(4, -1), bias_high.reshape(4, -1)], 1).reshape(-1, channels),
        ],
        0,
    )
    count = small.shape[0]
    small = jnp.pad(small, ((0, -count % 16), (0, 0)))
    back = functools.partial(back_conv, neighbours)
    grad_strips = after(grad_strips, small)
    input_grad = back(conv_grad, grad_strips, dw_weight, grad, 0, 3)
    small = trade(small, 8, input_grad)
    input_grad = back(after(conv_grad, small), grad_strips, dw_weight, grad, 1, 3, input_grad)
    small = trade(small, 32, input_grad)
    sent_z[0] = after(sent_z[0], input_grad)
    got_z = gather_sum(sent_z, z_distances, bf16)
    done_low = got_z[: 2 * rows]
    high_x = x_parts(got_z[2 * rows :].reshape(2, 4, rows, width))
    wide_x, small = ride(high_x, small)
    input_grad = back(after(conv_grad, *wide_x), grad_strips, dw_weight, grad, 2, 3, input_grad)
    done_high, small = land(wide_x, small, high_x, x_distances, bf16, input_grad)
    last = y_parts(jnp.concatenate([done_low, done_high.reshape(-1, width)], 0).reshape(2, 2, rows, width))
    wide_y, small = ride(last, small)
    weight_rows, small = land(wide_y, small, last, y_distances, f32, input_grad)
    small = trade(small, 96, small)[:count]
    split = taps * taps
    return (
        out.reshape(features.shape),
        input_grad[None, None],
        weight_rows[None],
        small[:split].reshape(1, taps, taps, channels),
        small[split : split + 4][None],
        small[split + 4 :].reshape(1, hidden),
    )


def solution(mesh):
    return jax.shard_map(
        on_device,
        mesh=mesh,
        in_specs=(
            P("slide", "tile", None, None, None),
            P("slide", "tile", None, None, None),
            P("slide", None, None),
            P(None, "slide"),
            P(),
            P(),
            P(),
            P(),
            P(),
            P(),
            P(),
            P(),
        ),
        out_specs=(
            P("slide", "tile", None, None, None),
            P("slide", "tile", None, None, None),
            P(None, ("slide", "tile"), None),
            P(),
            P(),
            P(),
        ),
        check_vma=False,
    )
```

time: 230 us -> 202 us (0.88)
  starting transfers between devices: 60.6 us -> 32.4 us
  waiting for transfers between devices: 50.7 us -> 34 us
  Pallas kernels: 97.9 us -> 111 us
  other arithmetic: 9.18 us -> 13.2 us
    ppermute x40 -> x17, starting transfers between devices: 60.6 us -> 22.5 us  [swap(): return lax.ppermute(value, both_axes, pairs)]
    ppermute x40 -> x17, waiting for transfers between devices: 50.7 us -> 20.1 us  [swap(): return lax.ppermute(value, both_axes, pairs)]
    all_to_all x0 -> x2, waiting for transfers between devices: none -> 13.9 us  [the longest x1 13.9 us: on_device(): strips = lax.all_to_all(pack_strips(neighbours, tile), 'tile', 0, 0)]
    pallas_call x4 -> x8, Pallas kernels: 63 us -> 76.3 us  [the longest x2 33 us: hidden_half(): pl.pallas_call(hidden_kernel, grid=(steps,), out_shape=[wide_shape, wide_...]
    all_to_all x0 -> x2, starting transfers between devices: none -> 9.92 us  [the longest x1 5.52 us: on_device(): strips = lax.all_to_all(pack_strips(neighbours, tile), 'tile', 0, 0)]
    concatenate x0 -> x7, other arithmetic: none -> 2.94 us  [the longest x4 2.83 us: on_device(): jnp.concatenate([low.reshape(-1, width), high.reshape(-1, width)], 0)]
    dynamic_slice x8 -> x2, local copies, waits for them, and re-layouts: 3.12 us -> 0.25 us  [pick(): value = lax.dynamic_index_in_dim(value, index, axis, keepdims=False)]
  transfers between devices with their start and end apart: 40 -> 19, of which waited for: 16 -> 8; matrix products, arithmetic and copies ran while one was open for 7% -> 8% of each run, Pallas kernels for 13% -> 35%
where the time goes in v2:
time: 202 us; the launch traced here: 200 us
  Pallas kernels  111 us (55%)
  waiting for transfers between devices  34 us (17%)
  starting transfers between devices  32.4 us (16%)
  other arithmetic  13.2 us (7%)
  local copies, waits for them, and re-layouts  8.35 us (4%)
    pallas_call x2, Pallas kernels, hidden_half(): pl.pallas_call(hidden_kernel, grid=(steps,), out_shape=[wide_shape, wide_...  33 us
    ppermute x17, starting transfers between devices, swap(): return lax.ppermute(value, both_axes, pairs)  22.5 us
    pallas_call x1, Pallas kernels, conv_norm(): pl.pallas_call(conv_kernel, grid=(blocks,), out_shape=[jax.ShapeDtypeStru...  20.9 us
    pallas_call x1, Pallas kernels, join(): pl.pallas_call(join_kernel, grid=(4,), out_shape=[pixel, pixel, jax.Shape...  20.5 us
    ppermute x17, waiting for transfers between devices, swap(): return lax.ppermute(value, both_axes, pairs)  20.1 us
    pallas_call x3, Pallas kernels, back_conv(): pl.pallas_call(back_kernel, grid=(steps,), out_shape=jax.ShapeDtypeStruct...  17.1 us
    all_to_all x1, waiting for transfers between devices, on_device(): strips = lax.all_to_all(pack_strips(neighbours, tile), 'tile', 0, 0)  13.9 us
    pallas_call x1, Pallas kernels, kernel_grad(): pl.pallas_call(kernel_grad_kernel, grid=(channels // lanes,), out_shape=j...  13.6 us
  transfers between devices with their start and end apart: 19, of which 8 were waited for; matrix products, arithmetic and copies ran while one was open for 8% of the time, Pallas kernels for 35%

profile of v2, /device:TPU:0, one launch (start us, length us, event | category | flops | bytes accessed | tf_op | source)
XLA Modules:
  0.0 200.5 jit_solution(11919308646494968648)
XLA Ops:
  0.6 2.8 %pack_strips.2 = bf16[8,3,32,768]{3,2,1,0:T(8,128)(2,1)} custom-call(s32[1,8,8]{2,1,0:T(8,128)} %table_ref.13, bf16[32,32,768]{2,1,0:T(8,128)(2,1)} %bitcast.65), custom_call_target="tpu_custom_call" | custom-call | tf_op jit(solution)/shard_map/pack_strips/pallas_call | solution.py:58
  3.5 5.5 %all-to-all-start = ((bf16[8,3,32,768]{3,2,1,0:T(8,128)(2,1)}), bf16[8,3,32,768]{3,2,1,0:T(8,128)(2,1)S(1)}, u32[]{:S(2)}, u32[]{:S(2)}) async-start(bf16[8,3,32,768]{3,2,1,0:T(8,128)(2,1)} %pack_strips.2), calls=%async_computation | async-start | bytes 2359296 | tf_op jit(solution)/shard_map/all_to_all | solution.py:604
  9.6 0.7 copy.25.refs_1_
  10.3 0.5 broadcast.20
  10.8 0.7 reduce.5
  11.6 0.6 reshape.134.up_bias_ref
  12.2 13.9 %all-to-all-done.refs_0_ = bf16[8,3,32,768]{3,2,1,0:T(8,128)(2,1)S(1)} async-done(((bf16[8,3,32,768]{3,2,1,0:T(8,128)(2,1)}), bf16[8,3,32,768]{3,2,1,0:T(8,128)(2,1)S(1)}, u32[]{:S(2)}, u32[]{:S(2)}) %all-to-all-start) | async-done | bytes 1179680 | tf_op jit(solution)/shard_map/all_to_all | solution.py:604
  26.1 1.0 copy-done.3
  27.1 20.9 %conv_norm.1 = (f32[1024,768]{1,0:T(8,128)}, f32[1024,1]{1,0:T(8,128)}, bf16[1024,768]{1,0:T(8,128)(2,1)}) custom-call(s32[1,8,8]{2,1,0:T(8,128)} %table_ref.13, bf16[32,32,768]{2,1,0:T(8,128)(2,1)} %bitcast.66, bf16[8,3,32,768]{3,2,1,0:T(8,128)(2,1)} %copy-done.3, f32[1,7,7,768]{3,2,1,0:T(8,128)} %copy.25.refs_1_, f32[1,768]{1,0:T(1,128)} %gain_ref.1, ...), custom_call_target="tpu_custom_call" | custom-call | flops 14000000000 | bytes 10000000 | tf_op jit(solution)/shard_map/conv_norm/pallas_call | solution.py:167
  48.0 16.4 %hidden_half.2 = (bf16[1024,1536]{1,0:T(8,128)(2,1)}, bf16[1024,1536]{1,0:T(8,128)(2,1)}, bf16[2,2,192,1536]{3,2,1,0:T(8,128)(2,1)}, bf16[2,2,192,1536]{3,2,1,0:T(8,128)(2,1)}, f32[2,1,768]{2,1,0:T(1,128)}) custom-call(s32[1,1]{1,0:T(1,128)S(6)} %copy.35.skip_ref, bf16[1024,768]{1,0:T(8,128)(2,1)} %get-tuple-element.43.normed_ref, ...), custom_call_target="tpu_custom_call" | custom-call | flops 14000000000 | bytes 20000000 | tf_op jit(solution)/shard_map/hidden_half/pallas_call | solution.py:284
  64.4 0.3 collective-permute-start
  64.8 0.0 copy-start.7
  64.8 16.5 %hidden_half.3 = (bf16[1024,1536]{1,0:T(8,128)(2,1)}, bf16[1024,1536]{1,0:T(8,128)(2,1)}, bf16[2,2,192,1536]{3,2,1,0:T(8,128)(2,1)}, bf16[2,2,192,1536]{3,2,1,0:T(8,128)(2,1)}, f32[2,1,768]{2,1,0:T(1,128)}) custom-call(s32[1,1]{1,0:T(1,128)S(6)} %copy.35.skip_ref, bf16[1024,768]{1,0:T(8,128)(2,1)} %get-tuple-element.43.normed_ref, ...), custom_call_target="tpu_custom_call" | custom-call | flops 14000000000 | bytes 20000000 | tf_op jit(solution)/shard_map/hidden_half/pallas_call | solution.py:284
  81.4 0.7 reduce.2
  82.2 0.4 collective-permute-start.4
  82.7 2.3 %add_convert_fusion.1 = bf16[2,2,192,1536]{3,2,1,0:T(8,128)(2,1)S(1)} fusion(bf16[2,2,192,1536]{3,2,1,0:T(8,128)(2,1)} %collective-permute-done, bf16[2,2,192,1536]{3,2,1,0:T(8,128)(2,1)S(1)} %copy-done.1), kind=kLoop, calls=%fused_computation.1 | loop fusion | flops 4718592 | bytes 7077888 | tf_op jit(solution)/shard_map/convert_element_type | solution.py:522
  84.9 1.2 dynamic-slice_bitcast_fusion
  86.1 0.6 collective-permute-start.3
  86.7 2.4 %collective-permute-start.2 = (bf16[4,2,24,1536]{3,2,1,0:T(8,128)(2,1)}, bf16[4,2,24,1536]{3,2,1,0:T(8,128)(2,1)}, u32[]{:S(2)}, u32[]{:S(2)}) collective-permute-start(bf16[4,2,24,1536]{3,2,1,0:T(8,128)(2,1)} %get-tuple-element.77), channel_id=1, source_target_pairs={{0,2},{1,3},{2,0},{3,1},{4,6},{5,7},{6,4},{7,5},{8,10},{9,11},{10,... | collective-permute-start | bytes 1769480 | tf_op jit(solution)/shard_map/ppermute | solution.py:28
  89.1 1.2 collective-permute-start.1
  90.2 20.5 %join_halves.1 = (bf16[1024,768]{1,0:T(8,128)(2,1)}, bf16[1024,768]{1,0:T(8,128)(2,1)}, f32[4,768]{1,0:T(4,128)}) custom-call(s32[1,1]{1,0:T(1,128)S(6)} %copy.35.skip_ref, bf16[1024,1536]{1,0:T(8,128)(2,1)} %get-tuple-element.46.act_low_ref, bf16[1024,1536]{1,0:T(8,128)(2,1)} %get-tuple-element.44.act_high_ref, ...), custom_call_target="tpu_custom_call" | custom-call | flops 14000000000 | bytes 30000000 | tf_op jit(solution)/shard_map/join_halves/pallas_call | solution.py:384
  110.8 2.8 %pack_strips.3 = bf16[8,3,32,768]{3,2,1,0:T(8,128)(2,1)} custom-call(s32[1,8,8]{2,1,0:T(8,128)} %table_ref.13, bf16[32,32,768]{2,1,0:T(8,128)(2,1)} %bitcast.69), custom_call_target="tpu_custom_call" | custom-call | tf_op jit(solution)/shard_map/pack_strips/pallas_call | solution.py:58
  113.6 4.4 %all-to-all-start.1 = ((bf16[8,3,32,768]{3,2,1,0:T(8,128)(2,1)}), bf16[8,3,32,768]{3,2,1,0:T(8,128)(2,1)}, u32[]{:S(2)}, u32[]{:S(2)}) async-start(bf16[8,3,32,768]{3,2,1,0:T(8,128)(2,1)} %pack_strips.3), calls=%async_computation.1 | async-start | bytes 2359296 | tf_op jit(solution)/shard_map/all_to_all | solution.py:625
  118.0 2.3 %add_convert_fusion = bf16[2,2,192,1536]{3,2,1,0:T(8,128)(2,1)S(1)} fusion(bf16[2,2,192,1536]{3,2,1,0:T(8,128)(2,1)} %collective-permute-done.4, bf16[2,2,192,1536]{3,2,1,0:T(8,128)(2,1)S(1)} %copy-done.2), kind=kLoop, calls=%fused_computation | loop fusion | flops 4718592 | bytes 7077888 | tf_op jit(solution)/shard_map/convert_element_type | solution.py:522
  120.3 0.2 constant_dynamic-slice_fusion.3
  120.5 0.0 collective-permute-done.3
  120.5 1.7 add_convert_fusion.3
  122.2 0.1 constant_dynamic-slice_fusion.4
  122.3 0.9 pad_maximum_fusion.3
  123.2 4.0 %collective-permute-start.8 = (bf16[240,1536]{1,0:T(8,128)(2,1)}, bf16[240,1536]{1,0:T(8,128)(2,1)S(1)}, u32[]{:S(2)}, u32[]{:S(2)}) collective-permute-start(bf16[240,1536]{1,0:T(8,128)(2,1)} %pad_maximum_fusion.3), channel_id=1, source_target_pairs={{0,96},{1,97},{2,98},{3,99},{4,100},{5,101},{6,102},{7,103},{8,104... | collective-permute-start | bytes 2211848 | tf_op jit(solution)/shard_map/ppermute | solution.py:28
  127.2 0.9 pad_maximum_fusion.2
  128.2 0.9 pad_maximum_fusion.1
  129.1 0.9 collective-permute-start.6
  130.0 0.0 copy-start.5
  130.0 13.6 %kernel_grad.1 = f32[7,7,768]{2,1,0:T(8,128)} custom-call(s32[1,8,8]{2,1,0:T(8,128)} %table_ref.13, bf16[32,32,768]{2,1,0:T(8,128)(2,1)} %bitcast.68, bf16[8,3,32,768]{3,2,1,0:T(8,128)(2,1)} %copy-done.3, bf16[32,32,768]{2,1,0:T(8,128)(2,1)} %bitcast.70), custom_call_target="tpu_custom_call" | custom-call | flops 14000000000 | bytes 5000000 | tf_op jit(solution)/shard_map/kernel_grad/pallas_call | solution.py:451
  143.6 0.9 reshape.147
  144.6 0.1 collective-permute-start.5
  144.7 5.7 %back_conv.3.refs_3_ = bf16[32,32,768]{2,1,0:T(8,128)(2,1)} custom-call(s32[1,8,8]{2,1,0:T(8,128)} %table_ref.13, bf16[32,32,768]{2,1,0:T(8,128)(2,1)} %bitcast.71, bf16[8,3,32,768]{3,2,1,0:T(8,128)(2,1)} %all-to-all-done.1.refs_0_, f32[1,7,7,768]{3,2,1,0:T(8,128)} %copy.25.refs_1_, bf16[32,32,768]{2,1,0:T(8,128)(2,1)} %bitcast.103), custom_call_target="tpu_custom_call" | custom-call | flops 4666666496 | bytes 1666666 | tf_op jit(solution)/shard_map/back_conv/pallas_call | solution.py:486
  150.4 1.5 collective-permute-start.9
  152.0 5.7 %back_conv.4.refs_3_ = bf16[32,32,768]{2,1,0:T(8,128)(2,1)} custom-call(s32[1,8,8]{2,1,0:T(8,128)} %table_ref.13, bf16[32,32,768]{2,1,0:T(8,128)(2,1)} %bitcast.72, bf16[8,3,32,768]{3,2,1,0:T(8,128)(2,1)} %all-to-all-done.1.refs_0_, f32[1,7,7,768]{3,2,1,0:T(8,128)} %copy.25.refs_1_, bf16[32,32,768]{2,1,0:T(8,128)(2,1)} %bitcast.104, ...), custom_call_target="tpu_custom_call", output_to_operand_aliasing={{}: (5, {})} | custom-call | flops 4666666496 | bytes 1666666 | tf_op jit(solution)/shard_map/back_conv/pallas_call | solution.py:486
  157.7 7.3 %collective-permute-done.9 = f32[64,768]{1,0:T(8,128)S(1)} collective-permute-done((f32[64,768]{1,0:T(8,128)S(1)}, f32[64,768]{1,0:T(8,128)S(1)}, u32[]{:S(2)}, u32[]{:S(2)}) %collective-permute-start.9) | collective-permute-done | bytes 196640 | tf_op jit(solution)/shard_map/ppermute | solution.py:28
  165.1 1.5 add_convert_fusion.2
  166.6 0.1 dynamic-slice_bitcast_fusion.4
  166.7 0.1 pad_maximum_fusion.4
  166.8 2.9 %collective-permute-start.12 = (bf16[80,1536]{1,0:T(8,128)(2,1)S(1)}, bf16[80,1536]{1,0:T(8,128)(2,1)S(1)}, u32[]{:S(2)}, u32[]{:S(2)}) collective-permute-start(bf16[80,1536]{1,0:T(8,128)(2,1)S(1)} %get-tuple-element.101), channel_id=1, source_target_pairs={{0,3},{1,2},{2,1},{3,0},{4,7},{5,6},{6,5},{7,4},{8,11},{9,10},{10,... | collective-permute-start | bytes 737288 | tf_op jit(solution)/shard_map/ppermute | solution.py:28
  169.7 0.8 collective-permute-start.11
  170.5 0.4 collective-permute-start.10
  170.9 5.7 %back_conv.5 = bf16[32,32,768]{2,1,0:T(8,128)(2,1)} custom-call(s32[1,8,8]{2,1,0:T(8,128)} %table_ref.13, bf16[32,32,768]{2,1,0:T(8,128)(2,1)} %bitcast.73, bf16[8,3,32,768]{3,2,1,0:T(8,128)(2,1)} %all-to-all-done.1.refs_0_, f32[1,7,7,768]{3,2,1,0:T(8,128)} %copy.25.refs_1_, bf16[32,32,768]{2,1,0:T(8,128)(2,1)} %bitcast.105, ...), custom_call_target="tpu_custom_call", output_to_operand_aliasing={{}: (5, {})} | custom-call | flops 4666666496 | bytes 1666666 | tf_op jit(solution)/shard_map/back_conv/pallas_call | solution.py:486
  176.7 2.7 %collective-permute-done.12 = bf16[80,1536]{1,0:T(8,128)(2,1)S(1)} collective-permute-done((bf16[80,1536]{1,0:T(8,128)(2,1)S(1)}, bf16[80,1536]{1,0:T(8,128)(2,1)S(1)}, u32[]{:S(2)}, u32[]{:S(2)}) %collective-permute-start.12) | collective-permute-done | bytes 245792 | tf_op jit(solution)/shard_map/ppermute | solution.py:28
  179.4 0.2 collective-permute-done.11
  179.7 0.6 collective-permute-done.10
  180.5 0.1 fusion.1
  180.5 0.7 slice-done
  181.3 2.9 %collective-permute-start.15 = (bf16[56,1536]{1,0:T(8,128)(2,1)S(1)}, bf16[56,1536]{1,0:T(8,128)(2,1)S(1)}, u32[]{:S(2)}, u32[]{:S(2)}) collective-permute-start(bf16[56,1536]{1,0:T(8,128)(2,1)S(1)} %get-tuple-element.100), channel_id=1, source_target_pairs={{0,20},{1,21},{2,22},{3,23},{4,16},{5,17},{6,18},{7,19},{8,28},{9,... | collective-permute-start | bytes 516104 | tf_op jit(solution)/shard_map/ppermute | solution.py:28
  184.2 0.6 collective-permute-start.14
  184.8 0.7 collective-permute-start.13
  185.5 4.0 %collective-permute-done.15 = bf16[56,1536]{1,0:T(8,128)(2,1)S(1)} collective-permute-done((bf16[56,1536]{1,0:T(8,128)(2,1)S(1)}, bf16[56,1536]{1,0:T(8,128)(2,1)S(1)}, u32[]{:S(2)}, u32[]{:S(2)}) %collective-permute-start.15) | collective-permute-done | bytes 172064 | tf_op jit(solution)/shard_map/ppermute | solution.py:28
  189.5 1.8 collective-permute-done.14
  191.4 2.9 %collective-permute-start.16 = (f32[64,768]{1,0:T(8,128)S(1)}, f32[64,768]{1,0:T(8,128)S(1)}, u32[]{:S(2)}, u32[]{:S(2)}) collective-permute-start(f32[64,768]{1,0:T(8,128)S(1)} %add_add_fusion), channel_id=1, source_target_pairs={{0,96},{1,97},{2,98},{3,99},{4,100},{5,101},{6,102},{7,103},{8,104... | collective-permute-start | bytes 589832 | tf_op jit(solution)/shard_map/ppermute | solution.py:28
  194.3 0.7 add_bitcast_fusion
  195.0 3.4 %collective-permute-done.16 = f32[64,768]{1,0:T(8,128)S(1)} collective-permute-done((f32[64,768]{1,0:T(8,128)S(1)}, f32[64,768]{1,0:T(8,128)S(1)}, u32[]{:S(2)}, u32[]{:S(2)}) %collective-permute-start.16) | collective-permute-done | bytes 196640 | tf_op jit(solution)/shard_map/ppermute | solution.py:28
  198.4 0.6 slice_bitcast_fusion
  199.1 0.8 reshape.157
  199.9 0.6 copy.30
  (55 shorter events, 0.8 us)
Async XLA Ops:
  3.5 6.2 %copy-start.4 = (f32[1,7,7,768]{3,0,2,1:T(1,128)S(1)}, f32[1,7,7,768]{3,0,2,1:T(1,128)}, u32[]{:S(2)}) copy-start(f32[1,7,7,768]{3,0,2,1:T(1,128)} %param.16) | copy-start | bytes 451588
  3.5 7.4 %copy-start.6 = (f32[1,3072]{1,0:T(1,128)S(1)}, f32[1,3072]{1,0:T(1,128)}, u32[]{:S(2)}) copy-start(f32[1,3072]{1,0:T(1,128)} %param.20) | copy-start | bytes 36868
  3.5 22.6 %all-to-all-start = ((bf16[8,3,32,768]{3,2,1,0:T(8,128)(2,1)}), bf16[8,3,32,768]{3,2,1,0:T(8,128)(2,1)S(1)}, u32[]{:S(2)}, u32[]{:S(2)}) async-start(bf16[8,3,32,768]{3,2,1,0:T(8,128)(2,1)} %pack_strips.2), calls=%async_computation | async-start | bytes 2359296 | tf_op jit(solution)/shard_map/all_to_all | solution.py:604
  26.1 1.0 copy-start.3
  64.4 18.2 %collective-permute-start = (bf16[2,2,192,1536]{3,2,1,0:T(8,128)(2,1)}, bf16[2,2,192,1536]{3,2,1,0:T(8,128)(2,1)}, u32[]{:S(2)}, u32[]{:S(2)}) collective-permute-start(bf16[2,2,192,1536]{3,2,1,0:T(8,128)(2,1)} %get-tuple-element.42), channel_id=1, source_target_pairs={{0,8},{1,9},{2,10},{3,11},{4,12},{5,13},{6,14},{7,15},{8,0},{9,1},... | collective-permute-start | bytes 7077896 | tf_op jit(solution)/shard_map/ppermute | solution.py:28
  64.8 17.3 %copy-start.7 = (f32[2,1,768]{2,1,0:T(1,128)S(1)}, f32[2,1,768]{2,1,0:T(1,128)}, u32[]{:S(2)}) copy-start(f32[2,1,768]{2,1,0:T(1,128)} %get-tuple-element.59) | copy-start | bytes 18436
  64.8 17.8 %copy-start.1 = (bf16[2,2,192,1536]{3,2,1,0:T(8,128)(2,1)S(1)}, bf16[2,2,192,1536]{3,2,1,0:T(8,128)(2,1)}, u32[]{:S(2)}) copy-start(bf16[2,2,192,1536]{3,2,1,0:T(8,128)(2,1)} %get-tuple-element.45) | copy-start | bytes 7077892
  82.2 35.8 %collective-permute-start.4 = (bf16[2,2,192,1536]{3,2,1,0:T(8,128)(2,1)}, bf16[2,2,192,1536]{3,2,1,0:T(8,128)(2,1)}, u32[]{:S(2)}, u32[]{:S(2)}) collective-permute-start(bf16[2,2,192,1536]{3,2,1,0:T(8,128)(2,1)} %get-tuple-element.56), channel_id=1, source_target_pairs={{0,8},{1,9},{2,10},{3,11},{4,12},{5,13},{6,14},{7,15},{8,0},{9,1},... | collective-permute-start | bytes 7077896 | tf_op jit(solution)/shard_map/ppermute | solution.py:28
  86.1 34.4 %collective-permute-start.3 = (bf16[4,2,24,1536]{3,2,1,0:T(8,128)(2,1)}, bf16[4,2,24,1536]{3,2,1,0:T(8,128)(2,1)}, u32[]{:S(2)}, u32[]{:S(2)}) collective-permute-start(bf16[4,2,24,1536]{3,2,1,0:T(8,128)(2,1)} %get-tuple-element.76), channel_id=1, source_target_pairs={{0,3},{1,2},{2,1},{3,0},{4,7},{5,6},{6,5},{7,4},{8,11},{9,10},{10,... | collective-permute-start | bytes 1769480 | tf_op jit(solution)/shard_map/ppermute | solution.py:28
  86.7 33.8 %collective-permute-start.2 = (bf16[4,2,24,1536]{3,2,1,0:T(8,128)(2,1)}, bf16[4,2,24,1536]{3,2,1,0:T(8,128)(2,1)}, u32[]{:S(2)}, u32[]{:S(2)}) collective-permute-start(bf16[4,2,24,1536]{3,2,1,0:T(8,128)(2,1)} %get-tuple-element.77), channel_id=1, source_target_pairs={{0,2},{1,3},{2,0},{3,1},{4,6},{5,7},{6,4},{7,5},{8,10},{9,11},{10,... | collective-permute-start | bytes 1769480 | tf_op jit(solution)/shard_map/ppermute | solution.py:28
  89.1 31.5 %collective-permute-start.1 = (bf16[4,2,24,1536]{3,2,1,0:T(8,128)(2,1)S(1)}, bf16[4,2,24,1536]{3,2,1,0:T(8,128)(2,1)}, u32[]{:S(2)}, u32[]{:S(2)}) collective-permute-start(bf16[4,2,24,1536]{3,2,1,0:T(8,128)(2,1)S(1)} %get-tuple-element.78), channel_id=1, source_target_pairs={{0,1},{1,0},{2,3},{3,2},{4,5},{5,4},{6,7},{7,6},{8,9},{9,8},{10,11... | collective-permute-start | bytes 1769480 | tf_op jit(solution)/shard_map/ppermute | solution.py:28
  113.6 4.4 %copy-start.2 = (bf16[2,2,192,1536]{3,2,1,0:T(8,128)(2,1)S(1)}, bf16[2,2,192,1536]{3,2,1,0:T(8,128)(2,1)}, u32[]{:S(2)}) copy-start(bf16[2,2,192,1536]{3,2,1,0:T(8,128)(2,1)} %get-tuple-element.55) | copy-start | bytes 7077892
  113.6 31.1 %all-to-all-start.1 = ((bf16[8,3,32,768]{3,2,1,0:T(8,128)(2,1)}), bf16[8,3,32,768]{3,2,1,0:T(8,128)(2,1)}, u32[]{:S(2)}, u32[]{:S(2)}) async-start(bf16[8,3,32,768]{3,2,1,0:T(8,128)(2,1)} %pack_strips.3), calls=%async_computation.1 | async-start | bytes 2359296 | tf_op jit(solution)/shard_map/all_to_all | solution.py:625
  123.2 41.9 %collective-permute-start.8 = (bf16[240,1536]{1,0:T(8,128)(2,1)}, bf16[240,1536]{1,0:T(8,128)(2,1)S(1)}, u32[]{:S(2)}, u32[]{:S(2)}) collective-permute-start(bf16[240,1536]{1,0:T(8,128)(2,1)} %pad_maximum_fusion.3), channel_id=1, source_target_pairs={{0,96},{1,97},{2,98},{3,99},{4,100},{5,101},{6,102},{7,103},{8,104... | collective-permute-start | bytes 2211848 | tf_op jit(solution)/shard_map/ppermute | solution.py:28
  128.2 36.9 %collective-permute-start.7 = (bf16[240,1536]{1,0:T(8,128)(2,1)}, bf16[240,1536]{1,0:T(8,128)(2,1)S(1)}, u32[]{:S(2)}, u32[]{:S(2)}) collective-permute-start(bf16[240,1536]{1,0:T(8,128)(2,1)} %pad_maximum_fusion.2), channel_id=1, source_target_pairs={{0,64},{1,65},{2,66},{3,67},{4,68},{5,69},{6,70},{7,71},{8,72},{9,... | collective-permute-start | bytes 2211848 | tf_op jit(solution)/shard_map/ppermute | solution.py:28
  129.1 36.0 %collective-permute-start.6 = (bf16[240,1536]{1,0:T(8,128)(2,1)}, bf16[240,1536]{1,0:T(8,128)(2,1)}, u32[]{:S(2)}, u32[]{:S(2)}) collective-permute-start(bf16[240,1536]{1,0:T(8,128)(2,1)} %pad_maximum_fusion.1), channel_id=1, source_target_pairs={{0,32},{1,33},{2,34},{3,35},{4,36},{5,37},{6,38},{7,39},{8,40},{9,... | collective-permute-start | bytes 2211848 | tf_op jit(solution)/shard_map/ppermute | solution.py:28
  130.0 14.5 %copy-start.5 = (f32[4,768]{1,0:T(4,128)S(1)}, f32[4,768]{1,0:T(4,128)}, u32[]{:S(2)}) copy-start(f32[4,768]{1,0:T(4,128)} %get-tuple-element.58) | copy-start | bytes 36868
  144.6 5.8 %collective-permute-start.5 = (f32[64,768]{1,0:T(8,128)S(1)}, f32[64,768]{1,0:T(8,128)S(1)}, u32[]{:S(2)}, u32[]{:S(2)}) collective-permute-start(f32[64,768]{1,0:T(8,128)S(1)} %select_maximum_fusion), channel_id=1, source_target_pairs={{0,8},{1,9},{2,10},{3,11},{4,12},{5,13},{6,14},{7,15},{8,0},{9,1},... | collective-permute-start | bytes 589832 | tf_op jit(solution)/shard_map/ppermute | solution.py:28
  150.4 14.5 %collective-permute-start.9 = (f32[64,768]{1,0:T(8,128)S(1)}, f32[64,768]{1,0:T(8,128)S(1)}, u32[]{:S(2)}, u32[]{:S(2)}) collective-permute-start(f32[64,768]{1,0:T(8,128)S(1)} %add.175), channel_id=1, source_target_pairs={{0,32},{1,33},{2,34},{3,35},{4,36},{5,37},{6,38},{7,39},{8,40},{9,... | collective-permute-start | bytes 589832 | tf_op jit(solution)/shard_map/ppermute | solution.py:28
  166.6 4.4 %copy-start = (bf16[240,1536]{1,0:T(8,128)(2,1)}, bf16[240,1536]{1,0:T(8,128)(2,1)S(1)}, u32[]{:S(2)}) copy-start(bf16[240,1536]{1,0:T(8,128)(2,1)S(1)} %add_convert_fusion.2) | copy-start | bytes 2211844
  166.8 12.6 %collective-permute-start.12 = (bf16[80,1536]{1,0:T(8,128)(2,1)S(1)}, bf16[80,1536]{1,0:T(8,128)(2,1)S(1)}, u32[]{:S(2)}, u32[]{:S(2)}) collective-permute-start(bf16[80,1536]{1,0:T(8,128)(2,1)S(1)} %get-tuple-element.101), channel_id=1, source_target_pairs={{0,3},{1,2},{2,1},{3,0},{4,7},{5,6},{6,5},{7,4},{8,11},{9,10},{10,... | collective-permute-start | bytes 737288 | tf_op jit(solution)/shard_map/ppermute | solution.py:28
  169.7 9.9 %collective-permute-start.11 = (bf16[80,1536]{1,0:T(8,128)(2,1)S(1)}, bf16[80,1536]{1,0:T(8,128)(2,1)S(1)}, u32[]{:S(2)}, u32[]{:S(2)}) collective-permute-start(bf16[80,1536]{1,0:T(8,128)(2,1)S(1)} %get-tuple-element.102), channel_id=1, source_target_pairs={{0,2},{1,3},{2,0},{3,1},{4,6},{5,7},{6,4},{7,5},{8,10},{9,11},{10,... | collective-permute-start | bytes 737288 | tf_op jit(solution)/shard_map/ppermute | solution.py:28
  170.5 9.7 %collective-permute-start.10 = (bf16[80,1536]{1,0:T(8,128)(2,1)S(1)}, bf16[80,1536]{1,0:T(8,128)(2,1)S(1)}, u32[]{:S(2)}, u32[]{:S(2)}) collective-permute-start(bf16[80,1536]{1,0:T(8,128)(2,1)S(1)} %get-tuple-element.103), channel_id=1, source_target_pairs={{0,1},{1,0},{2,3},{3,2},{4,5},{5,4},{6,7},{7,6},{8,9},{9,8},{10,11... | collective-permute-start | bytes 737288 | tf_op jit(solution)/shard_map/ppermute | solution.py:28
  180.3 0.9 slice-start
  181.3 8.2 %collective-permute-start.15 = (bf16[56,1536]{1,0:T(8,128)(2,1)S(1)}, bf16[56,1536]{1,0:T(8,128)(2,1)S(1)}, u32[]{:S(2)}, u32[]{:S(2)}) collective-permute-start(bf16[56,1536]{1,0:T(8,128)(2,1)S(1)} %get-tuple-element.100), channel_id=1, source_target_pairs={{0,20},{1,21},{2,22},{3,23},{4,16},{5,17},{6,18},{7,19},{8,28},{9,... | collective-permute-start | bytes 516104 | tf_op jit(solution)/shard_map/ppermute | solution.py:28
  184.2 7.1 %collective-permute-start.14 = (bf16[56,1536]{1,0:T(8,128)(2,1)S(1)}, bf16[56,1536]{1,0:T(8,128)(2,1)S(1)}, u32[]{:S(2)}, u32[]{:S(2)}) collective-permute-start(bf16[56,1536]{1,0:T(8,128)(2,1)S(1)} %get-tuple-element.99), channel_id=1, source_target_pairs={{0,16},{1,17},{2,18},{3,19},{4,20},{5,21},{6,22},{7,23},{8,24},{9,... | collective-permute-start | bytes 516104 | tf_op jit(solution)/shard_map/ppermute | solution.py:28
  184.8 6.6 %collective-permute-start.13 = (bf16[56,1536]{1,0:T(8,128)(2,1)S(1)}, bf16[56,1536]{1,0:T(8,128)(2,1)S(1)}, u32[]{:S(2)}, u32[]{:S(2)}) collective-permute-start(bf16[56,1536]{1,0:T(8,128)(2,1)S(1)} %get-tuple-element.98), channel_id=1, source_target_pairs={{0,4},{1,5},{2,6},{3,7},{4,0},{5,1},{6,2},{7,3},{8,12},{9,13},{10,... | collective-permute-start | bytes 516104 | tf_op jit(solution)/shard_map/ppermute | solution.py:28
  191.4 7.0 %collective-permute-start.16 = (f32[64,768]{1,0:T(8,128)S(1)}, f32[64,768]{1,0:T(8,128)S(1)}, u32[]{:S(2)}, u32[]{:S(2)}) collective-permute-start(f32[64,768]{1,0:T(8,128)S(1)} %add_add_fusion), channel_id=1, source_target_pairs={{0,96},{1,97},{2,98},{3,99},{4,100},{5,101},{6,102},{7,103},{8,104... | collective-permute-start | bytes 589832 | tf_op jit(solution)/shard_map/ppermute | solution.py:28

commit v3 on v2

--- a/solution.py
+++ b/solution.py
@@ -21,6 +21,8 @@
 own_column = 8
 wide = 48
 vmem_limit = 58 * 1024 * 1024
+middle_limit = vmem_limit
+small_limit = vmem_limit
 
 
 def swap(value, distance):
@@ -64,6 +66,7 @@
             pltpu.VMEM((16 * side, lanes), f32),
             pltpu.VMEM((2, rim, side, channels), bf16),
         ],
+        compiler_params=pltpu.CompilerParams(vmem_limit_bytes=small_limit),
         name="pack_strips",
     )(table, tile)
 
@@ -121,18 +124,109 @@
     lax.fori_loop(0, side // row_block, rows, 0)
 
 
-def conv_kernel(table_ref, tile_ref, *refs):
-    strip_ref, weight_ref, gain_ref, shift_ref = refs[:4]
-    whitened_ref, inv_ref, normed_ref, extended_ref, spread_ref, conv_ref = refs[4:]
+def inner_kernel(tile_ref, weight_ref, out_ref, extended_ref, spread_ref):
+    @pl.when(pl.program_id(0) == 0)
+    def _():
+        extended_ref[...] = jnp.zeros_like(extended_ref)
+
+    extended_ref[rim : rim + side, own_column : own_column + side, :] = tile_ref[...].astype(f32)
+    spread_weights(weight_ref, spread_ref, False)
+
+    def store(row, column, value):
+        out_ref[0, row, column : column + 8, :] = value
+
+    depthwise(extended_ref, spread_ref, store)
+
+
+def conv_inner(tile, weight):
+    channels = tile.shape[-1]
+    blocks = channels // lanes
+    return pl.pallas_call(
+        inner_kernel,
+        grid=(blocks,),
+        out_shape=jax.ShapeDtypeStruct((blocks, side, side, lanes), f32),
+        in_specs=[
+            pl.BlockSpec((side, side, lanes), lambda i: (0, 0, i)),
+            pl.BlockSpec((1, taps, taps, lanes), lambda i: (0, 0, 0, i)),
+        ],
+        out_specs=pl.BlockSpec((1, side, side, lanes), lambda i: (i, 0, 0, 0)),
+        scratch_shapes=[
+            pltpu.VMEM((side + 2 * rim, wide, lanes), f32),
+            pltpu.VMEM((taps, taps, 8, lanes), f32),
+        ],
+        compiler_params=pltpu.CompilerParams(vmem_limit_bytes=small_limit),
+        cost_estimate=pl.CostEstimate(flops=14_000_000_000, bytes_accessed=5_000_000, transcendentals=0),
+        name="conv_inner",
+    )(tile, weight)
+
+
+def add_rim(table_ref, strip_ref, spread_ref, rows_ref, edge_ref, conv_ref, block):
+    me = lax.axis_index("tile")
+    tiles = strip_ref.shape[0]
+
+    def strip(direction):
+        other = table_ref[0, me, direction]
+        values = strip_ref[jnp.minimum(other, tiles - 1)].astype(f32)
+        return jnp.where(other < tiles, values, jnp.zeros_like(values))
+
+    right = own_column + side
+    for at, (middle, left, end) in enumerate(((0, 4, 5), (1, 6, 7))):
+        rows_ref[at, :, own_column:right, :] = strip(middle)
+        rows_ref[at, :, 0:8, :] = strip(left)[:, side - 8 :]
+        rows_ref[at, :, right : right + 8, :] = strip(end)[:, :8]
+    west, east = strip(2), strip(3)
+    for c in range(rim):
+        edge_ref[0, rim : rim + side, own_column - rim + c, :] = west[c]
+        edge_ref[1, rim : rim + side, 8 + c, :] = east[c]
+
+    for w in range(side // 8):
+        for at, row, terms in (
+            (0, 0, ((0, 0), (1, 1), (2, 2))),
+            (0, 1, ((1, 0), (2, 1))),
+            (0, 2, ((2, 0),)),
+            (1, side - 1, ((0, 4), (1, 5), (2, 6))),
+            (1, side - 2, ((0, 5), (1, 6))),
+            (1, side - 3, ((0, 6),)),
+        ):
+            total = conv_ref[block, row, w * 8 : w * 8 + 8, :]
+            for b in range(taps):
+                start = own_column - rim + b + w * 8
+                for source, a in terms:
+                    total = total + rows_ref[at, source, start : start + 8, :] * spread_ref[b, a]
+            conv_ref[block, row, w * 8 : w * 8 + 8, :] = total
+
+    def columns(part, carry):
+        base = part * row_block
+        for which, w, picks in ((0, 0, ((0, 5), (1, 6), (2, 7))), (1, side // 8 - 1, ((4, 1), (5, 2), (6, 3)))):
+            here = slice(w * 8, w * 8 + 8)
+            totals = [conv_ref[block, base + r, here, :] for r in range(row_block)]
+            for b, start in picks:
+                values = [edge_ref[which, base + r, start : start + 8, :] for r in range(row_block + taps - 1)]
+                for a in range(taps):
+                    factor = spread_ref[b, a]
+                    for r in range(row_block):
+                        totals[r] = totals[r] + values[r + a] * factor
+            for r in range(row_block):
+                conv_ref[block, base + r, here, :] = totals[r]
+        return carry
+
+    lax.fori_loop(0, side // row_block, columns, 0)
+
+
+def norm_kernel(
+    table_ref, part_ref, strip_ref, weight_ref, gain_ref, shift_ref,
+    whitened_ref, inv_ref, normed_ref, spread_ref, rows_ref, edge_ref, conv_ref,
+):
     block = pl.program_id(0)
     blocks = whitened_ref.shape[1] // lanes
-    assemble(table_ref, tile_ref, strip_ref, extended_ref)
+
+    @pl.when(block == 0)
+    def _():
+        edge_ref[...] = jnp.zeros_like(edge_ref)
+
     spread_weights(weight_ref, spread_ref, False)
-
-    def store(row, column, value):
-        conv_ref[block, row, column : column + 8, :] = value
-
-    depthwise(extended_ref, spread_ref, store)
+    conv_ref[block] = part_ref[0]
+    add_rim(table_ref, strip_ref, spread_ref, rows_ref, edge_ref, conv_ref, block)
 
     @pl.when(block == blocks - 1)
     def _():
@@ -152,20 +246,20 @@
                 normed_ref[here, at] = (whitened * gain_ref[:, at] + shift_ref[:, at]).astype(bf16)
             return carry
 
-        lax.fori_loop(0, side, norm, 0)
+        lax.fori_loop(0, side, norm, 0, unroll=4)
 
 
 def strip_spec(strips, first=0):
     return pl.BlockSpec((*strips.shape[:3], lanes), lambda i: (0, 0, 0, first + i))
 
 
-def conv_norm(table, tile, strips, weight, gain, shift):
-    channels = tile.shape[-1]
+def conv_norm(table, part, strips, weight, gain, shift):
+    blocks = part.shape[0]
+    channels = blocks * lanes
     pixels = side * side
-    blocks = channels // lanes
     whole = lambda i: (0, 0)
     return pl.pallas_call(
-        conv_kernel,
+        norm_kernel,
         grid=(blocks,),
         out_shape=[
             jax.ShapeDtypeStruct((pixels, channels), f32),
@@ -174,26 +268,23 @@
         ],
         in_specs=[
             pl.BlockSpec(memory_space=pltpu.SMEM),
-            pl.BlockSpec((side, side, lanes), lambda i: (0, 0, i)),
+            pl.BlockSpec((1, side, side, lanes), lambda i: (i, 0, 0, 0)),
             strip_spec(strips),
             pl.BlockSpec((1, taps, taps, lanes), lambda i: (0, 0, 0, i)),
             pl.BlockSpec((1, channels), whole),
             pl.BlockSpec((1, channels), whole),
         ],
-        out_specs=[
-            pl.BlockSpec((pixels, channels), whole),
-            pl.BlockSpec((pixels, 1), whole),
-            pl.BlockSpec((pixels, channels), whole),
-        ],
+        out_specs=[full(pixels, channels), full(pixels, 1), full(pixels, channels)],
         scratch_shapes=[
-            pltpu.VMEM((side + 2 * rim, wide, lanes), f32),
             pltpu.VMEM((taps, taps, 8, lanes), f32),
+            pltpu.VMEM((2, rim, wide, lanes), f32),
+            pltpu.VMEM((2, side + 2 * rim, 16, lanes), f32),
             pltpu.VMEM((blocks, side, side, lanes), f32),
         ],
-        compiler_params=pltpu.CompilerParams(vmem_limit_bytes=vmem_limit),
-        cost_estimate=pl.CostEstimate(flops=14_000_000_000, bytes_accessed=10_000_000, transcendentals=0),
+        compiler_params=pltpu.CompilerParams(vmem_limit_bytes=middle_limit),
+        cost_estimate=pl.CostEstimate(flops=7_000_000_000, bytes_accessed=10_000_000, transcendentals=0),
         name="conv_norm",
-    )(table, tile, strips, weight, gain, shift)
+    )(table, part, strips, weight, gain, shift)
 
 
 dot = functools.partial(lax.dot_general, preferred_element_type=f32)
@@ -368,7 +459,7 @@
             )
 
         zero = jnp.zeros((8, channels), f32)
-        sums = lax.fori_loop(0, pixels // rows_each, finish, (zero,) * 4)
+        sums = lax.fori_loop(0, pixels // rows_each, finish, (zero,) * 4, unroll=2)
         for at in range(4):
             channel_ref[at : at + 1, :] = jnp.sum(sums[at], axis=0, keepdims=True)
 
@@ -459,6 +550,7 @@
             pltpu.VMEM((side, side, lanes), f32),
             pltpu.VMEM((taps, taps, 8, lanes), f32),
         ],
+        compiler_params=pltpu.CompilerParams(vmem_limit_bytes=small_limit),
         cost_estimate=pl.CostEstimate(flops=14_000_000_000, bytes_accessed=5_000_000, transcendentals=0),
         name="kernel_grad",
     )(table, tile, strips, conv_grad)
@@ -502,6 +594,7 @@
             pltpu.VMEM((side, side, lanes), f32),
         ],
         input_output_aliases={5: 0} if earlier else {},
+        compiler_params=pltpu.CompilerParams(vmem_limit_bytes=small_limit),
         cost_estimate=pl.CostEstimate(
             flops=14_000_000_000 // parts, bytes_accessed=5_000_000 // parts, transcendentals=0
         ),
@@ -553,9 +646,13 @@
 z_distances = (32, 64, 96)
 
 
-def gather_sum(parts, distances, dtype):
+def gather_sum(parts, distances, dtype, ready):
     arrived = [swap(part, d) for part, d in zip(parts[1:], distances)]
-    return fold([parts[0], *arrived], dtype)
+    return fold(gate([parts[0], *arrived], ready), dtype)
+
+
+def gate(values, ready):
+    return list(lax.optimization_barrier((*values, ready))[: len(values)])
 
 
 def after(value, *others):
@@ -563,8 +660,8 @@
 
 
 def trade(value, distance, ready):
-    arrived = swap(value, distance)
-    return after(value, ready) + arrived
+    value, arrived = gate([value, swap(value, distance)], ready)
+    return value + arrived
 
 
 def ride(parts, small):
@@ -577,7 +674,7 @@
 def land(sent, small, parts, distances, dtype, ready):
     arrived = [swap(value, d) for value, d in zip(sent, distances)]
     size = parts[0].size // parts[0].shape[-1]
-    mine, small = lax.optimization_barrier((parts[0], small, ready))[:2]
+    mine, small, *arrived = gate([parts[0], small, *arrived], ready)
     total = fold([mine, *[value[:size].reshape(mine.shape) for value in arrived]], dtype)
     return total, fold([small, *[value[size:].reshape(small.shape) for value in arrived]], f32)
 
@@ -601,8 +698,11 @@
     tile = features[0, 0]
     grad = cotangent[0, 0]
     flat = (side * side, channels)
-    strips = lax.all_to_all(pack_strips(neighbours, tile), "tile", 0, 0)
-    whitened, inv_std, normed = conv_norm(neighbours, tile, strips, dw_weight, ln_gain, ln_bias)
+    packed = pack_strips(neighbours, tile)
+    strips = lax.all_to_all(packed, "tile", 0, 0)
+    inner = conv_inner(after(tile, packed), dw_weight)
+    strips = after(strips, inner)
+    whitened, inv_std, normed = conv_norm(neighbours, inner, strips, dw_weight, ln_gain, ln_bias)
     flat_grad = grad.reshape(flat)
     bias_order = jnp.swapaxes(up_bias.reshape(4, 2, -1), 0, 1).reshape(4, 1, -1)
     mlp_in = (flat_grad, up_weight[0], bias_order, down_weight[0], layer_scale)
@@ -613,22 +713,21 @@
     width = mine_low.shape[3]
     grid = (4, 2, 4, rows, width)
     received_high = swap(theirs_high, 8)
-    low_x = x_parts(fold([after(mine_low, act_high), received_low], bf16).reshape(grid))
+    low_x = x_parts(fold(gate([mine_low, received_low], act_high), bf16).reshape(grid))
+    high_z = z_parts(fold([mine_high, received_high], bf16).reshape(grid))
+    got_high = [swap(high_z[1], 32), swap(high_z[3], 96)]
     out, conv_grad, channel_sums = join(
-        skip_flags, (after(act_low, *low_x), act_high), (pre_low, pre_high), up_weight[0], down_weight[0],
+        skip_flags, (after(act_low, *low_x, *high_z), act_high), (pre_low, pre_high), up_weight[0], down_weight[0],
         inv_std, down_bias, layer_scale, ln_gain, whitened, tile.reshape(flat), flat_grad,
     )
+    got_far = swap(after(high_z[2], conv_grad), 64)
     conv_grad = conv_grad.reshape(tile.shape)
     packed = pack_strips(neighbours, conv_grad)
-    low_x[0] = after(low_x[0], packed)
-    mine_high = after(mine_high, packed)
     grad_strips = lax.all_to_all(packed, "tile", 0, 0)
-    low_z = z_parts(gather_sum(low_x, x_distances, bf16))
-    high_z = z_parts(fold([mine_high, received_high], bf16).reshape(grid))
-    sent_z = [
-        jnp.concatenate([low.reshape(-1, width), high.reshape(-1, width)], 0) for low, high in zip(low_z, high_z)
-    ]
-    kernel_sums = kernel_grad(neighbours, tile, strips, after(conv_grad, *sent_z))
+    first, second, third = gate([high_z[0], *got_high], packed)
+    near = first.astype(f32) + second.astype(f32) + third.astype(f32)
+    low_z = z_parts(gather_sum(low_x, x_distances, bf16, packed))
+    kernel_sums = kernel_grad(neighbours, tile, strips, after(conv_grad, near, *low_z))
     small = jnp.concatenate(
         [
             kernel_sums.reshape(taps * taps, channels),
@@ -639,23 +738,22 @@
     )
     count = small.shape[0]
     small = jnp.pad(small, ((0, -count % 16), (0, 0)))
+    done_low = gather_sum(low_z, z_distances, bf16, kernel_sums)
+    high_x = x_parts(fold(gate([near, got_far], done_low), bf16))
     back = functools.partial(back_conv, neighbours)
     grad_strips = after(grad_strips, small)
-    input_grad = back(conv_grad, grad_strips, dw_weight, grad, 0, 3)
-    small = trade(small, 8, input_grad)
-    input_grad = back(after(conv_grad, small), grad_strips, dw_weight, grad, 1, 3, input_grad)
-    small = trade(small, 32, input_grad)
-    sent_z[0] = after(sent_z[0], input_grad)
-    got_z = gather_sum(sent_z, z_distances, bf16)
-    done_low = got_z[: 2 * rows]
-    high_x = x_parts(got_z[2 * rows :].reshape(2, 4, rows, width))
     wide_x, small = ride(high_x, small)
-    input_grad = back(after(conv_grad, *wide_x), grad_strips, dw_weight, grad, 2, 3, input_grad)
+    input_grad = back(after(conv_grad, *wide_x), grad_strips, dw_weight, grad, 0, 3)
     done_high, small = land(wide_x, small, high_x, x_distances, bf16, input_grad)
-    last = y_parts(jnp.concatenate([done_low, done_high.reshape(-1, width)], 0).reshape(2, 2, rows, width))
+    last = y_parts(jnp.concatenate([done_low, done_high], 0).reshape(2, 2, rows, width))
     wide_y, small = ride(last, small)
+    input_grad = back(after(conv_grad, *wide_y), grad_strips, dw_weight, grad, 1, 3, input_grad)
     weight_rows, small = land(wide_y, small, last, y_distances, f32, input_grad)
-    small = trade(small, 96, small)[:count]
+    sent_small = small.astype(bf16)
+    got_small = [swap(sent_small, d) for d in z_distances]
+    input_grad = back(after(conv_grad, sent_small), grad_strips, dw_weight, grad, 2, 3, input_grad)
+    small = fold(gate([lax.reduce_precision(small, 8, 7), *got_small], input_grad), f32)
+    small = trade(small, 8, small)[:count]
     split = taps * taps
     return (
         out.reshape(features.shape),

time: 202 us -> 190 us (0.941)
  waiting for transfers between devices: 34 us -> 13.7 us
  starting transfers between devices: 32.4 us -> 39.9 us
  other arithmetic: 13.2 us -> 10.7 us
    all_to_all x1, waiting for transfers between devices: 13.9 us -> 1.33 us  [on_device(): strips = lax.all_to_all(packed, 'tile', 0, 0)]
    ppermute x17 -> x21, starting transfers between devices: 22.5 us -> 30.2 us  [swap(): return lax.ppermute(value, both_axes, pairs)]
    ppermute x17 -> x21, waiting for transfers between devices: 20.1 us -> 12.4 us  [swap(): return lax.ppermute(value, both_axes, pairs)]
    concatenate x6 -> x1, other arithmetic: 2.87 us -> 0.03 us  [on_device(): jnp.concatenate([done_low, done_high], 0).reshape(2, 2, rows, width)]
    pallas_call x1 -> x2, Pallas kernels: 20.9 us -> 23.1 us  [the longest x1 12.6 us: conv_inner(): pl.pallas_call(inner_kernel, grid=(blocks,), out_shape=jax.ShapeDtypeStru...]
    squeeze x3 -> x4, local copies, waits for them, and re-layouts: 1.29 us -> 3.33 us  [pick(): value = lax.dynamic_index_in_dim(value, index, axis, keepdims=False)]
    convert_element_type x5 -> x6, other arithmetic: 7.81 us -> 6.65 us  [fold(): return wide_parts[0].astype(dtype)]
  transfers between devices with their start and end apart: 19 -> 23, of which waited for: 8 -> 7; matrix products, arithmetic and copies ran while one was open for 8% -> 7% of each run, Pallas kernels for 35% -> 44%
where the time goes in v3:
time: 190 us; the launch traced here: 189 us
  Pallas kernels  113 us (59%)
  starting transfers between devices  39.9 us (21%)
  waiting for transfers between devices  13.7 us (7%)
  other arithmetic  10.7 us (6%)
  local copies, waits for them, and re-layouts  9.53 us (5%)
    pallas_call x2, Pallas kernels, hidden_half(): pl.pallas_call(hidden_kernel, grid=(steps,), out_shape=[wide_shape, wide_...  32.9 us
    ppermute x21, starting transfers between devices, swap(): return lax.ppermute(value, both_axes, pairs)  30.2 us
    pallas_call x1, Pallas kernels, join(): pl.pallas_call(join_kernel, grid=(4,), out_shape=[pixel, pixel, jax.Shape...  20.7 us
    pallas_call x3, Pallas kernels, back_conv(): pl.pallas_call(back_kernel, grid=(steps,), out_shape=jax.ShapeDtypeStruct...  17.1 us
    pallas_call x1, Pallas kernels, kernel_grad(): pl.pallas_call(kernel_grad_kernel, grid=(channels // lanes,), out_shape=j...  13.6 us
    pallas_call x1, Pallas kernels, conv_inner(): pl.pallas_call(inner_kernel, grid=(blocks,), out_shape=jax.ShapeDtypeStru...  12.6 us
    ppermute x21, waiting for transfers between devices, swap(): return lax.ppermute(value, both_axes, pairs)  12.4 us
    pallas_call x1, Pallas kernels, conv_norm(): pl.pallas_call(norm_kernel, grid=(blocks,), out_shape=[jax.ShapeDtypeStru...  10.6 us
  transfers between devices with their start and end apart: 23, of which 7 were waited for; matrix products, arithmetic and copies ran while one was open for 7% of the time, Pallas kernels for 44%

profile of v3, /device:TPU:0, one launch (start us, length us, event | category | flops | bytes accessed | tf_op | source)
XLA Modules:
  0.0 188.6 jit_solution(317664826049349226)
XLA Ops:
  0.7 2.9 %pack_strips.2 = bf16[8,3,32,768]{3,2,1,0:T(8,128)(2,1)} custom-call(s32[1,8,8]{2,1,0:T(8,128)} %table_ref.13, bf16[32,32,768]{2,1,0:T(8,128)(2,1)} %bitcast.66), custom_call_target="tpu_custom_call" | custom-call | tf_op jit(solution)/shard_map/pack_strips/pallas_call | solution.py:60
  3.5 5.4 %all-to-all-start = ((bf16[8,3,32,768]{3,2,1,0:T(8,128)(2,1)}), bf16[8,3,32,768]{3,2,1,0:T(8,128)(2,1)S(1)}, u32[]{:S(2)}, u32[]{:S(2)}) async-start(bf16[8,3,32,768]{3,2,1,0:T(8,128)(2,1)} %pack_strips.2), calls=%async_computation | async-start | bytes 2359296 | tf_op jit(solution)/shard_map/all_to_all | solution.py:702
  9.6 0.7 copy.20.weight_ref.refs_1_
  10.3 0.5 broadcast.28
  10.8 0.7 reduce.5
  11.5 0.6 reshape.96.up_bias_ref
  12.1 12.6 %conv_inner.1.part_ref = f32[6,32,32,128]{3,2,1,0:T(8,128)} custom-call(bf16[32,32,768]{2,1,0:T(8,128)(2,1)} %bitcast.67, f32[1,7,7,768]{3,2,1,0:T(8,128)} %copy.20.weight_ref.refs_1_), custom_call_target="tpu_custom_call" | custom-call | flops 14000000000 | bytes 5000000 | tf_op jit(solution)/shard_map/conv_inner/pallas_call | solution.py:144
  24.7 1.3 all-to-all-done.strip_ref.refs_0_
  26.0 1.0 copy-done.1
  27.0 10.6 %conv_norm.1 = (f32[1024,768]{1,0:T(8,128)}, f32[1024,1]{1,0:T(8,128)}, bf16[1024,768]{1,0:T(8,128)(2,1)}) custom-call(s32[1,8,8]{2,1,0:T(8,128)} %table_ref.13, f32[6,32,32,128]{3,2,1,0:T(8,128)} %conv_inner.1.part_ref, bf16[8,3,32,768]{3,2,1,0:T(8,128)(2,1)} %copy-done.1, f32[1,7,7,768]{3,2,1,0:T(8,128)} %copy.20.weight_ref.refs_1_, f32[1,768]{1,0:T(1,128)} %gain_ref.3, ...), custom_call_target="tpu_custom_call" | custom-call | flops 7000000000 | bytes 10000000 | tf_op jit(solution)/shard_map/conv_norm/pallas_call | solution.py:261
  37.6 16.4 %hidden_half.2 = (bf16[1024,1536]{1,0:T(8,128)(2,1)}, bf16[1024,1536]{1,0:T(8,128)(2,1)}, bf16[2,2,192,1536]{3,2,1,0:T(8,128)(2,1)}, bf16[2,2,192,1536]{3,2,1,0:T(8,128)(2,1)}, f32[2,1,768]{2,1,0:T(1,128)}) custom-call(s32[1,1]{1,0:T(1,128)S(6)} %copy.31.skip_ref, bf16[1024,768]{1,0:T(8,128)(2,1)} %get-tuple-element.69.normed_ref, ...), custom_call_target="tpu_custom_call" | custom-call | flops 14000000000 | bytes 20000000 | tf_op jit(solution)/shard_map/hidden_half/pallas_call | solution.py:375
  54.0 0.3 collective-permute-start
  54.3 16.5 %hidden_half.3 = (bf16[1024,1536]{1,0:T(8,128)(2,1)}, bf16[1024,1536]{1,0:T(8,128)(2,1)}, bf16[2,2,192,1536]{3,2,1,0:T(8,128)(2,1)}, bf16[2,2,192,1536]{3,2,1,0:T(8,128)(2,1)}, f32[2,1,768]{2,1,0:T(1,128)}) custom-call(s32[1,1]{1,0:T(1,128)S(6)} %copy.31.skip_ref, bf16[1024,768]{1,0:T(8,128)(2,1)} %get-tuple-element.69.normed_ref, ...), custom_call_target="tpu_custom_call" | custom-call | flops 14000000000 | bytes 20000000 | tf_op jit(solution)/shard_map/hidden_half/pallas_call | solution.py:375
  70.8 0.6 collective-permute-start.1
  71.3 0.7 reduce.2
  72.1 3.7 %collective-permute-done.1 = bf16[2,2,192,1536]{3,2,1,0:T(8,128)(2,1)} collective-permute-done((bf16[2,2,192,1536]{3,2,1,0:T(8,128)(2,1)}, bf16[2,2,192,1536]{3,2,1,0:T(8,128)(2,1)}, u32[]{:S(2)}, u32[]{:S(2)}) %collective-permute-start.1) | collective-permute-done | bytes 2359328 | tf_op jit(solution)/shard_map/ppermute | solution.py:30
  75.8 3.0 %add_convert_fusion = bf16[2,2,192,1536]{3,2,1,0:T(8,128)(2,1)S(1)} fusion(bf16[2,2,192,1536]{3,2,1,0:T(8,128)(2,1)} %collective-permute-done.1, bf16[2,2,192,1536]{3,2,1,0:T(8,128)(2,1)} %get-tuple-element.73), kind=kLoop, calls=%fused_computation | loop fusion | flops 4718592 | bytes 7077888 | tf_op jit(solution)/shard_map/convert_element_type | solution.py:615
  78.8 1.3 dynamic-slice_bitcast_fusion
  80.1 1.9 %collective-permute-start.8 = (bf16[2,4,24,1536]{3,2,1,0:T(8,128)(2,1)}, bf16[2,4,24,1536]{3,2,1,0:T(8,128)(2,1)}, u32[]{:S(2)}, u32[]{:S(2)}) collective-permute-start(bf16[2,4,24,1536]{3,2,1,0:T(8,128)(2,1)} %get-tuple-element.122), channel_id=1, source_target_pairs={{0,32},{1,33},{2,34},{3,35},{4,36},{5,37},{6,38},{7,39},{8,40},{9,... | collective-permute-start | bytes 1769480 | tf_op jit(solution)/shard_map/ppermute | solution.py:30
  82.0 2.5 %collective-permute-start.9 = (bf16[2,4,24,1536]{3,2,1,0:T(8,128)(2,1)}, bf16[2,4,24,1536]{3,2,1,0:T(8,128)(2,1)}, u32[]{:S(2)}, u32[]{:S(2)}) collective-permute-start(bf16[2,4,24,1536]{3,2,1,0:T(8,128)(2,1)} %get-tuple-element.120), channel_id=1, source_target_pairs={{0,96},{1,97},{2,98},{3,99},{4,100},{5,101},{6,102},{7,103},{8,104... | collective-permute-start | bytes 1769480 | tf_op jit(solution)/shard_map/ppermute | solution.py:30
  84.5 0.6 add_convert_fusion.1
  85.1 1.3 dynamic-slice_bitcast_fusion.4
  86.4 0.9 collective-permute-start.2
  87.3 2.5 %collective-permute-start.3 = (bf16[4,2,24,1536]{3,2,1,0:T(8,128)(2,1)}, bf16[4,2,24,1536]{3,2,1,0:T(8,128)(2,1)}, u32[]{:S(2)}, u32[]{:S(2)}) collective-permute-start(bf16[4,2,24,1536]{3,2,1,0:T(8,128)(2,1)} %get-tuple-element.125), channel_id=1, source_target_pairs={{0,2},{1,3},{2,0},{3,1},{4,6},{5,7},{6,4},{7,5},{8,10},{9,11},{10,... | collective-permute-start | bytes 1769480 | tf_op jit(solution)/shard_map/ppermute | solution.py:30
  89.8 1.3 collective-permute-start.4
  91.1 20.7 %join_halves.1 = (bf16[1024,768]{1,0:T(8,128)(2,1)}, bf16[1024,768]{1,0:T(8,128)(2,1)}, f32[4,768]{1,0:T(4,128)}) custom-call(s32[1,1]{1,0:T(1,128)S(6)} %copy.31.skip_ref, bf16[1024,1536]{1,0:T(8,128)(2,1)} %get-tuple-element.75.act_low_ref, bf16[1024,1536]{1,0:T(8,128)(2,1)} %get-tuple-element.70.act_high_ref, ...), custom_call_target="tpu_custom_call" | custom-call | flops 14000000000 | bytes 30000000 | tf_op jit(solution)/shard_map/join_halves/pallas_call | solution.py:475
  111.8 2.8 %pack_strips.3 = bf16[8,3,32,768]{3,2,1,0:T(8,128)(2,1)} custom-call(s32[1,8,8]{2,1,0:T(8,128)} %table_ref.13, bf16[32,32,768]{2,1,0:T(8,128)(2,1)} %bitcast.70), custom_call_target="tpu_custom_call" | custom-call | tf_op jit(solution)/shard_map/pack_strips/pallas_call | solution.py:60
  114.7 4.3 %all-to-all-start.1 = ((bf16[8,3,32,768]{3,2,1,0:T(8,128)(2,1)}), bf16[8,3,32,768]{3,2,1,0:T(8,128)(2,1)}, u32[]{:S(2)}, u32[]{:S(2)}) async-start(bf16[8,3,32,768]{3,2,1,0:T(8,128)(2,1)} %pack_strips.3), calls=%async_computation.1 | async-start | bytes 2359296 | tf_op jit(solution)/shard_map/all_to_all | solution.py:726
  118.9 1.1 collective-permute-start.10
  120.1 1.7 add_convert_fusion.3
  121.8 0.8 dynamic-slice_bitcast_fusion.9
  122.6 0.5 collective-permute-start.5
  123.1 3.6 %collective-permute-start.6 = (bf16[2,24,1536]{2,1,0:T(8,128)(2,1)}, bf16[2,24,1536]{2,1,0:T(8,128)(2,1)}, u32[]{:S(2)}, u32[]{:S(2)}) collective-permute-start(bf16[2,24,1536]{2,1,0:T(8,128)(2,1)} %get-tuple-element.137), channel_id=1, source_target_pairs={{0,64},{1,65},{2,66},{3,67},{4,68},{5,69},{6,70},{7,71},{8,72},{9,... | collective-permute-start | bytes 442376 | tf_op jit(solution)/shard_map/ppermute | solution.py:30
  126.7 0.6 collective-permute-start.7
  127.3 1.4 convert_add_fusion
  128.8 13.6 %kernel_grad.1 = f32[7,7,768]{2,1,0:T(8,128)} custom-call(s32[1,8,8]{2,1,0:T(8,128)} %table_ref.13, bf16[32,32,768]{2,1,0:T(8,128)(2,1)} %bitcast.69, bf16[8,3,32,768]{3,2,1,0:T(8,128)(2,1)} %copy-done.1, bf16[32,32,768]{2,1,0:T(8,128)(2,1)} %bitcast.71), custom_call_target="tpu_custom_call" | custom-call | flops 14000000000 | bytes 5000000 | tf_op jit(solution)/shard_map/kernel_grad/pallas_call | solution.py:542
  142.3 0.9 reshape.101
  143.4 1.1 add_convert_fusion.4
  144.6 0.1 add_convert_fusion.2
  144.7 0.1 constant_dynamic-slice_fusion
  144.8 0.1 pad_maximum_fusion
  144.9 1.9 %collective-permute-start.11 = (bf16[80,1536]{1,0:T(8,128)(2,1)S(1)}, bf16[80,1536]{1,0:T(8,128)(2,1)S(1)}, u32[]{:S(2)}, u32[]{:S(2)}) collective-permute-start(bf16[80,1536]{1,0:T(8,128)(2,1)S(1)} %get-tuple-element.151), channel_id=1, source_target_pairs={{0,1},{1,0},{2,3},{3,2},{4,5},{5,4},{6,7},{7,6},{8,9},{9,8},{10,11... | collective-permute-start | bytes 737288 | tf_op jit(solution)/shard_map/ppermute | solution.py:30
  146.7 2.7 %collective-permute-start.12 = (bf16[80,1536]{1,0:T(8,128)(2,1)S(1)}, bf16[80,1536]{1,0:T(8,128)(2,1)S(1)}, u32[]{:S(2)}, u32[]{:S(2)}) collective-permute-start(bf16[80,1536]{1,0:T(8,128)(2,1)S(1)} %get-tuple-element.150), channel_id=1, source_target_pairs={{0,2},{1,3},{2,0},{3,1},{4,6},{5,7},{6,4},{7,5},{8,10},{9,11},{10,... | collective-permute-start | bytes 737288 | tf_op jit(solution)/shard_map/ppermute | solution.py:30
  149.4 0.2 collective-permute-start.13
  149.6 5.7 %back_conv.3.refs_3_ = bf16[32,32,768]{2,1,0:T(8,128)(2,1)} custom-call(s32[1,8,8]{2,1,0:T(8,128)} %table_ref.13, bf16[32,32,768]{2,1,0:T(8,128)(2,1)} %bitcast.72, bf16[8,3,32,768]{3,2,1,0:T(8,128)(2,1)} %all-to-all-done.1.refs_0_, f32[1,7,7,768]{3,2,1,0:T(8,128)} %copy.20.weight_ref.refs_1_, bf16[32,32,768]{2,1,0:T(8,128)(2,1)} %bitcast.100), custom_call_target="tpu_custom_call" | custom-call | flops 4666666496 | bytes 1666666 | tf_op jit(solution)/shard_map/back_conv/pallas_call | solution.py:578
  155.3 3.1 %collective-permute-done.12 = bf16[80,1536]{1,0:T(8,128)(2,1)S(1)} collective-permute-done((bf16[80,1536]{1,0:T(8,128)(2,1)S(1)}, bf16[80,1536]{1,0:T(8,128)(2,1)S(1)}, u32[]{:S(2)}, u32[]{:S(2)}) %collective-permute-start.12) | collective-permute-done | bytes 245792 | tf_op jit(solution)/shard_map/ppermute | solution.py:30
  158.4 2.6 %collective-permute-done.13 = bf16[80,1536]{1,0:T(8,128)(2,1)S(1)} collective-permute-done((bf16[80,1536]{1,0:T(8,128)(2,1)S(1)}, bf16[80,1536]{1,0:T(8,128)(2,1)S(1)}, u32[]{:S(2)}, u32[]{:S(2)}) %collective-permute-start.13) | collective-permute-done | bytes 245792 | tf_op jit(solution)/shard_map/ppermute | solution.py:30
  161.1 0.1 fusion.1
  161.5 1.6 collective-permute-start.14
  163.0 2.9 %collective-permute-start.15 = (bf16[56,1536]{1,0:T(8,128)(2,1)S(1)}, bf16[56,1536]{1,0:T(8,128)(2,1)S(1)}, u32[]{:S(2)}, u32[]{:S(2)}) collective-permute-start(bf16[56,1536]{1,0:T(8,128)(2,1)S(1)} %get-tuple-element.147), channel_id=1, source_target_pairs={{0,16},{1,17},{2,18},{3,19},{4,20},{5,21},{6,22},{7,23},{8,24},{9,... | collective-permute-start | bytes 516104 | tf_op jit(solution)/shard_map/ppermute | solution.py:30
  166.0 0.3 collective-permute-start.16
  166.3 5.7 %back_conv.4.refs_3_ = bf16[32,32,768]{2,1,0:T(8,128)(2,1)} custom-call(s32[1,8,8]{2,1,0:T(8,128)} %table_ref.13, bf16[32,32,768]{2,1,0:T(8,128)(2,1)} %bitcast.73, bf16[8,3,32,768]{3,2,1,0:T(8,128)(2,1)} %all-to-all-done.1.refs_0_, f32[1,7,7,768]{3,2,1,0:T(8,128)} %copy.20.weight_ref.refs_1_, ...), custom_call_target="tpu_custom_call", output_to_operand_aliasing={{}: (5, {})} | custom-call | flops 4666666496 | bytes 1666666 | tf_op jit(solution)/shard_map/back_conv/pallas_call | solution.py:578
  172.0 0.5 collective-permute-done.15
  172.5 1.8 collective-permute-done.16
  174.5 0.1 collective-permute-start.17
  174.5 3.8 %collective-permute-start.18 = (bf16[64,768]{1,0:T(8,128)(2,1)S(1)}, bf16[64,768]{1,0:T(8,128)(2,1)S(1)}, u32[]{:S(2)}, u32[]{:S(2)}) collective-permute-start(bf16[64,768]{1,0:T(8,128)(2,1)S(1)} %get-tuple-element.129), channel_id=1, source_target_pairs={{0,64},{1,65},{2,66},{3,67},{4,68},{5,69},{6,70},{7,71},{8,72},{9,... | collective-permute-start | bytes 294920 | tf_op jit(solution)/shard_map/ppermute | solution.py:30
  178.3 0.9 collective-permute-start.19
  179.2 5.7 %back_conv.5 = bf16[32,32,768]{2,1,0:T(8,128)(2,1)} custom-call(s32[1,8,8]{2,1,0:T(8,128)} %table_ref.13, bf16[32,32,768]{2,1,0:T(8,128)(2,1)} %bitcast.74, bf16[8,3,32,768]{3,2,1,0:T(8,128)(2,1)} %all-to-all-done.1.refs_0_, f32[1,7,7,768]{3,2,1,0:T(8,128)} %copy.20.weight_ref.refs_1_, ...), custom_call_target="tpu_custom_call", output_to_operand_aliasing={{}: (5, {})} | custom-call | flops 4666666496 | bytes 1666666 | tf_op jit(solution)/shard_map/back_conv/pallas_call | solution.py:578
  185.0 0.1 collective-permute-start.20
  185.1 0.7 add_bitcast_fusion
  185.8 0.7 collective-permute-done.20
  186.6 0.6 slice_bitcast_fusion
  187.2 0.8 reshape.109
  188.0 0.6 copy.26
  (55 shorter events, 0.8 us)
Async XLA Ops:
  0.6 8.9 %copy-start.2 = (f32[1,7,7,768]{3,0,2,1:T(1,128)S(1)}, f32[1,7,7,768]{3,0,2,1:T(1,128)}, u32[]{:S(2)}) copy-start(f32[1,7,7,768]{3,0,2,1:T(1,128)} %param.16) | copy-start | bytes 451588
  0.6 10.1 %copy-start.4 = (f32[1,3072]{1,0:T(1,128)S(1)}, f32[1,3072]{1,0:T(1,128)}, u32[]{:S(2)}) copy-start(f32[1,3072]{1,0:T(1,128)} %param.20) | copy-start | bytes 36868
  3.5 22.5 %all-to-all-start = ((bf16[8,3,32,768]{3,2,1,0:T(8,128)(2,1)}), bf16[8,3,32,768]{3,2,1,0:T(8,128)(2,1)S(1)}, u32[]{:S(2)}, u32[]{:S(2)}) async-start(bf16[8,3,32,768]{3,2,1,0:T(8,128)(2,1)} %pack_strips.2), calls=%async_computation | async-start | bytes 2359296 | tf_op jit(solution)/shard_map/all_to_all | solution.py:702
  26.0 1.0 copy-start.1
  54.0 18.1 %copy-start.5 = (f32[2,1,768]{2,1,0:T(1,128)S(1)}, f32[2,1,768]{2,1,0:T(1,128)}, u32[]{:S(2)}) copy-start(f32[2,1,768]{2,1,0:T(1,128)} %get-tuple-element.98) | copy-start | bytes 18436
  54.0 18.1 %collective-permute-start = (bf16[2,2,192,1536]{3,2,1,0:T(8,128)(2,1)}, bf16[2,2,192,1536]{3,2,1,0:T(8,128)(2,1)S(1)}, u32[]{:S(2)}, u32[]{:S(2)}) collective-permute-start(bf16[2,2,192,1536]{3,2,1,0:T(8,128)(2,1)} %get-tuple-element.68), channel_id=1, source_target_pairs={{0,8},{1,9},{2,10},{3,11},{4,12},{5,13},{6,14},{7,15},{8,0},{9,1},... | collective-permute-start | bytes 7077896 | tf_op jit(solution)/shard_map/ppermute | solution.py:30
  70.8 5.1 %collective-permute-start.1 = (bf16[2,2,192,1536]{3,2,1,0:T(8,128)(2,1)}, bf16[2,2,192,1536]{3,2,1,0:T(8,128)(2,1)}, u32[]{:S(2)}, u32[]{:S(2)}) collective-permute-start(bf16[2,2,192,1536]{3,2,1,0:T(8,128)(2,1)} %get-tuple-element.74), channel_id=1, source_target_pairs={{0,8},{1,9},{2,10},{3,11},{4,12},{5,13},{6,14},{7,15},{8,0},{9,1},... | collective-permute-start | bytes 7077896 | tf_op jit(solution)/shard_map/ppermute | solution.py:30
  78.8 5.7 %copy-start = (bf16[2,2,192,1536]{3,2,1,0:T(8,128)(2,1)S(1)}, bf16[2,2,192,1536]{3,2,1,0:T(8,128)(2,1)}, u32[]{:S(2)}) copy-start(bf16[2,2,192,1536]{3,2,1,0:T(8,128)(2,1)} %get-tuple-element.71) | copy-start | bytes 7077892
  80.1 38.9 %collective-permute-start.8 = (bf16[2,4,24,1536]{3,2,1,0:T(8,128)(2,1)}, bf16[2,4,24,1536]{3,2,1,0:T(8,128)(2,1)}, u32[]{:S(2)}, u32[]{:S(2)}) collective-permute-start(bf16[2,4,24,1536]{3,2,1,0:T(8,128)(2,1)} %get-tuple-element.122), channel_id=1, source_target_pairs={{0,32},{1,33},{2,34},{3,35},{4,36},{5,37},{6,38},{7,39},{8,40},{9,... | collective-permute-start | bytes 1769480 | tf_op jit(solution)/shard_map/ppermute | solution.py:30
  82.0 38.1 %collective-permute-start.9 = (bf16[2,4,24,1536]{3,2,1,0:T(8,128)(2,1)}, bf16[2,4,24,1536]{3,2,1,0:T(8,128)(2,1)}, u32[]{:S(2)}, u32[]{:S(2)}) collective-permute-start(bf16[2,4,24,1536]{3,2,1,0:T(8,128)(2,1)} %get-tuple-element.120), channel_id=1, source_target_pairs={{0,96},{1,97},{2,98},{3,99},{4,100},{5,101},{6,102},{7,103},{8,104... | collective-permute-start | bytes 1769480 | tf_op jit(solution)/shard_map/ppermute | solution.py:30
  86.4 33.7 %collective-permute-start.2 = (bf16[4,2,24,1536]{3,2,1,0:T(8,128)(2,1)}, bf16[4,2,24,1536]{3,2,1,0:T(8,128)(2,1)}, u32[]{:S(2)}, u32[]{:S(2)}) collective-permute-start(bf16[4,2,24,1536]{3,2,1,0:T(8,128)(2,1)} %get-tuple-element.126), channel_id=1, source_target_pairs={{0,1},{1,0},{2,3},{3,2},{4,5},{5,4},{6,7},{7,6},{8,9},{9,8},{10,11... | collective-permute-start | bytes 1769480 | tf_op jit(solution)/shard_map/ppermute | solution.py:30
  87.3 32.8 %collective-permute-start.3 = (bf16[4,2,24,1536]{3,2,1,0:T(8,128)(2,1)}, bf16[4,2,24,1536]{3,2,1,0:T(8,128)(2,1)}, u32[]{:S(2)}, u32[]{:S(2)}) collective-permute-start(bf16[4,2,24,1536]{3,2,1,0:T(8,128)(2,1)} %get-tuple-element.125), channel_id=1, source_target_pairs={{0,2},{1,3},{2,0},{3,1},{4,6},{5,7},{6,4},{7,5},{8,10},{9,11},{10,... | collective-permute-start | bytes 1769480 | tf_op jit(solution)/shard_map/ppermute | solution.py:30
  89.8 30.3 %collective-permute-start.4 = (bf16[4,2,24,1536]{3,2,1,0:T(8,128)(2,1)S(1)}, bf16[4,2,24,1536]{3,2,1,0:T(8,128)(2,1)}, u32[]{:S(2)}, u32[]{:S(2)}) collective-permute-start(bf16[4,2,24,1536]{3,2,1,0:T(8,128)(2,1)S(1)} %get-tuple-element.124), channel_id=1, source_target_pairs={{0,3},{1,2},{2,1},{3,0},{4,7},{5,6},{6,5},{7,4},{8,11},{9,10},{10,... | collective-permute-start | bytes 1769480 | tf_op jit(solution)/shard_map/ppermute | solution.py:30
  114.7 35.0 %all-to-all-start.1 = ((bf16[8,3,32,768]{3,2,1,0:T(8,128)(2,1)}), bf16[8,3,32,768]{3,2,1,0:T(8,128)(2,1)}, u32[]{:S(2)}, u32[]{:S(2)}) async-start(bf16[8,3,32,768]{3,2,1,0:T(8,128)(2,1)} %pack_strips.3), calls=%async_computation.1 | async-start | bytes 2359296 | tf_op jit(solution)/shard_map/all_to_all | solution.py:726
  118.9 25.6 %collective-permute-start.10 = (bf16[2,4,24,1536]{3,2,1,0:T(8,128)(2,1)S(1)}, bf16[2,4,24,1536]{3,2,1,0:T(8,128)(2,1)S(1)}, u32[]{:S(2)}, u32[]{:S(2)}) collective-permute-start(bf16[2,4,24,1536]{3,2,1,0:T(8,128)(2,1)S(1)} %get-tuple-element.94), channel_id=1, source_target_pairs={{0,64},{1,65},{2,66},{3,67},{4,68},{5,69},{6,70},{7,71},{8,72},{9,... | collective-permute-start | bytes 1769480 | tf_op jit(solution)/shard_map/ppermute | solution.py:30
  122.6 20.8 %collective-permute-start.5 = (bf16[2,24,1536]{2,1,0:T(8,128)(2,1)}, bf16[2,24,1536]{2,1,0:T(8,128)(2,1)}, u32[]{:S(2)}, u32[]{:S(2)}) collective-permute-start(bf16[2,24,1536]{2,1,0:T(8,128)(2,1)} %get-tuple-element.138), channel_id=1, source_target_pairs={{0,32},{1,33},{2,34},{3,35},{4,36},{5,37},{6,38},{7,39},{8,40},{9,... | collective-permute-start | bytes 442376 | tf_op jit(solution)/shard_map/ppermute | solution.py:30
  123.1 20.3 %collective-permute-start.6 = (bf16[2,24,1536]{2,1,0:T(8,128)(2,1)}, bf16[2,24,1536]{2,1,0:T(8,128)(2,1)}, u32[]{:S(2)}, u32[]{:S(2)}) collective-permute-start(bf16[2,24,1536]{2,1,0:T(8,128)(2,1)} %get-tuple-element.137), channel_id=1, source_target_pairs={{0,64},{1,65},{2,66},{3,67},{4,68},{5,69},{6,70},{7,71},{8,72},{9,... | collective-permute-start | bytes 442376 | tf_op jit(solution)/shard_map/ppermute | solution.py:30
  126.7 16.7 %collective-permute-start.7 = (bf16[2,24,1536]{2,1,0:T(8,128)(2,1)}, bf16[2,24,1536]{2,1,0:T(8,128)(2,1)}, u32[]{:S(2)}, u32[]{:S(2)}) collective-permute-start(bf16[2,24,1536]{2,1,0:T(8,128)(2,1)} %get-tuple-element.136), channel_id=1, source_target_pairs={{0,96},{1,97},{2,98},{3,99},{4,100},{5,101},{6,102},{7,103},{8,104... | collective-permute-start | bytes 442376 | tf_op jit(solution)/shard_map/ppermute | solution.py:30
  128.8 14.5 %copy-start.3 = (f32[4,768]{1,0:T(4,128)S(1)}, f32[4,768]{1,0:T(4,128)}, u32[]{:S(2)}) copy-start(f32[4,768]{1,0:T(4,128)} %get-tuple-element.97) | copy-start | bytes 36868
  144.9 10.5 %collective-permute-start.11 = (bf16[80,1536]{1,0:T(8,128)(2,1)S(1)}, bf16[80,1536]{1,0:T(8,128)(2,1)S(1)}, u32[]{:S(2)}, u32[]{:S(2)}) collective-permute-start(bf16[80,1536]{1,0:T(8,128)(2,1)S(1)} %get-tuple-element.151), channel_id=1, source_target_pairs={{0,1},{1,0},{2,3},{3,2},{4,5},{5,4},{6,7},{7,6},{8,9},{9,8},{10,11... | collective-permute-start | bytes 737288 | tf_op jit(solution)/shard_map/ppermute | solution.py:30
  146.7 11.7 %collective-permute-start.12 = (bf16[80,1536]{1,0:T(8,128)(2,1)S(1)}, bf16[80,1536]{1,0:T(8,128)(2,1)S(1)}, u32[]{:S(2)}, u32[]{:S(2)}) collective-permute-start(bf16[80,1536]{1,0:T(8,128)(2,1)S(1)} %get-tuple-element.150), channel_id=1, source_target_pairs={{0,2},{1,3},{2,0},{3,1},{4,6},{5,7},{6,4},{7,5},{8,10},{9,11},{10,... | collective-permute-start | bytes 737288 | tf_op jit(solution)/shard_map/ppermute | solution.py:30
  149.4 11.6 %collective-permute-start.13 = (bf16[80,1536]{1,0:T(8,128)(2,1)S(1)}, bf16[80,1536]{1,0:T(8,128)(2,1)S(1)}, u32[]{:S(2)}, u32[]{:S(2)}) collective-permute-start(bf16[80,1536]{1,0:T(8,128)(2,1)S(1)} %get-tuple-element.149), channel_id=1, source_target_pairs={{0,3},{1,2},{2,1},{3,0},{4,7},{5,6},{6,5},{7,4},{8,11},{9,10},{10,... | collective-permute-start | bytes 737288 | tf_op jit(solution)/shard_map/ppermute | solution.py:30
  161.5 10.5 %collective-permute-start.14 = (bf16[56,1536]{1,0:T(8,128)(2,1)S(1)}, bf16[56,1536]{1,0:T(8,128)(2,1)S(1)}, u32[]{:S(2)}, u32[]{:S(2)}) collective-permute-start(bf16[56,1536]{1,0:T(8,128)(2,1)S(1)} %get-tuple-element.148), channel_id=1, source_target_pairs={{0,4},{1,5},{2,6},{3,7},{4,0},{5,1},{6,2},{7,3},{8,12},{9,13},{10,... | collective-permute-start | bytes 516104 | tf_op jit(solution)/shard_map/ppermute | solution.py:30
  163.0 9.4 %collective-permute-start.15 = (bf16[56,1536]{1,0:T(8,128)(2,1)S(1)}, bf16[56,1536]{1,0:T(8,128)(2,1)S(1)}, u32[]{:S(2)}, u32[]{:S(2)}) collective-permute-start(bf16[56,1536]{1,0:T(8,128)(2,1)S(1)} %get-tuple-element.147), channel_id=1, source_target_pairs={{0,16},{1,17},{2,18},{3,19},{4,20},{5,21},{6,22},{7,23},{8,24},{9,... | collective-permute-start | bytes 516104 | tf_op jit(solution)/shard_map/ppermute | solution.py:30
  166.0 8.3 %collective-permute-start.16 = (bf16[56,1536]{1,0:T(8,128)(2,1)S(1)}, bf16[56,1536]{1,0:T(8,128)(2,1)S(1)}, u32[]{:S(2)}, u32[]{:S(2)}) collective-permute-start(bf16[56,1536]{1,0:T(8,128)(2,1)S(1)} %get-tuple-element.146), channel_id=1, source_target_pairs={{0,20},{1,21},{2,22},{3,23},{4,16},{5,17},{6,18},{7,19},{8,28},{9,... | collective-permute-start | bytes 516104 | tf_op jit(solution)/shard_map/ppermute | solution.py:30
  174.5 10.5 %collective-permute-start.17 = (bf16[64,768]{1,0:T(8,128)(2,1)S(1)}, bf16[64,768]{1,0:T(8,128)(2,1)S(1)}, u32[]{:S(2)}, u32[]{:S(2)}) collective-permute-start(bf16[64,768]{1,0:T(8,128)(2,1)S(1)} %get-tuple-element.129), channel_id=1, source_target_pairs={{0,32},{1,33},{2,34},{3,35},{4,36},{5,37},{6,38},{7,39},{8,40},{9,... | collective-permute-start | bytes 294920 | tf_op jit(solution)/shard_map/ppermute | solution.py:30
  174.5 10.4 %collective-permute-start.18 = (bf16[64,768]{1,0:T(8,128)(2,1)S(1)}, bf16[64,768]{1,0:T(8,128)(2,1)S(1)}, u32[]{:S(2)}, u32[]{:S(2)}) collective-permute-start(bf16[64,768]{1,0:T(8,128)(2,1)S(1)} %get-tuple-element.129), channel_id=1, source_target_pairs={{0,64},{1,65},{2,66},{3,67},{4,68},{5,69},{6,70},{7,71},{8,72},{9,... | collective-permute-start | bytes 294920 | tf_op jit(solution)/shard_map/ppermute | solution.py:30
  178.3 6.6 %collective-permute-start.19 = (bf16[64,768]{1,0:T(8,128)(2,1)S(1)}, bf16[64,768]{1,0:T(8,128)(2,1)S(1)}, u32[]{:S(2)}, u32[]{:S(2)}) collective-permute-start(bf16[64,768]{1,0:T(8,128)(2,1)S(1)} %get-tuple-element.129), channel_id=1, source_target_pairs={{0,96},{1,97},{2,98},{3,99},{4,100},{5,101},{6,102},{7,103},{8,104... | collective-permute-start | bytes 294920 | tf_op jit(solution)/shard_map/ppermute | solution.py:30
  185.0 1.5 collective-permute-start.20

commit v4 on v3

--- a/solution.py
+++ b/solution.py
@@ -652,7 +652,7 @@
 
 
 def gate(values, ready):
-    return list(lax.optimization_barrier((*values, ready))[: len(values)])
+    return list(lax.optimization_barrier((*values, ready)))[: len(values)]
 
 
 def after(value, *others):
@@ -714,7 +714,7 @@
     grid = (4, 2, 4, rows, width)
     received_high = swap(theirs_high, 8)
     low_x = x_parts(fold(gate([mine_low, received_low], act_high), bf16).reshape(grid))
-    high_z = z_parts(fold([mine_high, received_high], bf16).reshape(grid))
+    high_z = z_parts(fold(gate([mine_high, received_high], tuple(low_x)), bf16).reshape(grid))
     got_high = [swap(high_z[1], 32), swap(high_z[3], 96)]
     out, conv_grad, channel_sums = join(
         skip_flags, (after(act_low, *low_x, *high_z), act_high), (pre_low, pre_high), up_weight[0], down_weight[0],

time: 190 us -> 186 us (0.979)
  waiting for transfers between devices: 13.7 us -> 9.8 us
    ppermute x21, waiting for transfers between devices: 12.4 us -> 8.49 us  [swap(): return lax.ppermute(value, both_axes, pairs)]
    unnamed x16 -> x20, local copies, waits for them, and re-layouts: 3.47 us -> 4.3 us
  transfers between devices with their start and end apart: 23 -> 23, of which waited for: 7 -> 6; matrix products, arithmetic and copies ran while one was open for 7% -> 8% of each run, Pallas kernels for 44% -> 45%
where the time goes in v4:
time: 186 us; the launch traced here: 184 us
  Pallas kernels  113 us (61%)
  starting transfers between devices  39.9 us (21%)
  other arithmetic  10.5 us (6%)
  waiting for transfers between devices  9.8 us (5%)
  local copies, waits for them, and re-layouts  9.46 us (5%)
    pallas_call x2, Pallas kernels, hidden_half(): pl.pallas_call(hidden_kernel, grid=(steps,), out_shape=[wide_shape, wide_...  32.9 us
    ppermute x21, starting transfers between devices, swap(): return lax.ppermute(value, both_axes, pairs)  30.3 us
    pallas_call x1, Pallas kernels, join(): pl.pallas_call(join_kernel, grid=(4,), out_shape=[pixel, pixel, jax.Shape...  20.7 us
    pallas_call x3, Pallas kernels, back_conv(): pl.pallas_call(back_kernel, grid=(steps,), out_shape=jax.ShapeDtypeStruct...  17.1 us
    pallas_call x1, Pallas kernels, kernel_grad(): pl.pallas_call(kernel_grad_kernel, grid=(channels // lanes,), out_shape=j...  13.6 us
    pallas_call x1, Pallas kernels, conv_inner(): pl.pallas_call(inner_kernel, grid=(blocks,), out_shape=jax.ShapeDtypeStru...  12.6 us
    pallas_call x1, Pallas kernels, conv_norm(): pl.pallas_call(norm_kernel, grid=(blocks,), out_shape=[jax.ShapeDtypeStru...  10.6 us
    ppermute x21, waiting for transfers between devices, swap(): return lax.ppermute(value, both_axes, pairs)  8.49 us
  transfers between devices with their start and end apart: 23, of which 6 were waited for; matrix products, arithmetic and copies ran while one was open for 8% of the time, Pallas kernels for 45%

profile of v4, /device:TPU:0, one launch (start us, length us, event | category | flops | bytes accessed | tf_op | source)
XLA Modules:
  0.0 184.5 jit_solution(7827226480143597948)
XLA Ops:
  0.7 2.9 %pack_strips.2 = bf16[8,3,32,768]{3,2,1,0:T(8,128)(2,1)} custom-call(s32[1,8,8]{2,1,0:T(8,128)} %table_ref.13, bf16[32,32,768]{2,1,0:T(8,128)(2,1)} %bitcast.66), custom_call_target="tpu_custom_call" | custom-call | tf_op jit(solution)/shard_map/pack_strips/pallas_call | solution.py:60
  3.5 5.4 %all-to-all-start = ((bf16[8,3,32,768]{3,2,1,0:T(8,128)(2,1)}), bf16[8,3,32,768]{3,2,1,0:T(8,128)(2,1)S(1)}, u32[]{:S(2)}, u32[]{:S(2)}) async-start(bf16[8,3,32,768]{3,2,1,0:T(8,128)(2,1)} %pack_strips.2), calls=%async_computation | async-start | bytes 2359296 | tf_op jit(solution)/shard_map/all_to_all | solution.py:702
  9.6 0.7 copy.20.weight_ref.refs_1_
  10.3 0.5 broadcast.28
  10.8 0.7 reduce.5
  11.5 0.6 reshape.96.up_bias_ref
  12.1 12.6 %conv_inner.1.part_ref = f32[6,32,32,128]{3,2,1,0:T(8,128)} custom-call(bf16[32,32,768]{2,1,0:T(8,128)(2,1)} %bitcast.67, f32[1,7,7,768]{3,2,1,0:T(8,128)} %copy.20.weight_ref.refs_1_), custom_call_target="tpu_custom_call" | custom-call | flops 14000000000 | bytes 5000000 | tf_op jit(solution)/shard_map/conv_inner/pallas_call | solution.py:144
  24.7 1.3 all-to-all-done.strip_ref.refs_0_
  26.0 1.0 copy-done.1
  27.0 10.6 %conv_norm.1 = (f32[1024,768]{1,0:T(8,128)}, f32[1024,1]{1,0:T(8,128)}, bf16[1024,768]{1,0:T(8,128)(2,1)}) custom-call(s32[1,8,8]{2,1,0:T(8,128)} %table_ref.13, f32[6,32,32,128]{3,2,1,0:T(8,128)} %conv_inner.1.part_ref, bf16[8,3,32,768]{3,2,1,0:T(8,128)(2,1)} %copy-done.1, f32[1,7,7,768]{3,2,1,0:T(8,128)} %copy.20.weight_ref.refs_1_, f32[1,768]{1,0:T(1,128)} %gain_ref.3, ...), custom_call_target="tpu_custom_call" | custom-call | flops 7000000000 | bytes 10000000 | tf_op jit(solution)/shard_map/conv_norm/pallas_call | solution.py:261
  37.6 16.4 %hidden_half.2 = (bf16[1024,1536]{1,0:T(8,128)(2,1)}, bf16[1024,1536]{1,0:T(8,128)(2,1)}, bf16[2,2,192,1536]{3,2,1,0:T(8,128)(2,1)}, bf16[2,2,192,1536]{3,2,1,0:T(8,128)(2,1)}, f32[2,1,768]{2,1,0:T(1,128)}) custom-call(s32[1,1]{1,0:T(1,128)S(6)} %copy.31.skip_ref, bf16[1024,768]{1,0:T(8,128)(2,1)} %get-tuple-element.71.normed_ref, ...), custom_call_target="tpu_custom_call" | custom-call | flops 14000000000 | bytes 20000000 | tf_op jit(solution)/shard_map/hidden_half/pallas_call | solution.py:375
  54.0 0.0 copy-start.7
  54.0 0.3 collective-permute-start
  54.3 16.4 %hidden_half.3 = (bf16[1024,1536]{1,0:T(8,128)(2,1)}, bf16[1024,1536]{1,0:T(8,128)(2,1)}, bf16[2,2,192,1536]{3,2,1,0:T(8,128)(2,1)}, bf16[2,2,192,1536]{3,2,1,0:T(8,128)(2,1)}, f32[2,1,768]{2,1,0:T(1,128)}) custom-call(s32[1,1]{1,0:T(1,128)S(6)} %copy.31.skip_ref, bf16[1024,768]{1,0:T(8,128)(2,1)} %get-tuple-element.71.normed_ref, ...), custom_call_target="tpu_custom_call" | custom-call | flops 14000000000 | bytes 20000000 | tf_op jit(solution)/shard_map/hidden_half/pallas_call | solution.py:375
  70.7 0.5 collective-permute-start.1
  71.3 0.7 reduce.2
  72.1 3.0 %add_convert_fusion.1 = bf16[2,2,192,1536]{3,2,1,0:T(8,128)(2,1)S(1)} fusion(bf16[2,2,192,1536]{3,2,1,0:T(8,128)(2,1)} %collective-permute-done, bf16[2,2,192,1536]{3,2,1,0:T(8,128)(2,1)} %get-tuple-element.73), kind=kLoop, calls=%fused_computation.1 | loop fusion | flops 4718592 | bytes 7077888 | tf_op jit(solution)/shard_map/convert_element_type | solution.py:615
  75.1 1.3 dynamic-slice_bitcast_fusion.4
  76.4 0.9 collective-permute-start.2
  77.2 2.5 %collective-permute-start.3 = (bf16[4,2,24,1536]{3,2,1,0:T(8,128)(2,1)}, bf16[4,2,24,1536]{3,2,1,0:T(8,128)(2,1)}, u32[]{:S(2)}, u32[]{:S(2)}) collective-permute-start(bf16[4,2,24,1536]{3,2,1,0:T(8,128)(2,1)} %get-tuple-element.129), channel_id=1, source_target_pairs={{0,2},{1,3},{2,0},{3,1},{4,6},{5,7},{6,4},{7,5},{8,10},{9,11},{10,... | collective-permute-start | bytes 1769480 | tf_op jit(solution)/shard_map/ppermute | solution.py:30
  79.8 1.3 collective-permute-start.4
  81.1 0.6 add_convert_fusion
  81.7 1.1 dynamic-slice_bitcast_fusion
  82.7 1.9 %collective-permute-start.8 = (bf16[2,4,24,1536]{3,2,1,0:T(8,128)(2,1)}, bf16[2,4,24,1536]{3,2,1,0:T(8,128)(2,1)S(1)}, u32[]{:S(2)}, u32[]{:S(2)}) collective-permute-start(bf16[2,4,24,1536]{3,2,1,0:T(8,128)(2,1)} %get-tuple-element.126), channel_id=1, source_target_pairs={{0,32},{1,33},{2,34},{3,35},{4,36},{5,37},{6,38},{7,39},{8,40},{9,... | collective-permute-start | bytes 1769480 | tf_op jit(solution)/shard_map/ppermute | solution.py:30
  84.7 2.5 %collective-permute-start.9 = (bf16[2,4,24,1536]{3,2,1,0:T(8,128)(2,1)S(1)}, bf16[2,4,24,1536]{3,2,1,0:T(8,128)(2,1)S(1)}, u32[]{:S(2)}, u32[]{:S(2)}) collective-permute-start(bf16[2,4,24,1536]{3,2,1,0:T(8,128)(2,1)S(1)} %get-tuple-element.124), channel_id=1, source_target_pairs={{0,96},{1,97},{2,98},{3,99},{4,100},{5,101},{6,102},{7,103},{8,104... | collective-permute-start | bytes 1769480 | tf_op jit(solution)/shard_map/ppermute | solution.py:30
  87.2 20.7 %join_halves.1 = (bf16[1024,768]{1,0:T(8,128)(2,1)}, bf16[1024,768]{1,0:T(8,128)(2,1)}, f32[4,768]{1,0:T(4,128)}) custom-call(s32[1,1]{1,0:T(1,128)S(6)} %copy.31.skip_ref, bf16[1024,1536]{1,0:T(8,128)(2,1)} %get-tuple-element.79.act_low_ref, bf16[1024,1536]{1,0:T(8,128)(2,1)} %get-tuple-element.72.act_high_ref, ...), custom_call_target="tpu_custom_call" | custom-call | flops 14000000000 | bytes 30000000 | tf_op jit(solution)/shard_map/join_halves/pallas_call | solution.py:475
  107.9 2.8 %pack_strips.3 = bf16[8,3,32,768]{3,2,1,0:T(8,128)(2,1)} custom-call(s32[1,8,8]{2,1,0:T(8,128)} %table_ref.13, bf16[32,32,768]{2,1,0:T(8,128)(2,1)} %bitcast.70), custom_call_target="tpu_custom_call" | custom-call | tf_op jit(solution)/shard_map/pack_strips/pallas_call | solution.py:60
  110.7 4.3 %all-to-all-start.1 = ((bf16[8,3,32,768]{3,2,1,0:T(8,128)(2,1)}), bf16[8,3,32,768]{3,2,1,0:T(8,128)(2,1)}, u32[]{:S(2)}, u32[]{:S(2)}) async-start(bf16[8,3,32,768]{3,2,1,0:T(8,128)(2,1)} %pack_strips.3), calls=%async_computation.1 | async-start | bytes 2359296 | tf_op jit(solution)/shard_map/all_to_all | solution.py:726
  115.0 1.1 collective-permute-start.10
  116.2 0.8 copy-done.2
  117.0 1.8 add_convert_fusion.3
  118.8 0.1 dynamic-slice_bitcast_fusion.9
  118.8 0.6 collective-permute-start.5
  119.4 3.6 %collective-permute-start.6 = (bf16[2,24,1536]{2,1,0:T(8,128)(2,1)S(1)}, bf16[2,24,1536]{2,1,0:T(8,128)(2,1)}, u32[]{:S(2)}, u32[]{:S(2)}) collective-permute-start(bf16[2,24,1536]{2,1,0:T(8,128)(2,1)S(1)} %get-tuple-element.141), channel_id=1, source_target_pairs={{0,64},{1,65},{2,66},{3,67},{4,68},{5,69},{6,70},{7,71},{8,72},{9,... | collective-permute-start | bytes 442376 | tf_op jit(solution)/shard_map/ppermute | solution.py:30
  123.0 0.6 collective-permute-start.7
  123.6 0.2 convert_add_fusion
  123.8 13.6 %kernel_grad.1 = f32[7,7,768]{2,1,0:T(8,128)} custom-call(s32[1,8,8]{2,1,0:T(8,128)} %table_ref.13, bf16[32,32,768]{2,1,0:T(8,128)(2,1)} %bitcast.69, bf16[8,3,32,768]{3,2,1,0:T(8,128)(2,1)} %copy-done.1, bf16[32,32,768]{2,1,0:T(8,128)(2,1)} %bitcast.71), custom_call_target="tpu_custom_call" | custom-call | flops 14000000000 | bytes 5000000 | tf_op jit(solution)/shard_map/kernel_grad/pallas_call | solution.py:542
  137.4 0.9 reshape.101
  138.5 1.1 add_convert_fusion.4
  139.7 1.2 add_convert_fusion.2
  140.8 0.1 constant_dynamic-slice_fusion
  140.9 0.1 pad_maximum_fusion
  141.0 1.9 %collective-permute-start.11 = (bf16[80,1536]{1,0:T(8,128)(2,1)S(1)}, bf16[80,1536]{1,0:T(8,128)(2,1)S(1)}, u32[]{:S(2)}, u32[]{:S(2)}) collective-permute-start(bf16[80,1536]{1,0:T(8,128)(2,1)S(1)} %get-tuple-element.155), channel_id=1, source_target_pairs={{0,1},{1,0},{2,3},{3,2},{4,5},{5,4},{6,7},{7,6},{8,9},{9,8},{10,11... | collective-permute-start | bytes 737288 | tf_op jit(solution)/shard_map/ppermute | solution.py:30
  142.9 2.7 %collective-permute-start.12 = (bf16[80,1536]{1,0:T(8,128)(2,1)S(1)}, bf16[80,1536]{1,0:T(8,128)(2,1)S(1)}, u32[]{:S(2)}, u32[]{:S(2)}) collective-permute-start(bf16[80,1536]{1,0:T(8,128)(2,1)S(1)} %get-tuple-element.154), channel_id=1, source_target_pairs={{0,2},{1,3},{2,0},{3,1},{4,6},{5,7},{6,4},{7,5},{8,10},{9,11},{10,... | collective-permute-start | bytes 737288 | tf_op jit(solution)/shard_map/ppermute | solution.py:30
  145.6 0.2 collective-permute-start.13
  145.8 5.7 %back_conv.3.refs_3_ = bf16[32,32,768]{2,1,0:T(8,128)(2,1)} custom-call(s32[1,8,8]{2,1,0:T(8,128)} %table_ref.13, bf16[32,32,768]{2,1,0:T(8,128)(2,1)} %bitcast.72, bf16[8,3,32,768]{3,2,1,0:T(8,128)(2,1)} %all-to-all-done.1.refs_0_, f32[1,7,7,768]{3,2,1,0:T(8,128)} %copy.20.weight_ref.refs_1_, bf16[32,32,768]{2,1,0:T(8,128)(2,1)} %bitcast.100), custom_call_target="tpu_custom_call" | custom-call | flops 4666666496 | bytes 1666666 | tf_op jit(solution)/shard_map/back_conv/pallas_call | solution.py:578
  151.5 2.9 %collective-permute-done.12 = bf16[80,1536]{1,0:T(8,128)(2,1)S(1)} collective-permute-done((bf16[80,1536]{1,0:T(8,128)(2,1)S(1)}, bf16[80,1536]{1,0:T(8,128)(2,1)S(1)}, u32[]{:S(2)}, u32[]{:S(2)}) %collective-permute-start.12) | collective-permute-done | bytes 245792 | tf_op jit(solution)/shard_map/ppermute | solution.py:30
  154.3 2.6 %collective-permute-done.13 = bf16[80,1536]{1,0:T(8,128)(2,1)S(1)} collective-permute-done((bf16[80,1536]{1,0:T(8,128)(2,1)S(1)}, bf16[80,1536]{1,0:T(8,128)(2,1)S(1)}, u32[]{:S(2)}, u32[]{:S(2)}) %collective-permute-start.13) | collective-permute-done | bytes 245792 | tf_op jit(solution)/shard_map/ppermute | solution.py:30
  157.4 1.6 collective-permute-start.14
  158.9 2.9 %collective-permute-start.15 = (bf16[56,1536]{1,0:T(8,128)(2,1)S(1)}, bf16[56,1536]{1,0:T(8,128)(2,1)S(1)}, u32[]{:S(2)}, u32[]{:S(2)}) collective-permute-start(bf16[56,1536]{1,0:T(8,128)(2,1)S(1)} %get-tuple-element.151), channel_id=1, source_target_pairs={{0,16},{1,17},{2,18},{3,19},{4,20},{5,21},{6,22},{7,23},{8,24},{9,... | collective-permute-start | bytes 516104 | tf_op jit(solution)/shard_map/ppermute | solution.py:30
  161.8 0.3 collective-permute-start.16
  162.2 5.7 %back_conv.4.refs_3_ = bf16[32,32,768]{2,1,0:T(8,128)(2,1)} custom-call(s32[1,8,8]{2,1,0:T(8,128)} %table_ref.13, bf16[32,32,768]{2,1,0:T(8,128)(2,1)} %bitcast.73, bf16[8,3,32,768]{3,2,1,0:T(8,128)(2,1)} %all-to-all-done.1.refs_0_, f32[1,7,7,768]{3,2,1,0:T(8,128)} %copy.20.weight_ref.refs_1_, ...), custom_call_target="tpu_custom_call", output_to_operand_aliasing={{}: (5, {})} | custom-call | flops 4666666496 | bytes 1666666 | tf_op jit(solution)/shard_map/back_conv/pallas_call | solution.py:578
  167.9 0.5 collective-permute-done.15
  168.4 1.8 collective-permute-done.16
  170.3 0.1 collective-permute-start.17
  170.4 3.8 %collective-permute-start.18 = (bf16[64,768]{1,0:T(8,128)(2,1)S(1)}, bf16[64,768]{1,0:T(8,128)(2,1)S(1)}, u32[]{:S(2)}, u32[]{:S(2)}) collective-permute-start(bf16[64,768]{1,0:T(8,128)(2,1)S(1)} %get-tuple-element.133), channel_id=1, source_target_pairs={{0,64},{1,65},{2,66},{3,67},{4,68},{5,69},{6,70},{7,71},{8,72},{9,... | collective-permute-start | bytes 294920 | tf_op jit(solution)/shard_map/ppermute | solution.py:30
  174.2 0.9 collective-permute-start.19
  175.1 5.7 %back_conv.5 = bf16[32,32,768]{2,1,0:T(8,128)(2,1)} custom-call(s32[1,8,8]{2,1,0:T(8,128)} %table_ref.13, bf16[32,32,768]{2,1,0:T(8,128)(2,1)} %bitcast.74, bf16[8,3,32,768]{3,2,1,0:T(8,128)(2,1)} %all-to-all-done.1.refs_0_, f32[1,7,7,768]{3,2,1,0:T(8,128)} %copy.20.weight_ref.refs_1_, ...), custom_call_target="tpu_custom_call", output_to_operand_aliasing={{}: (5, {})} | custom-call | flops 4666666496 | bytes 1666666 | tf_op jit(solution)/shard_map/back_conv/pallas_call | solution.py:578
  180.9 0.1 collective-permute-start.20
  181.0 0.7 add_bitcast_fusion
  181.7 0.7 collective-permute-done.20
  182.4 0.6 slice_bitcast_fusion
  183.1 0.8 reshape.109
  183.9 0.6 copy.26
  (59 shorter events, 0.9 us)
Async XLA Ops:
  0.6 8.9 %copy-start.4 = (f32[1,7,7,768]{3,0,2,1:T(1,128)S(1)}, f32[1,7,7,768]{3,0,2,1:T(1,128)}, u32[]{:S(2)}) copy-start(f32[1,7,7,768]{3,0,2,1:T(1,128)} %param.16) | copy-start | bytes 451588
  0.6 10.1 %copy-start.6 = (f32[1,3072]{1,0:T(1,128)S(1)}, f32[1,3072]{1,0:T(1,128)}, u32[]{:S(2)}) copy-start(f32[1,3072]{1,0:T(1,128)} %param.20) | copy-start | bytes 36868
  3.5 22.5 %all-to-all-start = ((bf16[8,3,32,768]{3,2,1,0:T(8,128)(2,1)}), bf16[8,3,32,768]{3,2,1,0:T(8,128)(2,1)S(1)}, u32[]{:S(2)}, u32[]{:S(2)}) async-start(bf16[8,3,32,768]{3,2,1,0:T(8,128)(2,1)} %pack_strips.2), calls=%async_computation | async-start | bytes 2359296 | tf_op jit(solution)/shard_map/all_to_all | solution.py:702
  26.0 1.0 copy-start.1
  54.0 18.0 %copy-start.7 = (f32[2,1,768]{2,1,0:T(1,128)S(1)}, f32[2,1,768]{2,1,0:T(1,128)}, u32[]{:S(2)}) copy-start(f32[2,1,768]{2,1,0:T(1,128)} %get-tuple-element.102) | copy-start | bytes 18436
  54.0 18.0 %collective-permute-start = (bf16[2,2,192,1536]{3,2,1,0:T(8,128)(2,1)}, bf16[2,2,192,1536]{3,2,1,0:T(8,128)(2,1)}, u32[]{:S(2)}, u32[]{:S(2)}) collective-permute-start(bf16[2,2,192,1536]{3,2,1,0:T(8,128)(2,1)} %get-tuple-element.70), channel_id=1, source_target_pairs={{0,8},{1,9},{2,10},{3,11},{4,12},{5,13},{6,14},{7,15},{8,0},{9,1},... | collective-permute-start | bytes 7077896 | tf_op jit(solution)/shard_map/ppermute | solution.py:30
  70.7 10.3 %collective-permute-start.1 = (bf16[2,2,192,1536]{3,2,1,0:T(8,128)(2,1)}, bf16[2,2,192,1536]{3,2,1,0:T(8,128)(2,1)S(1)}, u32[]{:S(2)}, u32[]{:S(2)}) collective-permute-start(bf16[2,2,192,1536]{3,2,1,0:T(8,128)(2,1)} %get-tuple-element.76), channel_id=1, source_target_pairs={{0,8},{1,9},{2,10},{3,11},{4,12},{5,13},{6,14},{7,15},{8,0},{9,1},... | collective-permute-start | bytes 7077896 | tf_op jit(solution)/shard_map/ppermute | solution.py:30
  75.1 6.0 %copy-start = (bf16[2,2,192,1536]{3,2,1,0:T(8,128)(2,1)S(1)}, bf16[2,2,192,1536]{3,2,1,0:T(8,128)(2,1)}, u32[]{:S(2)}) copy-start(bf16[2,2,192,1536]{3,2,1,0:T(8,128)(2,1)} %get-tuple-element.77) | copy-start | bytes 7077892
  76.4 39.8 %collective-permute-start.2 = (bf16[4,2,24,1536]{3,2,1,0:T(8,128)(2,1)}, bf16[4,2,24,1536]{3,2,1,0:T(8,128)(2,1)}, u32[]{:S(2)}, u32[]{:S(2)}) collective-permute-start(bf16[4,2,24,1536]{3,2,1,0:T(8,128)(2,1)} %get-tuple-element.130), channel_id=1, source_target_pairs={{0,1},{1,0},{2,3},{3,2},{4,5},{5,4},{6,7},{7,6},{8,9},{9,8},{10,11... | collective-permute-start | bytes 1769480 | tf_op jit(solution)/shard_map/ppermute | solution.py:30
  77.2 39.0 %collective-permute-start.3 = (bf16[4,2,24,1536]{3,2,1,0:T(8,128)(2,1)}, bf16[4,2,24,1536]{3,2,1,0:T(8,128)(2,1)}, u32[]{:S(2)}, u32[]{:S(2)}) collective-permute-start(bf16[4,2,24,1536]{3,2,1,0:T(8,128)(2,1)} %get-tuple-element.129), channel_id=1, source_target_pairs={{0,2},{1,3},{2,0},{3,1},{4,6},{5,7},{6,4},{7,5},{8,10},{9,11},{10,... | collective-permute-start | bytes 1769480 | tf_op jit(solution)/shard_map/ppermute | solution.py:30
  79.8 37.2 %collective-permute-start.4 = (bf16[4,2,24,1536]{3,2,1,0:T(8,128)(2,1)}, bf16[4,2,24,1536]{3,2,1,0:T(8,128)(2,1)}, u32[]{:S(2)}, u32[]{:S(2)}) collective-permute-start(bf16[4,2,24,1536]{3,2,1,0:T(8,128)(2,1)} %get-tuple-element.128), channel_id=1, source_target_pairs={{0,3},{1,2},{2,1},{3,0},{4,7},{5,6},{6,5},{7,4},{8,11},{9,10},{10,... | collective-permute-start | bytes 1769480 | tf_op jit(solution)/shard_map/ppermute | solution.py:30
  82.7 32.2 %collective-permute-start.8 = (bf16[2,4,24,1536]{3,2,1,0:T(8,128)(2,1)}, bf16[2,4,24,1536]{3,2,1,0:T(8,128)(2,1)S(1)}, u32[]{:S(2)}, u32[]{:S(2)}) collective-permute-start(bf16[2,4,24,1536]{3,2,1,0:T(8,128)(2,1)} %get-tuple-element.126), channel_id=1, source_target_pairs={{0,32},{1,33},{2,34},{3,35},{4,36},{5,37},{6,38},{7,39},{8,40},{9,... | collective-permute-start | bytes 1769480 | tf_op jit(solution)/shard_map/ppermute | solution.py:30
  84.7 31.5 %collective-permute-start.9 = (bf16[2,4,24,1536]{3,2,1,0:T(8,128)(2,1)S(1)}, bf16[2,4,24,1536]{3,2,1,0:T(8,128)(2,1)S(1)}, u32[]{:S(2)}, u32[]{:S(2)}) collective-permute-start(bf16[2,4,24,1536]{3,2,1,0:T(8,128)(2,1)S(1)} %get-tuple-element.124), channel_id=1, source_target_pairs={{0,96},{1,97},{2,98},{3,99},{4,100},{5,101},{6,102},{7,103},{8,104... | collective-permute-start | bytes 1769480 | tf_op jit(solution)/shard_map/ppermute | solution.py:30
  110.7 35.0 %all-to-all-start.1 = ((bf16[8,3,32,768]{3,2,1,0:T(8,128)(2,1)}), bf16[8,3,32,768]{3,2,1,0:T(8,128)(2,1)}, u32[]{:S(2)}, u32[]{:S(2)}) async-start(bf16[8,3,32,768]{3,2,1,0:T(8,128)(2,1)} %pack_strips.3), calls=%async_computation.1 | async-start | bytes 2359296 | tf_op jit(solution)/shard_map/all_to_all | solution.py:726
  115.0 24.7 %collective-permute-start.10 = (bf16[2,4,24,1536]{3,2,1,0:T(8,128)(2,1)S(1)}, bf16[2,4,24,1536]{3,2,1,0:T(8,128)(2,1)}, u32[]{:S(2)}, u32[]{:S(2)}) collective-permute-start(bf16[2,4,24,1536]{3,2,1,0:T(8,128)(2,1)S(1)} %get-tuple-element.98), channel_id=1, source_target_pairs={{0,64},{1,65},{2,66},{3,67},{4,68},{5,69},{6,70},{7,71},{8,72},{9,... | collective-permute-start | bytes 1769480 | tf_op jit(solution)/shard_map/ppermute | solution.py:30
  116.2 0.8 copy-start.2
  117.0 6.6 %copy-start.3 = (bf16[2,4,24,1536]{3,2,1,0:T(8,128)(2,1)S(1)}, bf16[2,4,24,1536]{3,2,1,0:T(8,128)(2,1)}, u32[]{:S(2)}) copy-start(bf16[2,4,24,1536]{3,2,1,0:T(8,128)(2,1)} %copy-done.2) | copy-start | bytes 1769476
  118.8 19.7 %collective-permute-start.5 = (bf16[2,24,1536]{2,1,0:T(8,128)(2,1)S(1)}, bf16[2,24,1536]{2,1,0:T(8,128)(2,1)}, u32[]{:S(2)}, u32[]{:S(2)}) collective-permute-start(bf16[2,24,1536]{2,1,0:T(8,128)(2,1)S(1)} %get-tuple-element.142), channel_id=1, source_target_pairs={{0,32},{1,33},{2,34},{3,35},{4,36},{5,37},{6,38},{7,39},{8,40},{9,... | collective-permute-start | bytes 442376 | tf_op jit(solution)/shard_map/ppermute | solution.py:30
  119.4 19.1 %collective-permute-start.6 = (bf16[2,24,1536]{2,1,0:T(8,128)(2,1)S(1)}, bf16[2,24,1536]{2,1,0:T(8,128)(2,1)}, u32[]{:S(2)}, u32[]{:S(2)}) collective-permute-start(bf16[2,24,1536]{2,1,0:T(8,128)(2,1)S(1)} %get-tuple-element.141), channel_id=1, source_target_pairs={{0,64},{1,65},{2,66},{3,67},{4,68},{5,69},{6,70},{7,71},{8,72},{9,... | collective-permute-start | bytes 442376 | tf_op jit(solution)/shard_map/ppermute | solution.py:30
  123.0 15.5 %collective-permute-start.7 = (bf16[2,24,1536]{2,1,0:T(8,128)(2,1)S(1)}, bf16[2,24,1536]{2,1,0:T(8,128)(2,1)}, u32[]{:S(2)}, u32[]{:S(2)}) collective-permute-start(bf16[2,24,1536]{2,1,0:T(8,128)(2,1)S(1)} %get-tuple-element.140), channel_id=1, source_target_pairs={{0,96},{1,97},{2,98},{3,99},{4,100},{5,101},{6,102},{7,103},{8,104... | collective-permute-start | bytes 442376 | tf_op jit(solution)/shard_map/ppermute | solution.py:30
  123.8 14.6 %copy-start.5 = (f32[4,768]{1,0:T(4,128)S(1)}, f32[4,768]{1,0:T(4,128)}, u32[]{:S(2)}) copy-start(f32[4,768]{1,0:T(4,128)} %get-tuple-element.101) | copy-start | bytes 36868
  141.0 10.5 %collective-permute-start.11 = (bf16[80,1536]{1,0:T(8,128)(2,1)S(1)}, bf16[80,1536]{1,0:T(8,128)(2,1)S(1)}, u32[]{:S(2)}, u32[]{:S(2)}) collective-permute-start(bf16[80,1536]{1,0:T(8,128)(2,1)S(1)} %get-tuple-element.155), channel_id=1, source_target_pairs={{0,1},{1,0},{2,3},{3,2},{4,5},{5,4},{6,7},{7,6},{8,9},{9,8},{10,11... | collective-permute-start | bytes 737288 | tf_op jit(solution)/shard_map/ppermute | solution.py:30
  142.9 11.5 %collective-permute-start.12 = (bf16[80,1536]{1,0:T(8,128)(2,1)S(1)}, bf16[80,1536]{1,0:T(8,128)(2,1)S(1)}, u32[]{:S(2)}, u32[]{:S(2)}) collective-permute-start(bf16[80,1536]{1,0:T(8,128)(2,1)S(1)} %get-tuple-element.154), channel_id=1, source_target_pairs={{0,2},{1,3},{2,0},{3,1},{4,6},{5,7},{6,4},{7,5},{8,10},{9,11},{10,... | collective-permute-start | bytes 737288 | tf_op jit(solution)/shard_map/ppermute | solution.py:30
  145.6 11.4 %collective-permute-start.13 = (bf16[80,1536]{1,0:T(8,128)(2,1)S(1)}, bf16[80,1536]{1,0:T(8,128)(2,1)S(1)}, u32[]{:S(2)}, u32[]{:S(2)}) collective-permute-start(bf16[80,1536]{1,0:T(8,128)(2,1)S(1)} %get-tuple-element.153), channel_id=1, source_target_pairs={{0,3},{1,2},{2,1},{3,0},{4,7},{5,6},{6,5},{7,4},{8,11},{9,10},{10,... | collective-permute-start | bytes 737288 | tf_op jit(solution)/shard_map/ppermute | solution.py:30
  157.4 10.5 %collective-permute-start.14 = (bf16[56,1536]{1,0:T(8,128)(2,1)S(1)}, bf16[56,1536]{1,0:T(8,128)(2,1)S(1)}, u32[]{:S(2)}, u32[]{:S(2)}) collective-permute-start(bf16[56,1536]{1,0:T(8,128)(2,1)S(1)} %get-tuple-element.152), channel_id=1, source_target_pairs={{0,4},{1,5},{2,6},{3,7},{4,0},{5,1},{6,2},{7,3},{8,12},{9,13},{10,... | collective-permute-start | bytes 516104 | tf_op jit(solution)/shard_map/ppermute | solution.py:30
  158.9 9.4 %collective-permute-start.15 = (bf16[56,1536]{1,0:T(8,128)(2,1)S(1)}, bf16[56,1536]{1,0:T(8,128)(2,1)S(1)}, u32[]{:S(2)}, u32[]{:S(2)}) collective-permute-start(bf16[56,1536]{1,0:T(8,128)(2,1)S(1)} %get-tuple-element.151), channel_id=1, source_target_pairs={{0,16},{1,17},{2,18},{3,19},{4,20},{5,21},{6,22},{7,23},{8,24},{9,... | collective-permute-start | bytes 516104 | tf_op jit(solution)/shard_map/ppermute | solution.py:30
  161.8 8.3 %collective-permute-start.16 = (bf16[56,1536]{1,0:T(8,128)(2,1)S(1)}, bf16[56,1536]{1,0:T(8,128)(2,1)S(1)}, u32[]{:S(2)}, u32[]{:S(2)}) collective-permute-start(bf16[56,1536]{1,0:T(8,128)(2,1)S(1)} %get-tuple-element.150), channel_id=1, source_target_pairs={{0,20},{1,21},{2,22},{3,23},{4,16},{5,17},{6,18},{7,19},{8,28},{9,... | collective-permute-start | bytes 516104 | tf_op jit(solution)/shard_map/ppermute | solution.py:30
  170.3 10.5 %collective-permute-start.17 = (bf16[64,768]{1,0:T(8,128)(2,1)S(1)}, bf16[64,768]{1,0:T(8,128)(2,1)S(1)}, u32[]{:S(2)}, u32[]{:S(2)}) collective-permute-start(bf16[64,768]{1,0:T(8,128)(2,1)S(1)} %get-tuple-element.133), channel_id=1, source_target_pairs={{0,32},{1,33},{2,34},{3,35},{4,36},{5,37},{6,38},{7,39},{8,40},{9,... | collective-permute-start | bytes 294920 | tf_op jit(solution)/shard_map/ppermute | solution.py:30
  170.4 10.4 %collective-permute-start.18 = (bf16[64,768]{1,0:T(8,128)(2,1)S(1)}, bf16[64,768]{1,0:T(8,128)(2,1)S(1)}, u32[]{:S(2)}, u32[]{:S(2)}) collective-permute-start(bf16[64,768]{1,0:T(8,128)(2,1)S(1)} %get-tuple-element.133), channel_id=1, source_target_pairs={{0,64},{1,65},{2,66},{3,67},{4,68},{5,69},{6,70},{7,71},{8,72},{9,... | collective-permute-start | bytes 294920 | tf_op jit(solution)/shard_map/ppermute | solution.py:30
  174.2 6.6 %collective-permute-start.19 = (bf16[64,768]{1,0:T(8,128)(2,1)S(1)}, bf16[64,768]{1,0:T(8,128)(2,1)S(1)}, u32[]{:S(2)}, u32[]{:S(2)}) collective-permute-start(bf16[64,768]{1,0:T(8,128)(2,1)S(1)} %get-tuple-element.133), channel_id=1, source_target_pairs={{0,96},{1,97},{2,98},{3,99},{4,100},{5,101},{6,102},{7,103},{8,104... | collective-permute-start | bytes 294920 | tf_op jit(solution)/shard_map/ppermute | solution.py:30
  180.9 1.5 collective-permute-start.20

commit v5 on v4

--- a/solution.py
+++ b/solution.py
@@ -742,6 +742,7 @@
     high_x = x_parts(fold(gate([near, got_far], done_low), bf16))
     back = functools.partial(back_conv, neighbours)
     grad_strips = after(grad_strips, small)
+    small = trade(small, 8, tuple(high_x))
     wide_x, small = ride(high_x, small)
     input_grad = back(after(conv_grad, *wide_x), grad_strips, dw_weight, grad, 0, 3)
     done_high, small = land(wide_x, small, high_x, x_distances, bf16, input_grad)
@@ -752,8 +753,7 @@
     sent_small = small.astype(bf16)
     got_small = [swap(sent_small, d) for d in z_distances]
     input_grad = back(after(conv_grad, sent_small), grad_strips, dw_weight, grad, 2, 3, input_grad)
-    small = fold(gate([lax.reduce_precision(small, 8, 7), *got_small], input_grad), f32)
-    small = trade(small, 8, small)[:count]
+    small = fold(gate([lax.reduce_precision(small, 8, 7), *got_small], input_grad), f32)[:count]
     split = taps * taps
     return (
         out.reshape(features.shape),

time: 186 us -> 188 us (1.011)
  waiting for transfers between devices: 9.8 us -> 12.9 us
    ppermute x21, waiting for transfers between devices: 8.49 us -> 11.6 us  [swap(): return lax.ppermute(value, both_axes, pairs)]
  transfers between devices with their start and end apart: 23 -> 23, of which waited for: 6 -> 5; matrix products, arithmetic and copies ran while one was open for 8% -> 8% of each run, Pallas kernels for 45% -> 44%
where the time goes in v5:
time: 188 us
  Pallas kernels  113 us (60%)
  starting transfers between devices  39.9 us (21%)
  waiting for transfers between devices  12.9 us (7%)
  other arithmetic  10.5 us (6%)
  local copies, waits for them, and re-layouts  9.41 us (5%)
    pallas_call x2, Pallas kernels, hidden_half(): pl.pallas_call(hidden_kernel, grid=(steps,), out_shape=[wide_shape, wide_...  32.8 us
    ppermute x21, starting transfers between devices, swap(): return lax.ppermute(value, both_axes, pairs)  30.3 us
    pallas_call x1, Pallas kernels, join(): pl.pallas_call(join_kernel, grid=(4,), out_shape=[pixel, pixel, jax.Shape...  20.7 us
    pallas_call x3, Pallas kernels, back_conv(): pl.pallas_call(back_kernel, grid=(steps,), out_shape=jax.ShapeDtypeStruct...  17.1 us
    pallas_call x1, Pallas kernels, kernel_grad(): pl.pallas_call(kernel_grad_kernel, grid=(channels // lanes,), out_shape=j...  13.6 us
    pallas_call x1, Pallas kernels, conv_inner(): pl.pallas_call(inner_kernel, grid=(blocks,), out_shape=jax.ShapeDtypeStru...  12.6 us
    ppermute x21, waiting for transfers between devices, swap(): return lax.ppermute(value, both_axes, pairs)  11.6 us
    pallas_call x1, Pallas kernels, conv_norm(): pl.pallas_call(norm_kernel, grid=(blocks,), out_shape=[jax.ShapeDtypeStru...  10.6 us
  transfers between devices with their start and end apart: 23, of which 5 were waited for; matrix products, arithmetic and copies ran while one was open for 8% of the time, Pallas kernels for 44%

profile of v5, /device:TPU:0, one launch (start us, length us, event | category | flops | bytes accessed | tf_op | source)
XLA Modules:
  0.0 187.5 jit_solution(3832556748345763868)
XLA Ops:
  0.7 2.9 %pack_strips.2 = bf16[8,3,32,768]{3,2,1,0:T(8,128)(2,1)} custom-call(s32[1,8,8]{2,1,0:T(8,128)} %table_ref.13, bf16[32,32,768]{2,1,0:T(8,128)(2,1)} %bitcast.66), custom_call_target="tpu_custom_call" | custom-call | tf_op jit(solution)/shard_map/pack_strips/pallas_call | solution.py:60
  3.5 5.4 %all-to-all-start = ((bf16[8,3,32,768]{3,2,1,0:T(8,128)(2,1)}), bf16[8,3,32,768]{3,2,1,0:T(8,128)(2,1)S(1)}, u32[]{:S(2)}, u32[]{:S(2)}) async-start(bf16[8,3,32,768]{3,2,1,0:T(8,128)(2,1)} %pack_strips.2), calls=%async_computation | async-start | bytes 2359296 | tf_op jit(solution)/shard_map/all_to_all | solution.py:702
  9.6 0.7 copy.20.weight_ref.refs_1_
  10.3 0.5 broadcast.20
  10.8 0.7 reduce.5
  11.5 0.6 reshape.96.up_bias_ref
  12.1 12.6 %conv_inner.1.part_ref = f32[6,32,32,128]{3,2,1,0:T(8,128)} custom-call(bf16[32,32,768]{2,1,0:T(8,128)(2,1)} %bitcast.67, f32[1,7,7,768]{3,2,1,0:T(8,128)} %copy.20.weight_ref.refs_1_), custom_call_target="tpu_custom_call" | custom-call | flops 14000000000 | bytes 5000000 | tf_op jit(solution)/shard_map/conv_inner/pallas_call | solution.py:144
  24.7 1.3 all-to-all-done.strip_ref.refs_0_
  26.0 1.0 copy-done.1
  27.0 10.6 %conv_norm.1 = (f32[1024,768]{1,0:T(8,128)}, f32[1024,1]{1,0:T(8,128)}, bf16[1024,768]{1,0:T(8,128)(2,1)}) custom-call(s32[1,8,8]{2,1,0:T(8,128)} %table_ref.13, f32[6,32,32,128]{3,2,1,0:T(8,128)} %conv_inner.1.part_ref, bf16[8,3,32,768]{3,2,1,0:T(8,128)(2,1)} %copy-done.1, f32[1,7,7,768]{3,2,1,0:T(8,128)} %copy.20.weight_ref.refs_1_, f32[1,768]{1,0:T(1,128)} %gain_ref.3, ...), custom_call_target="tpu_custom_call" | custom-call | flops 7000000000 | bytes 10000000 | tf_op jit(solution)/shard_map/conv_norm/pallas_call | solution.py:261
  37.6 16.4 %hidden_half.2 = (bf16[1024,1536]{1,0:T(8,128)(2,1)}, bf16[1024,1536]{1,0:T(8,128)(2,1)}, bf16[2,2,192,1536]{3,2,1,0:T(8,128)(2,1)}, bf16[2,2,192,1536]{3,2,1,0:T(8,128)(2,1)}, f32[2,1,768]{2,1,0:T(1,128)}) custom-call(s32[1,1]{1,0:T(1,128)S(6)} %copy.31.skip_ref, bf16[1024,768]{1,0:T(8,128)(2,1)} %get-tuple-element.71.normed_ref, ...), custom_call_target="tpu_custom_call" | custom-call | flops 14000000000 | bytes 20000000 | tf_op jit(solution)/shard_map/hidden_half/pallas_call | solution.py:375
  54.0 0.0 copy-start.7
  54.0 0.3 collective-permute-start
  54.3 16.4 %hidden_half.3 = (bf16[1024,1536]{1,0:T(8,128)(2,1)}, bf16[1024,1536]{1,0:T(8,128)(2,1)}, bf16[2,2,192,1536]{3,2,1,0:T(8,128)(2,1)}, bf16[2,2,192,1536]{3,2,1,0:T(8,128)(2,1)}, f32[2,1,768]{2,1,0:T(1,128)}) custom-call(s32[1,1]{1,0:T(1,128)S(6)} %copy.31.skip_ref, bf16[1024,768]{1,0:T(8,128)(2,1)} %get-tuple-element.71.normed_ref, ...), custom_call_target="tpu_custom_call" | custom-call | flops 14000000000 | bytes 20000000 | tf_op jit(solution)/shard_map/hidden_half/pallas_call | solution.py:375
  70.7 0.6 collective-permute-start.1
  71.2 0.7 reduce.2
  72.1 3.0 %add_convert_fusion.1 = bf16[2,2,192,1536]{3,2,1,0:T(8,128)(2,1)S(1)} fusion(bf16[2,2,192,1536]{3,2,1,0:T(8,128)(2,1)} %collective-permute-done, bf16[2,2,192,1536]{3,2,1,0:T(8,128)(2,1)} %get-tuple-element.73), kind=kLoop, calls=%fused_computation.1 | loop fusion | flops 4718592 | bytes 7077888 | tf_op jit(solution)/shard_map/convert_element_type | solution.py:615
  75.1 1.3 dynamic-slice_bitcast_fusion.4
  76.3 0.9 collective-permute-start.2
  77.2 2.5 %collective-permute-start.3 = (bf16[4,2,24,1536]{3,2,1,0:T(8,128)(2,1)}, bf16[4,2,24,1536]{3,2,1,0:T(8,128)(2,1)}, u32[]{:S(2)}, u32[]{:S(2)}) collective-permute-start(bf16[4,2,24,1536]{3,2,1,0:T(8,128)(2,1)} %get-tuple-element.129), channel_id=1, source_target_pairs={{0,2},{1,3},{2,0},{3,1},{4,6},{5,7},{6,4},{7,5},{8,10},{9,11},{10,... | collective-permute-start | bytes 1769480 | tf_op jit(solution)/shard_map/ppermute | solution.py:30
  79.7 1.3 collective-permute-start.4
  81.1 0.6 add_convert_fusion
  81.7 1.1 dynamic-slice_bitcast_fusion
  82.7 1.9 %collective-permute-start.8 = (bf16[2,4,24,1536]{3,2,1,0:T(8,128)(2,1)}, bf16[2,4,24,1536]{3,2,1,0:T(8,128)(2,1)S(1)}, u32[]{:S(2)}, u32[]{:S(2)}) collective-permute-start(bf16[2,4,24,1536]{3,2,1,0:T(8,128)(2,1)} %get-tuple-element.126), channel_id=1, source_target_pairs={{0,32},{1,33},{2,34},{3,35},{4,36},{5,37},{6,38},{7,39},{8,40},{9,... | collective-permute-start | bytes 1769480 | tf_op jit(solution)/shard_map/ppermute | solution.py:30
  84.6 2.5 %collective-permute-start.9 = (bf16[2,4,24,1536]{3,2,1,0:T(8,128)(2,1)S(1)}, bf16[2,4,24,1536]{3,2,1,0:T(8,128)(2,1)S(1)}, u32[]{:S(2)}, u32[]{:S(2)}) collective-permute-start(bf16[2,4,24,1536]{3,2,1,0:T(8,128)(2,1)S(1)} %get-tuple-element.124), channel_id=1, source_target_pairs={{0,96},{1,97},{2,98},{3,99},{4,100},{5,101},{6,102},{7,103},{8,104... | collective-permute-start | bytes 1769480 | tf_op jit(solution)/shard_map/ppermute | solution.py:30
  87.2 20.7 %join_halves.1 = (bf16[1024,768]{1,0:T(8,128)(2,1)}, bf16[1024,768]{1,0:T(8,128)(2,1)}, f32[4,768]{1,0:T(4,128)}) custom-call(s32[1,1]{1,0:T(1,128)S(6)} %copy.31.skip_ref, bf16[1024,1536]{1,0:T(8,128)(2,1)} %get-tuple-element.79.act_low_ref, bf16[1024,1536]{1,0:T(8,128)(2,1)} %get-tuple-element.72.act_high_ref, ...), custom_call_target="tpu_custom_call" | custom-call | flops 14000000000 | bytes 30000000 | tf_op jit(solution)/shard_map/join_halves/pallas_call | solution.py:475
  107.9 2.8 %pack_strips.3 = bf16[8,3,32,768]{3,2,1,0:T(8,128)(2,1)} custom-call(s32[1,8,8]{2,1,0:T(8,128)} %table_ref.13, bf16[32,32,768]{2,1,0:T(8,128)(2,1)} %bitcast.70), custom_call_target="tpu_custom_call" | custom-call | tf_op jit(solution)/shard_map/pack_strips/pallas_call | solution.py:60
  110.7 4.3 %all-to-all-start.1 = ((bf16[8,3,32,768]{3,2,1,0:T(8,128)(2,1)}), bf16[8,3,32,768]{3,2,1,0:T(8,128)(2,1)}, u32[]{:S(2)}, u32[]{:S(2)}) async-start(bf16[8,3,32,768]{3,2,1,0:T(8,128)(2,1)} %pack_strips.3), calls=%async_computation.1 | async-start | bytes 2359296 | tf_op jit(solution)/shard_map/all_to_all | solution.py:726
  115.0 1.1 collective-permute-start.10
  116.2 0.8 copy-done.2
  117.0 1.8 add_convert_fusion.3
  118.8 0.1 dynamic-slice_bitcast_fusion.9
  118.8 0.6 collective-permute-start.5
  119.4 3.6 %collective-permute-start.6 = (bf16[2,24,1536]{2,1,0:T(8,128)(2,1)S(1)}, bf16[2,24,1536]{2,1,0:T(8,128)(2,1)}, u32[]{:S(2)}, u32[]{:S(2)}) collective-permute-start(bf16[2,24,1536]{2,1,0:T(8,128)(2,1)S(1)} %get-tuple-element.141), channel_id=1, source_target_pairs={{0,64},{1,65},{2,66},{3,67},{4,68},{5,69},{6,70},{7,71},{8,72},{9,... | collective-permute-start | bytes 442376 | tf_op jit(solution)/shard_map/ppermute | solution.py:30
  123.0 0.6 collective-permute-start.7
  123.6 0.2 convert_add_fusion
  123.8 13.6 %kernel_grad.1 = f32[7,7,768]{2,1,0:T(8,128)} custom-call(s32[1,8,8]{2,1,0:T(8,128)} %table_ref.13, bf16[32,32,768]{2,1,0:T(8,128)(2,1)} %bitcast.69, bf16[8,3,32,768]{3,2,1,0:T(8,128)(2,1)} %copy-done.1, bf16[32,32,768]{2,1,0:T(8,128)(2,1)} %bitcast.71), custom_call_target="tpu_custom_call" | custom-call | flops 14000000000 | bytes 5000000 | tf_op jit(solution)/shard_map/kernel_grad/pallas_call | solution.py:542
  137.4 0.9 reshape.101
  138.4 0.1 collective-permute-start.11
  138.5 1.1 add_convert_fusion.4
  139.7 1.2 add_convert_fusion.2
  140.8 0.1 constant_dynamic-slice_fusion
  141.0 0.1 pad_maximum_fusion
  141.1 1.9 %collective-permute-start.12 = (bf16[80,1536]{1,0:T(8,128)(2,1)S(1)}, bf16[80,1536]{1,0:T(8,128)(2,1)S(1)}, u32[]{:S(2)}, u32[]{:S(2)}) collective-permute-start(bf16[80,1536]{1,0:T(8,128)(2,1)S(1)} %get-tuple-element.157), channel_id=1, source_target_pairs={{0,1},{1,0},{2,3},{3,2},{4,5},{5,4},{6,7},{7,6},{8,9},{9,8},{10,11... | collective-permute-start | bytes 737288 | tf_op jit(solution)/shard_map/ppermute | solution.py:30
  143.0 2.7 %collective-permute-start.13 = (bf16[80,1536]{1,0:T(8,128)(2,1)S(1)}, bf16[80,1536]{1,0:T(8,128)(2,1)S(1)}, u32[]{:S(2)}, u32[]{:S(2)}) collective-permute-start(bf16[80,1536]{1,0:T(8,128)(2,1)S(1)} %get-tuple-element.156), channel_id=1, source_target_pairs={{0,2},{1,3},{2,0},{3,1},{4,6},{5,7},{6,4},{7,5},{8,10},{9,11},{10,... | collective-permute-start | bytes 737288 | tf_op jit(solution)/shard_map/ppermute | solution.py:30
  145.6 0.2 collective-permute-start.14
  145.8 5.7 %back_conv.3.refs_3_ = bf16[32,32,768]{2,1,0:T(8,128)(2,1)} custom-call(s32[1,8,8]{2,1,0:T(8,128)} %table_ref.13, bf16[32,32,768]{2,1,0:T(8,128)(2,1)} %bitcast.72, bf16[8,3,32,768]{3,2,1,0:T(8,128)(2,1)} %all-to-all-done.1.refs_0_, f32[1,7,7,768]{3,2,1,0:T(8,128)} %copy.20.weight_ref.refs_1_, bf16[32,32,768]{2,1,0:T(8,128)(2,1)} %bitcast.99), custom_call_target="tpu_custom_call" | custom-call | flops 4666666496 | bytes 1666666 | tf_op jit(solution)/shard_map/back_conv/pallas_call | solution.py:578
  151.6 5.8 %collective-permute-done.13 = bf16[80,1536]{1,0:T(8,128)(2,1)S(1)} collective-permute-done((bf16[80,1536]{1,0:T(8,128)(2,1)S(1)}, bf16[80,1536]{1,0:T(8,128)(2,1)S(1)}, u32[]{:S(2)}, u32[]{:S(2)}) %collective-permute-start.13) | collective-permute-done | bytes 245792 | tf_op jit(solution)/shard_map/ppermute | solution.py:30
  157.3 2.6 %collective-permute-done.14 = bf16[80,1536]{1,0:T(8,128)(2,1)S(1)} collective-permute-done((bf16[80,1536]{1,0:T(8,128)(2,1)S(1)}, bf16[80,1536]{1,0:T(8,128)(2,1)S(1)}, u32[]{:S(2)}, u32[]{:S(2)}) %collective-permute-start.14) | collective-permute-done | bytes 245792 | tf_op jit(solution)/shard_map/ppermute | solution.py:30
  160.0 0.1 fusion.1
  160.4 1.6 collective-permute-start.15
  161.9 2.9 %collective-permute-start.16 = (bf16[56,1536]{1,0:T(8,128)(2,1)S(1)}, bf16[56,1536]{1,0:T(8,128)(2,1)S(1)}, u32[]{:S(2)}, u32[]{:S(2)}) collective-permute-start(bf16[56,1536]{1,0:T(8,128)(2,1)S(1)} %get-tuple-element.153), channel_id=1, source_target_pairs={{0,16},{1,17},{2,18},{3,19},{4,20},{5,21},{6,22},{7,23},{8,24},{9,... | collective-permute-start | bytes 516104 | tf_op jit(solution)/shard_map/ppermute | solution.py:30
  164.8 0.3 collective-permute-start.17
  165.1 5.7 %back_conv.4.refs_3_ = bf16[32,32,768]{2,1,0:T(8,128)(2,1)} custom-call(s32[1,8,8]{2,1,0:T(8,128)} %table_ref.13, bf16[32,32,768]{2,1,0:T(8,128)(2,1)} %bitcast.73, bf16[8,3,32,768]{3,2,1,0:T(8,128)(2,1)} %all-to-all-done.1.refs_0_, f32[1,7,7,768]{3,2,1,0:T(8,128)} %copy.20.weight_ref.refs_1_, ...), custom_call_target="tpu_custom_call", output_to_operand_aliasing={{}: (5, {})} | custom-call | flops 4666666496 | bytes 1666666 | tf_op jit(solution)/shard_map/back_conv/pallas_call | solution.py:578
  170.8 1.1 collective-permute-done.16
  171.9 2.1 %collective-permute-done.17 = bf16[56,1536]{1,0:T(8,128)(2,1)S(1)} collective-permute-done((bf16[56,1536]{1,0:T(8,128)(2,1)S(1)}, bf16[56,1536]{1,0:T(8,128)(2,1)S(1)}, u32[]{:S(2)}, u32[]{:S(2)}) %collective-permute-start.17) | collective-permute-done | bytes 172064 | tf_op jit(solution)/shard_map/ppermute | solution.py:30
  174.2 0.1 collective-permute-start.18
  174.3 4.1 %collective-permute-start.19 = (bf16[64,768]{1,0:T(8,128)(2,1)S(1)}, bf16[64,768]{1,0:T(8,128)(2,1)S(1)}, u32[]{:S(2)}, u32[]{:S(2)}) collective-permute-start(bf16[64,768]{1,0:T(8,128)(2,1)S(1)} %get-tuple-element.133), channel_id=1, source_target_pairs={{0,64},{1,65},{2,66},{3,67},{4,68},{5,69},{6,70},{7,71},{8,72},{9,... | collective-permute-start | bytes 294920 | tf_op jit(solution)/shard_map/ppermute | solution.py:30
  178.4 0.6 collective-permute-start.20
  179.0 0.7 add_bitcast_fusion
  179.7 5.7 %back_conv.5 = bf16[32,32,768]{2,1,0:T(8,128)(2,1)} custom-call(s32[1,8,8]{2,1,0:T(8,128)} %table_ref.13, bf16[32,32,768]{2,1,0:T(8,128)(2,1)} %bitcast.74, bf16[8,3,32,768]{3,2,1,0:T(8,128)(2,1)} %all-to-all-done.1.refs_0_, f32[1,7,7,768]{3,2,1,0:T(8,128)} %copy.20.weight_ref.refs_1_, ...), custom_call_target="tpu_custom_call", output_to_operand_aliasing={{}: (5, {})} | custom-call | flops 4666666496 | bytes 1666666 | tf_op jit(solution)/shard_map/back_conv/pallas_call | solution.py:578
  185.5 0.6 slice_bitcast_fusion
  186.1 0.8 reshape.109
  186.9 0.6 copy.26
  (58 shorter events, 0.8 us)
Async XLA Ops:
  0.6 8.9 %copy-start.4 = (f32[1,7,7,768]{3,0,2,1:T(1,128)S(1)}, f32[1,7,7,768]{3,0,2,1:T(1,128)}, u32[]{:S(2)}) copy-start(f32[1,7,7,768]{3,0,2,1:T(1,128)} %param.16) | copy-start | bytes 451588
  0.6 10.1 %copy-start.6 = (f32[1,3072]{1,0:T(1,128)S(1)}, f32[1,3072]{1,0:T(1,128)}, u32[]{:S(2)}) copy-start(f32[1,3072]{1,0:T(1,128)} %param.20) | copy-start | bytes 36868
  3.5 22.5 %all-to-all-start = ((bf16[8,3,32,768]{3,2,1,0:T(8,128)(2,1)}), bf16[8,3,32,768]{3,2,1,0:T(8,128)(2,1)S(1)}, u32[]{:S(2)}, u32[]{:S(2)}) async-start(bf16[8,3,32,768]{3,2,1,0:T(8,128)(2,1)} %pack_strips.2), calls=%async_computation | async-start | bytes 2359296 | tf_op jit(solution)/shard_map/all_to_all | solution.py:702
  26.0 1.0 copy-start.1
  54.0 18.0 %copy-start.7 = (f32[2,1,768]{2,1,0:T(1,128)S(1)}, f32[2,1,768]{2,1,0:T(1,128)}, u32[]{:S(2)}) copy-start(f32[2,1,768]{2,1,0:T(1,128)} %get-tuple-element.102) | copy-start | bytes 18436
  54.0 18.0 %collective-permute-start = (bf16[2,2,192,1536]{3,2,1,0:T(8,128)(2,1)}, bf16[2,2,192,1536]{3,2,1,0:T(8,128)(2,1)}, u32[]{:S(2)}, u32[]{:S(2)}) collective-permute-start(bf16[2,2,192,1536]{3,2,1,0:T(8,128)(2,1)} %get-tuple-element.70), channel_id=1, source_target_pairs={{0,8},{1,9},{2,10},{3,11},{4,12},{5,13},{6,14},{7,15},{8,0},{9,1},... | collective-permute-start | bytes 7077896 | tf_op jit(solution)/shard_map/ppermute | solution.py:30
  70.7 10.4 %collective-permute-start.1 = (bf16[2,2,192,1536]{3,2,1,0:T(8,128)(2,1)}, bf16[2,2,192,1536]{3,2,1,0:T(8,128)(2,1)S(1)}, u32[]{:S(2)}, u32[]{:S(2)}) collective-permute-start(bf16[2,2,192,1536]{3,2,1,0:T(8,128)(2,1)} %get-tuple-element.76), channel_id=1, source_target_pairs={{0,8},{1,9},{2,10},{3,11},{4,12},{5,13},{6,14},{7,15},{8,0},{9,1},... | collective-permute-start | bytes 7077896 | tf_op jit(solution)/shard_map/ppermute | solution.py:30
  75.1 6.0 %copy-start = (bf16[2,2,192,1536]{3,2,1,0:T(8,128)(2,1)S(1)}, bf16[2,2,192,1536]{3,2,1,0:T(8,128)(2,1)}, u32[]{:S(2)}) copy-start(bf16[2,2,192,1536]{3,2,1,0:T(8,128)(2,1)} %get-tuple-element.77) | copy-start | bytes 7077892
  76.3 39.8 %collective-permute-start.2 = (bf16[4,2,24,1536]{3,2,1,0:T(8,128)(2,1)}, bf16[4,2,24,1536]{3,2,1,0:T(8,128)(2,1)}, u32[]{:S(2)}, u32[]{:S(2)}) collective-permute-start(bf16[4,2,24,1536]{3,2,1,0:T(8,128)(2,1)} %get-tuple-element.130), channel_id=1, source_target_pairs={{0,1},{1,0},{2,3},{3,2},{4,5},{5,4},{6,7},{7,6},{8,9},{9,8},{10,11... | collective-permute-start | bytes 1769480 | tf_op jit(solution)/shard_map/ppermute | solution.py:30
  77.2 39.0 %collective-permute-start.3 = (bf16[4,2,24,1536]{3,2,1,0:T(8,128)(2,1)}, bf16[4,2,24,1536]{3,2,1,0:T(8,128)(2,1)}, u32[]{:S(2)}, u32[]{:S(2)}) collective-permute-start(bf16[4,2,24,1536]{3,2,1,0:T(8,128)(2,1)} %get-tuple-element.129), channel_id=1, source_target_pairs={{0,2},{1,3},{2,0},{3,1},{4,6},{5,7},{6,4},{7,5},{8,10},{9,11},{10,... | collective-permute-start | bytes 1769480 | tf_op jit(solution)/shard_map/ppermute | solution.py:30
  79.7 37.3 %collective-permute-start.4 = (bf16[4,2,24,1536]{3,2,1,0:T(8,128)(2,1)}, bf16[4,2,24,1536]{3,2,1,0:T(8,128)(2,1)}, u32[]{:S(2)}, u32[]{:S(2)}) collective-permute-start(bf16[4,2,24,1536]{3,2,1,0:T(8,128)(2,1)} %get-tuple-element.128), channel_id=1, source_target_pairs={{0,3},{1,2},{2,1},{3,0},{4,7},{5,6},{6,5},{7,4},{8,11},{9,10},{10,... | collective-permute-start | bytes 1769480 | tf_op jit(solution)/shard_map/ppermute | solution.py:30
  82.7 32.3 %collective-permute-start.8 = (bf16[2,4,24,1536]{3,2,1,0:T(8,128)(2,1)}, bf16[2,4,24,1536]{3,2,1,0:T(8,128)(2,1)S(1)}, u32[]{:S(2)}, u32[]{:S(2)}) collective-permute-start(bf16[2,4,24,1536]{3,2,1,0:T(8,128)(2,1)} %get-tuple-element.126), channel_id=1, source_target_pairs={{0,32},{1,33},{2,34},{3,35},{4,36},{5,37},{6,38},{7,39},{8,40},{9,... | collective-permute-start | bytes 1769480 | tf_op jit(solution)/shard_map/ppermute | solution.py:30
  84.6 31.5 %collective-permute-start.9 = (bf16[2,4,24,1536]{3,2,1,0:T(8,128)(2,1)S(1)}, bf16[2,4,24,1536]{3,2,1,0:T(8,128)(2,1)S(1)}, u32[]{:S(2)}, u32[]{:S(2)}) collective-permute-start(bf16[2,4,24,1536]{3,2,1,0:T(8,128)(2,1)S(1)} %get-tuple-element.124), channel_id=1, source_target_pairs={{0,96},{1,97},{2,98},{3,99},{4,100},{5,101},{6,102},{7,103},{8,104... | collective-permute-start | bytes 1769480 | tf_op jit(solution)/shard_map/ppermute | solution.py:30
  110.7 35.1 %all-to-all-start.1 = ((bf16[8,3,32,768]{3,2,1,0:T(8,128)(2,1)}), bf16[8,3,32,768]{3,2,1,0:T(8,128)(2,1)}, u32[]{:S(2)}, u32[]{:S(2)}) async-start(bf16[8,3,32,768]{3,2,1,0:T(8,128)(2,1)} %pack_strips.3), calls=%async_computation.1 | async-start | bytes 2359296 | tf_op jit(solution)/shard_map/all_to_all | solution.py:726
  115.0 24.6 %collective-permute-start.10 = (bf16[2,4,24,1536]{3,2,1,0:T(8,128)(2,1)S(1)}, bf16[2,4,24,1536]{3,2,1,0:T(8,128)(2,1)}, u32[]{:S(2)}, u32[]{:S(2)}) collective-permute-start(bf16[2,4,24,1536]{3,2,1,0:T(8,128)(2,1)S(1)} %get-tuple-element.98), channel_id=1, source_target_pairs={{0,64},{1,65},{2,66},{3,67},{4,68},{5,69},{6,70},{7,71},{8,72},{9,... | collective-permute-start | bytes 1769480 | tf_op jit(solution)/shard_map/ppermute | solution.py:30
  116.2 0.8 copy-start.2
  117.0 6.6 %copy-start.3 = (bf16[2,4,24,1536]{3,2,1,0:T(8,128)(2,1)S(1)}, bf16[2,4,24,1536]{3,2,1,0:T(8,128)(2,1)}, u32[]{:S(2)}) copy-start(bf16[2,4,24,1536]{3,2,1,0:T(8,128)(2,1)} %copy-done.2) | copy-start | bytes 1769476
  118.8 19.7 %collective-permute-start.5 = (bf16[2,24,1536]{2,1,0:T(8,128)(2,1)S(1)}, bf16[2,24,1536]{2,1,0:T(8,128)(2,1)}, u32[]{:S(2)}, u32[]{:S(2)}) collective-permute-start(bf16[2,24,1536]{2,1,0:T(8,128)(2,1)S(1)} %get-tuple-element.142), channel_id=1, source_target_pairs={{0,32},{1,33},{2,34},{3,35},{4,36},{5,37},{6,38},{7,39},{8,40},{9,... | collective-permute-start | bytes 442376 | tf_op jit(solution)/shard_map/ppermute | solution.py:30
  119.4 19.1 %collective-permute-start.6 = (bf16[2,24,1536]{2,1,0:T(8,128)(2,1)S(1)}, bf16[2,24,1536]{2,1,0:T(8,128)(2,1)}, u32[]{:S(2)}, u32[]{:S(2)}) collective-permute-start(bf16[2,24,1536]{2,1,0:T(8,128)(2,1)S(1)} %get-tuple-element.141), channel_id=1, source_target_pairs={{0,64},{1,65},{2,66},{3,67},{4,68},{5,69},{6,70},{7,71},{8,72},{9,... | collective-permute-start | bytes 442376 | tf_op jit(solution)/shard_map/ppermute | solution.py:30
  123.0 15.5 %collective-permute-start.7 = (bf16[2,24,1536]{2,1,0:T(8,128)(2,1)S(1)}, bf16[2,24,1536]{2,1,0:T(8,128)(2,1)}, u32[]{:S(2)}, u32[]{:S(2)}) collective-permute-start(bf16[2,24,1536]{2,1,0:T(8,128)(2,1)S(1)} %get-tuple-element.140), channel_id=1, source_target_pairs={{0,96},{1,97},{2,98},{3,99},{4,100},{5,101},{6,102},{7,103},{8,104... | collective-permute-start | bytes 442376 | tf_op jit(solution)/shard_map/ppermute | solution.py:30
  123.8 14.5 %copy-start.5 = (f32[4,768]{1,0:T(4,128)S(1)}, f32[4,768]{1,0:T(4,128)}, u32[]{:S(2)}) copy-start(f32[4,768]{1,0:T(4,128)} %get-tuple-element.101) | copy-start | bytes 36868
  138.4 2.5 %collective-permute-start.11 = (f32[64,768]{1,0:T(8,128)S(1)}, f32[64,768]{1,0:T(8,128)S(1)}, u32[]{:S(2)}, u32[]{:S(2)}) collective-permute-start(f32[64,768]{1,0:T(8,128)S(1)} %select_maximum_fusion), channel_id=1, source_target_pairs={{0,8},{1,9},{2,10},{3,11},{4,12},{5,13},{6,14},{7,15},{8,0},{9,1},... | collective-permute-start | bytes 589832 | tf_op jit(solution)/shard_map/ppermute | solution.py:30
  141.1 10.5 %collective-permute-start.12 = (bf16[80,1536]{1,0:T(8,128)(2,1)S(1)}, bf16[80,1536]{1,0:T(8,128)(2,1)S(1)}, u32[]{:S(2)}, u32[]{:S(2)}) collective-permute-start(bf16[80,1536]{1,0:T(8,128)(2,1)S(1)} %get-tuple-element.157), channel_id=1, source_target_pairs={{0,1},{1,0},{2,3},{3,2},{4,5},{5,4},{6,7},{7,6},{8,9},{9,8},{10,11... | collective-permute-start | bytes 737288 | tf_op jit(solution)/shard_map/ppermute | solution.py:30
  143.0 14.4 %collective-permute-start.13 = (bf16[80,1536]{1,0:T(8,128)(2,1)S(1)}, bf16[80,1536]{1,0:T(8,128)(2,1)S(1)}, u32[]{:S(2)}, u32[]{:S(2)}) collective-permute-start(bf16[80,1536]{1,0:T(8,128)(2,1)S(1)} %get-tuple-element.156), channel_id=1, source_target_pairs={{0,2},{1,3},{2,0},{3,1},{4,6},{5,7},{6,4},{7,5},{8,10},{9,11},{10,... | collective-permute-start | bytes 737288 | tf_op jit(solution)/shard_map/ppermute | solution.py:30
  145.6 14.3 %collective-permute-start.14 = (bf16[80,1536]{1,0:T(8,128)(2,1)S(1)}, bf16[80,1536]{1,0:T(8,128)(2,1)S(1)}, u32[]{:S(2)}, u32[]{:S(2)}) collective-permute-start(bf16[80,1536]{1,0:T(8,128)(2,1)S(1)} %get-tuple-element.155), channel_id=1, source_target_pairs={{0,3},{1,2},{2,1},{3,0},{4,7},{5,6},{6,5},{7,4},{8,11},{9,10},{10,... | collective-permute-start | bytes 737288 | tf_op jit(solution)/shard_map/ppermute | solution.py:30
  160.4 10.5 %collective-permute-start.15 = (bf16[56,1536]{1,0:T(8,128)(2,1)S(1)}, bf16[56,1536]{1,0:T(8,128)(2,1)S(1)}, u32[]{:S(2)}, u32[]{:S(2)}) collective-permute-start(bf16[56,1536]{1,0:T(8,128)(2,1)S(1)} %get-tuple-element.154), channel_id=1, source_target_pairs={{0,4},{1,5},{2,6},{3,7},{4,0},{5,1},{6,2},{7,3},{8,12},{9,13},{10,... | collective-permute-start | bytes 516104 | tf_op jit(solution)/shard_map/ppermute | solution.py:30
  161.9 10.0 %collective-permute-start.16 = (bf16[56,1536]{1,0:T(8,128)(2,1)S(1)}, bf16[56,1536]{1,0:T(8,128)(2,1)S(1)}, u32[]{:S(2)}, u32[]{:S(2)}) collective-permute-start(bf16[56,1536]{1,0:T(8,128)(2,1)S(1)} %get-tuple-element.153), channel_id=1, source_target_pairs={{0,16},{1,17},{2,18},{3,19},{4,20},{5,21},{6,22},{7,23},{8,24},{9,... | collective-permute-start | bytes 516104 | tf_op jit(solution)/shard_map/ppermute | solution.py:30
  164.8 9.2 %collective-permute-start.17 = (bf16[56,1536]{1,0:T(8,128)(2,1)S(1)}, bf16[56,1536]{1,0:T(8,128)(2,1)S(1)}, u32[]{:S(2)}, u32[]{:S(2)}) collective-permute-start(bf16[56,1536]{1,0:T(8,128)(2,1)S(1)} %get-tuple-element.152), channel_id=1, source_target_pairs={{0,20},{1,21},{2,22},{3,23},{4,16},{5,17},{6,18},{7,19},{8,28},{9,... | collective-permute-start | bytes 516104 | tf_op jit(solution)/shard_map/ppermute | solution.py:30
  174.2 11.2 %collective-permute-start.18 = (bf16[64,768]{1,0:T(8,128)(2,1)S(1)}, bf16[64,768]{1,0:T(8,128)(2,1)S(1)}, u32[]{:S(2)}, u32[]{:S(2)}) collective-permute-start(bf16[64,768]{1,0:T(8,128)(2,1)S(1)} %get-tuple-element.133), channel_id=1, source_target_pairs={{0,32},{1,33},{2,34},{3,35},{4,36},{5,37},{6,38},{7,39},{8,40},{9,... | collective-permute-start | bytes 294920 | tf_op jit(solution)/shard_map/ppermute | solution.py:30
  174.3 11.1 %collective-permute-start.19 = (bf16[64,768]{1,0:T(8,128)(2,1)S(1)}, bf16[64,768]{1,0:T(8,128)(2,1)S(1)}, u32[]{:S(2)}, u32[]{:S(2)}) collective-permute-start(bf16[64,768]{1,0:T(8,128)(2,1)S(1)} %get-tuple-element.133), channel_id=1, source_target_pairs={{0,64},{1,65},{2,66},{3,67},{4,68},{5,69},{6,70},{7,71},{8,72},{9,... | collective-permute-start | bytes 294920 | tf_op jit(solution)/shard_map/ppermute | solution.py:30
  178.4 7.0 %collective-permute-start.20 = (bf16[64,768]{1,0:T(8,128)(2,1)S(1)}, bf16[64,768]{1,0:T(8,128)(2,1)S(1)}, u32[]{:S(2)}, u32[]{:S(2)}) collective-permute-start(bf16[64,768]{1,0:T(8,128)(2,1)S(1)} %get-tuple-element.133), channel_id=1, source_target_pairs={{0,96},{1,97},{2,98},{3,99},{4,100},{5,101},{6,102},{7,103},{8,104... | collective-permute-start | bytes 294920 | tf_op jit(solution)/shard_map/ppermute | solution.py:30
